TPU v7x, 32 devices: a whole 2x2x4 slice. The times are simulated.
32 devices in a mesh: dp: 8 (over z, y), mp: 4 (over x, core).
Axes of the slice: x: 2, y: 2, z: 4, core: 2. Of those that a mesh axis runs over, the one named last changes fastest.
Arguments:
- tokens: bfloat16 [128, 147, 768], P('dp'), may hold values from -6 to 6
- cotangent: bfloat16 [128, 147, 768], P('dp'), may hold values from -6 to 6
- visible: int32 [128, 147], P('dp'), may hold values from 0 to 587, as said below
- tile_counts: int32 [8], P('dp'), may hold values from 1 to 16, as said below
- attend_weight: float32 [768, 3, 768], P('dp', None, 'mp'), may hold values from -0.3125 to 0.3125
- project_weight: float32 [768, 768], P('mp', 'dp'), may hold values from -0.875 to 0.875
- widen_weight: float32 [768, 3072], P('dp', 'mp'), may hold values from -0.21875 to 0.21875
- narrow_weight: float32 [3072, 768], P('mp', 'dp'), may hold values from -0.109375 to 0.109375
- heads_offset: float32 [2, 12, 64], P(None, 'mp', 'dp'), may hold values from -0.6 to 0.6
- hidden_offset: float32 [48, 64], P('mp', 'dp'), may hold values from -0.6 to 0.6
- layer_vectors: float32 [6, 768], P(None, 'dp'), may hold values from -1 to 2
- attend_first: float32 [768, 3, 768], P('dp', None, 'mp')
- project_first: float32 [768, 768], P('mp', 'dp')
- widen_first: float32 [768, 3072], P('dp', 'mp')
- narrow_first: float32 [3072, 768], P('mp', 'dp')
- heads_first: float32 [2, 12, 64], P(None, 'mp', 'dp')
- hidden_first: float32 [48, 64], P('mp', 'dp')
- vectors_first: float32 [6, 768], P(None, 'dp')
- attend_second: float32 [768, 3, 768], P('dp', None, 'mp')
- project_second: float32 [768, 768], P('mp', 'dp')
- widen_second: float32 [768, 3072], P('dp', 'mp')
- narrow_second: float32 [3072, 768], P('mp', 'dp')
- heads_second: float32 [2, 12, 64], P(None, 'mp', 'dp')
- hidden_second: float32 [48, 64], P('mp', 'dp')
- vectors_second: float32 [6, 768], P(None, 'dp')
Outputs:
- output: bfloat16 [128, 147, 768], P('dp')
- input_grad: float32 [128, 147, 768], P('dp')
- grad_attend: float32 [768, 3, 768], P('dp', None, 'mp')
- grad_project: float32 [768, 768], P('mp', 'dp')
- grad_widen: float32 [768, 3072], P('dp', 'mp')
- grad_narrow: float32 [3072, 768], P('mp', 'dp')
- grad_heads: float32 [2, 12, 64], P(None, 'mp', 'dp')
- grad_hidden: float32 [48, 64], P('mp', 'dp')
- grad_vectors: float32 [6, 768], P(None, 'dp')
- new_attend: float32 [768, 3, 768], P('dp', None, 'mp')
- new_project: float32 [768, 768], P('mp', 'dp')
- new_widen: float32 [768, 3072], P('dp', 'mp')
- new_narrow: float32 [3072, 768], P('mp', 'dp')
- new_heads: float32 [2, 12, 64], P(None, 'mp', 'dp')
- new_hidden: float32 [48, 64], P('mp', 'dp')
- new_vectors: float32 [6, 768], P(None, 'dp')
- first_attend: float32 [768, 3, 768], P('dp', None, 'mp')
- first_project: float32 [768, 768], P('mp', 'dp')
- first_widen: float32 [768, 3072], P('dp', 'mp')
- first_narrow: float32 [3072, 768], P('mp', 'dp')
- first_heads: float32 [2, 12, 64], P(None, 'mp', 'dp')
- first_hidden: float32 [48, 64], P('mp', 'dp')
- first_vectors: float32 [6, 768], P(None, 'dp')
- second_attend: float32 [768, 3, 768], P('dp', None, 'mp')
- second_project: float32 [768, 768], P('mp', 'dp')
- second_widen: float32 [768, 3072], P('dp', 'mp')
- second_narrow: float32 [3072, 768], P('mp', 'dp')
- second_heads: float32 [2, 12, 64], P(None, 'mp', 'dp')
- second_hidden: float32 [48, 64], P('mp', 'dp')
- second_vectors: float32 [6, 768], P(None, 'dp')
- copy_attend: bfloat16 [768, 3, 768], P('dp', None, 'mp')
- copy_project: bfloat16 [768, 768], P('mp', 'dp')
- copy_widen: bfloat16 [768, 3072], P('dp', 'mp')
- copy_narrow: bfloat16 [3072, 768], P('mp', 'dp')
- copy_heads: bfloat16 [2, 12, 64], P(None, 'mp', 'dp')
- copy_hidden: bfloat16 [48, 64], P('mp', 'dp')
- copy_vectors: bfloat16 [6, 768], P(None, 'dp')
Inputs may be any that keep to these rules, and one draw needn't show every extreme that they name: `visible`: the 147 places of one tile are distinct, of 3 frames of 14 x 14 patches. `tile_counts`: slots from this count on hold padding; some device has every slot live and some has one.
All inputs are finite; a program needn't handle non-finite values.
Results may differ from a plain program's by a relative error of at most 0.017.
The roundings to bfloat16 on the way count: a program that leaves them out, or rounds other values in their place, can miss the bound.
Values may be sent and summed in bfloat16 or wider, within the bound.
A program may use at most 192 MiB of HBM per device.

v0:
```python
import math

import jax
import jax.numpy as jnp
from jax import lax
from jax.sharding import PartitionSpec as P

D = 768
FF = 3072
GRID = 14
STEP = 3


LN_EPS = 1e-06
BETA_ONE = 0.5
BETA_TWO = 0.5
ADAM_EPS = 1e-08
DECAY = 0.05


def cut_along(x, dim, size):
    dims = x.shape
    parts = x.reshape(*dims[:dim], size, dims[dim] // size, *dims[dim + 1 :])
    return jnp.moveaxis(parts, dim, 0)


def summed_on_arrival(x, axis, dim):
    size = lax.axis_size(axis)
    parts = lax.all_to_all(cut_along(x, dim, size), axis, 0, 0, tiled=True)
    return jnp.sum(parts.astype(jnp.float32), axis=0)


def sine_table(places, feature_width):
    half_width = feature_width // 2
    spread = jnp.arange(half_width, dtype=jnp.float32) / half_width
    frequency = jnp.exp(-math.log(10000.0) * spread)
    angles = places[..., None] * frequency
    return jnp.concatenate([jnp.sin(angles), jnp.cos(angles)], axis=-1)


def position_table(visible, feature_width):
    plane_size = GRID * GRID
    frame_place = (visible // plane_size).astype(jnp.float32)
    within = visible % plane_size
    row_place = (within // GRID).astype(jnp.float32)
    column_place = (within % GRID).astype(jnp.float32)
    time_width = feature_width // 16 * 4
    space_width = feature_width // 16 * 6
    return jnp.concatenate(
        [
            sine_table(frame_place, time_width),
            sine_table(row_place, space_width),
            sine_table(column_place, space_width),
        ],
        axis=-1,
    )


def normalize(values):
    center = values - jnp.mean(values, axis=-1, keepdims=True)
    inverse = lax.rsqrt(jnp.mean(center * center, axis=-1, keepdims=True) + LN_EPS)
    return (center * inverse, inverse)


def norm_back(grad_normed, normed, inverse):
    return inverse * (
        grad_normed
        - jnp.mean(grad_normed, axis=-1, keepdims=True)
        - normed * jnp.mean(grad_normed * normed, axis=-1, keepdims=True)
    )


def over_rows(former, latter):
    return lax.dot_general(
        former, latter, (((0,), (0,)), ((), ())), preferred_element_type=jnp.float32
    )


def over_cols(former, latter):
    return lax.dot_general(
        former, latter, (((1,), (1,)), ((), ())), preferred_element_type=jnp.float32
    )


def exact_gelu(values):
    return jax.nn.gelu(values, approximate=False)


def adamw_update(
    master, first_moment, second_moment, gradient, step_rate, weight_decay, correction
):
    first_new = BETA_ONE * first_moment + (1.0 - BETA_ONE) * gradient
    second_new = BETA_TWO * second_moment + (1.0 - BETA_TWO) * gradient * gradient
    ratio = first_new / correction / (jnp.sqrt(second_new / correction) + ADAM_EPS)
    master_new = master - step_rate * (ratio + weight_decay * master)
    return (master_new, first_new, second_new)


def shards(
    tokens,
    cotangent,
    visible,
    tile_counts,
    attend_weight,
    project_weight,
    widen_weight,
    narrow_weight,
    heads_offset,
    hidden_offset,
    layer_vectors,
    attend_first,
    project_first,
    widen_first,
    narrow_first,
    heads_first,
    hidden_first,
    vectors_first,
    attend_second,
    project_second,
    widen_second,
    narrow_second,
    heads_second,
    hidden_second,
    vectors_second,
):
    fore_attend, fore_project, fore_widen, fore_narrow, fore_heads, fore_hidden, fore_vectors = (
        lax.all_gather(attend_weight.astype(jnp.bfloat16), "dp", axis=0, tiled=True),
        lax.all_gather(project_weight.astype(jnp.bfloat16), "dp", axis=1, tiled=True),
        lax.all_gather(widen_weight.astype(jnp.bfloat16), "dp", axis=0, tiled=True),
        lax.all_gather(narrow_weight.astype(jnp.bfloat16), "dp", axis=1, tiled=True),
        lax.all_gather(heads_offset.astype(jnp.bfloat16), "dp", axis=2, tiled=True),
        lax.all_gather(hidden_offset.astype(jnp.bfloat16), "dp", axis=1, tiled=True),
        lax.all_gather(layer_vectors.astype(jnp.bfloat16), "dp", axis=1, tiled=True),
    )
    tile_count, seq_length, model_width = tokens.shape
    row_count = tile_count * seq_length
    local_width = fore_attend.shape[2]
    heads_local = fore_heads.shape[1]
    head_size = fore_heads.shape[2]
    score_scale = 1.0 / math.sqrt(head_size)
    live_tiles = (jnp.arange(tile_count, dtype=jnp.int32) < tile_counts[0]).astype(jnp.float32)
    live_rows = jnp.broadcast_to(live_tiles[:, None], (tile_count, seq_length)).reshape(
        row_count, 1
    )
    vectors = fore_vectors.astype(jnp.float32)
    summed = (tokens.astype(jnp.float32) + position_table(visible, model_width)).reshape(
        row_count, model_width
    )
    normed_one, inverse_one = normalize(summed)
    attend_low = (normed_one * vectors[0] + vectors[1]).astype(jnp.bfloat16)
    linear = jnp.dot(
        attend_low,
        fore_attend.reshape(model_width, 3 * local_width),
        preferred_element_type=jnp.float32,
    ).reshape(row_count, 3, local_width)
    offsets = fore_heads.astype(jnp.float32).reshape(2, local_width)
    head_shape = (tile_count, seq_length, heads_local, head_size)
    query_low = (linear[:, 0] + offsets[0]).astype(jnp.bfloat16).reshape(head_shape)
    key_low = linear[:, 1].astype(jnp.bfloat16).reshape(head_shape)
    value_low = (linear[:, 2] + offsets[1]).astype(jnp.bfloat16).reshape(head_shape)
    scores = (
        jnp.einsum("tqhd,tkhd->thqk", query_low, key_low, preferred_element_type=jnp.float32)
        * score_scale
    )
    row_top = jnp.max(scores, axis=-1, keepdims=True)
    log_total = row_top + jnp.log(jnp.sum(jnp.exp(scores - row_top), axis=-1, keepdims=True))
    weights_low = jnp.exp(scores - log_total).astype(jnp.bfloat16)
    context = jnp.einsum(
        "thqk,tkhd->tqhd", weights_low, value_low, preferred_element_type=jnp.float32
    )
    context_low = context.reshape(row_count, local_width).astype(jnp.bfloat16)
    attention_part = jnp.dot(context_low, fore_project, preferred_element_type=jnp.float32)
    attention = lax.psum(attention_part.astype(jnp.bfloat16), "mp").astype(jnp.float32)
    middle = summed + attention + vectors[4]
    normed_two, inverse_two = normalize(middle)
    widen_low = (normed_two * vectors[2] + vectors[3]).astype(jnp.bfloat16)
    hidden = jnp.dot(
        widen_low, fore_widen, preferred_element_type=jnp.float32
    ) + fore_hidden.astype(jnp.float32).reshape(-1)
    active_low = exact_gelu(hidden).astype(jnp.bfloat16)
    feed_part = jnp.dot(active_low, fore_narrow, preferred_element_type=jnp.float32)
    feed_sum = lax.psum(feed_part.astype(jnp.bfloat16), "mp").astype(jnp.float32)
    result = (middle + feed_sum + vectors[5]) * live_rows
    output_low = result.astype(jnp.bfloat16)
    back_attend, back_project, back_widen, back_narrow, back_vectors = (
        fore_attend,
        fore_project,
        fore_widen,
        fore_narrow,
        fore_vectors,
    )
    vectors_back = back_vectors.astype(jnp.float32)
    grad_out = cotangent.astype(jnp.float32).reshape(row_count, model_width) * live_rows
    grad_out_low = grad_out.astype(jnp.bfloat16)
    grad_narrow = over_rows(active_low, grad_out_low)
    grad_active = over_cols(grad_out_low, back_narrow)
    gelu_back = jax.vjp(exact_gelu, hidden)[1]
    grad_hidden_low = gelu_back(grad_active)[0].astype(jnp.bfloat16)
    grad_widen = over_rows(widen_low, grad_hidden_low)
    grad_hidden = jnp.sum(grad_hidden_low.astype(jnp.float32), axis=0).reshape(fore_hidden.shape)
    normed_two_part = over_cols(grad_hidden_low, back_widen)
    grad_normed_two = lax.psum(normed_two_part.astype(jnp.bfloat16), "mp").astype(jnp.float32)
    grad_middle = grad_out + norm_back(grad_normed_two * vectors_back[2], normed_two, inverse_two)
    grad_middle_low = grad_middle.astype(jnp.bfloat16)
    grad_project = over_rows(context_low, grad_middle_low)
    grad_context_low = (
        over_cols(grad_middle_low, back_project).astype(jnp.bfloat16).reshape(head_shape)
    )
    scores_again = (
        jnp.einsum("tqhd,tkhd->thqk", query_low, key_low, preferred_element_type=jnp.float32)
        * score_scale
    )
    weights_full = jnp.exp(scores_again - log_total)
    weights_again_low = weights_full.astype(jnp.bfloat16)
    grad_weights = jnp.einsum(
        "tqhd,tkhd->thqk", grad_context_low, value_low, preferred_element_type=jnp.float32
    )
    grad_value = jnp.einsum(
        "thqk,tqhd->tkhd", weights_again_low, grad_context_low, preferred_element_type=jnp.float32
    )
    row_dot = jnp.sum(grad_weights * weights_full, axis=-1, keepdims=True)
    grad_scores_low = (weights_full * (grad_weights - row_dot)).astype(jnp.bfloat16)
    grad_query = (
        jnp.einsum("thqk,tkhd->tqhd", grad_scores_low, key_low, preferred_element_type=jnp.float32)
        * score_scale
    )
    grad_key = (
        jnp.einsum(
            "thqk,tqhd->tkhd", grad_scores_low, query_low, preferred_element_type=jnp.float32
        )
        * score_scale
    )
    grad_qkv_low = jnp.stack(
        [
            grad_query.reshape(row_count, local_width),
            grad_key.reshape(row_count, local_width),
            grad_value.reshape(row_count, local_width),
        ],
        axis=1,
    ).astype(jnp.bfloat16)
    grad_offsets = jnp.sum(grad_qkv_low.astype(jnp.float32), axis=0)
    grad_heads = jnp.stack([grad_offsets[0], grad_offsets[2]]).reshape(2, heads_local, head_size)
    flat_qkv = grad_qkv_low.reshape(row_count, 3 * local_width)
    grad_attend = over_rows(attend_low, flat_qkv).reshape(model_width, 3, local_width)
    normed_one_part = over_cols(flat_qkv, back_attend.reshape(model_width, 3 * local_width))
    grad_normed_one = lax.psum(normed_one_part.astype(jnp.bfloat16), "mp").astype(jnp.float32)
    grad_inputs = grad_middle + norm_back(
        grad_normed_one * vectors_back[0], normed_one, inverse_one
    )
    grad_vectors = jnp.stack(
        [
            jnp.sum(grad_normed_one * normed_one, axis=0),
            jnp.sum(grad_normed_one, axis=0),
            jnp.sum(grad_normed_two * normed_two, axis=0),
            jnp.sum(grad_normed_two, axis=0),
            jnp.sum(grad_middle, axis=0),
            jnp.sum(grad_out, axis=0),
        ]
    )
    output = output_low.reshape(tile_count, seq_length, model_width)
    input_grad = grad_inputs.reshape(tile_count, seq_length, model_width)
    (
        shard_attend,
        shard_project,
        shard_widen,
        shard_narrow,
        shard_heads,
        shard_hidden,
        shard_vectors,
    ) = (
        summed_on_arrival(grad_attend.astype(jnp.bfloat16), "dp", 0),
        summed_on_arrival(grad_project.astype(jnp.bfloat16), "dp", 1),
        summed_on_arrival(grad_widen.astype(jnp.bfloat16), "dp", 0),
        summed_on_arrival(grad_narrow.astype(jnp.bfloat16), "dp", 1),
        summed_on_arrival(grad_heads.astype(jnp.bfloat16), "dp", 2),
        summed_on_arrival(grad_hidden.astype(jnp.bfloat16), "dp", 1),
        summed_on_arrival(grad_vectors.astype(jnp.bfloat16), "dp", 1),
    )
    correction = 1.0 - 0.5**STEP
    new_attend, first_attend, second_attend = adamw_update(
        attend_weight,
        attend_first,
        attend_second,
        shard_attend,
        (D // 2) ** (-0.5),
        DECAY,
        correction,
    )
    new_project, first_project, second_project = adamw_update(
        project_weight,
        project_first,
        project_second,
        shard_project,
        (D // 16) ** (-0.5),
        DECAY,
        correction,
    )
    new_widen, first_widen, second_widen = adamw_update(
        widen_weight, widen_first, widen_second, shard_widen, D ** (-0.5), DECAY, correction
    )
    new_narrow, first_narrow, second_narrow = adamw_update(
        narrow_weight, narrow_first, narrow_second, shard_narrow, FF ** (-0.5), DECAY, correction
    )
    new_heads, first_heads, second_heads = adamw_update(
        heads_offset, heads_first, heads_second, shard_heads, 0.1, 0.0, correction
    )
    new_hidden, first_hidden, second_hidden = adamw_update(
        hidden_offset, hidden_first, hidden_second, shard_hidden, 0.1, 0.0, correction
    )
    new_vectors, first_vectors, second_vectors = adamw_update(
        layer_vectors, vectors_first, vectors_second, shard_vectors, 0.15, 0.0, correction
    )
    return (
        output,
        input_grad,
        shard_attend,
        shard_project,
        shard_widen,
        shard_narrow,
        shard_heads,
        shard_hidden,
        shard_vectors,
        new_attend,
        new_project,
        new_widen,
        new_narrow,
        new_heads,
        new_hidden,
        new_vectors,
        first_attend,
        first_project,
        first_widen,
        first_narrow,
        first_heads,
        first_hidden,
        first_vectors,
        second_attend,
        second_project,
        second_widen,
        second_narrow,
        second_heads,
        second_hidden,
        second_vectors,
        new_attend.astype(jnp.bfloat16),
        new_project.astype(jnp.bfloat16),
        new_widen.astype(jnp.bfloat16),
        new_narrow.astype(jnp.bfloat16),
        new_heads.astype(jnp.bfloat16),
        new_hidden.astype(jnp.bfloat16),
        new_vectors.astype(jnp.bfloat16),
    )


def solution(mesh):
    in_specs = (
        P("dp", None, None),
        P("dp", None, None),
        P("dp", None),
        P("dp"),
        P("dp", None, "mp"),
        P("mp", "dp"),
        P("dp", "mp"),
        P("mp", "dp"),
        P(None, "mp", "dp"),
        P("mp", "dp"),
        P(None, "dp"),
        P("dp", None, "mp"),
        P("mp", "dp"),
        P("dp", "mp"),
        P("mp", "dp"),
        P(None, "mp", "dp"),
        P("mp", "dp"),
        P(None, "dp"),
        P("dp", None, "mp"),
        P("mp", "dp"),
        P("dp", "mp"),
        P("mp", "dp"),
        P(None, "mp", "dp"),
        P("mp", "dp"),
        P(None, "dp"),
    )
    out_specs = (
        P("dp", None, None),
        P("dp", None, None),
        P("dp", None, "mp"),
        P("mp", "dp"),
        P("dp", "mp"),
        P("mp", "dp"),
        P(None, "mp", "dp"),
        P("mp", "dp"),
        P(None, "dp"),
        P("dp", None, "mp"),
        P("mp", "dp"),
        P("dp", "mp"),
        P("mp", "dp"),
        P(None, "mp", "dp"),
        P("mp", "dp"),
        P(None, "dp"),
        P("dp", None, "mp"),
        P("mp", "dp"),
        P("dp", "mp"),
        P("mp", "dp"),
        P(None, "mp", "dp"),
        P("mp", "dp"),
        P(None, "dp"),
        P("dp", None, "mp"),
        P("mp", "dp"),
        P("dp", "mp"),
        P("mp", "dp"),
        P(None, "mp", "dp"),
        P("mp", "dp"),
        P(None, "dp"),
        P("dp", None, "mp"),
        P("mp", "dp"),
        P("dp", "mp"),
        P("mp", "dp"),
        P(None, "mp", "dp"),
        P("mp", "dp"),
        P(None, "dp"),
    )
    return jax.shard_map(shards, mesh=mesh, in_specs=in_specs, out_specs=out_specs, check_vma=False)
```

profile of v0, /device:TPU:0, one launch (start us, length us, event | category | flops | bytes accessed | tf_op | source)
XLA Modules:
  0.0 817.2 jit_solution(17125010776778953683)
XLA Ops:
  8.8 27.9 %all-gather = bf16[8,96,6]{1,2,0:T(8,128)(2,1)S(1)} all-gather(bf16[1,96,6]{1,2,0:T(8,128)(2,1)S(1)} %convert_bitcast_fusion), channel_id=1, replica_groups=mesh['dp'=8,'mp'=4] {'dp'}, dimensions={0}, use_global_device_ids=true | all-gather | bytes 10368 | tf_op jit(solution)/shard_map/all_gather | solution.py:133
  39.5 33.2 %all_gather.22 = bf16[768,3,192]{2,0,1:T(8,128)(2,1)S(1)} all-gather(bf16[96,3,192]{2,0,1:T(8,128)(2,1)S(1)} %convert_element_type.217), channel_id=1, replica_groups=mesh['dp'=8,'mp'=4] {'dp'}, dimensions={0}, use_global_device_ids=true | all-gather | bytes 995328 | tf_op jit(solution)/shard_map/all_gather | solution.py:127
  73.7 5.7 multiply_cosine_fusion.2
  79.4 19.3 %multiply_cosine_fusion = (f32[16,147,144]{2,0,1:T(8,128)S(1)}, f32[16,147,144]{2,0,1:T(8,128)}, f32[16,147,144]{2,0,1:T(8,128)}, f32[16,147,144]{2,0,1:T(8,128)}) fusion(f32[16,147]{0,1:T(8,128)S(1)} %copy.347, f32[144]{0:T(256)S(1)} %multiply_exponential_fusion, f32[16,147]{0,1:T(8,128)S(1)} %copy.346), kind=kLoop, calls=%fused_computation.60 | loop fusion | flops 677376 | bytes 5438400 | tf_op jit(solution)/shard_map/cos | solution.py:38
  98.7 11.6 %concatenate.5 = f32[16,147,768]{2,0,1:T(8,128)} concatenate(f32[16,147,96]{2,0,1:T(8,128)} %get-tuple-element.356, f32[16,147,96]{2,0,1:T(8,128)} %get-tuple-element.355, f32[16,147,144]{2,0,1:T(8,128)} %get-tuple-element.364, f32[16,147,144]{2,0,1:T(8,128)} %get-tuple-element.365, f32[16,147,144]{2,0,1:T(8,128)} %get-tuple-element.352, f32[16,147,144]{2,0,1:T(8,128)S(1)} %get-tuple-element.351), dimensions={2} | concatenate | bytes 14450688 | tf_op jit(solution)/shard_map/concatenate | solution.py:49
  110.3 7.8 fusion.87
  133.8 4.5 fusion.43
  140.7 30.6 %all_gather.23 = bf16[2,3,64]{1,0,2:T(2,128)(2,1)S(1)} all-gather(bf16[2,3,8]{1,0,2:T(2,128)(2,1)S(1)} %copy.356), channel_id=1, replica_groups=mesh['dp'=8,'mp'=4] {'dp'}, dimensions={2}, use_global_device_ids=true | all-gather | bytes 864 | tf_op jit(solution)/shard_map/all_gather | solution.py:131
  171.6 31.4 %all_gather.24 = bf16[192,768]{0,1:T(8,128)(2,1)S(1)} all-gather(bf16[192,96]{0,1:T(8,128)(2,1)S(1)} %copy.364), channel_id=1, replica_groups=mesh['dp'=8,'mp'=4] {'dp'}, dimensions={1}, use_global_device_ids=true | all-gather | bytes 331776 | tf_op jit(solution)/shard_map/all_gather | solution.py:128
  202.9 5.3 convert_element_type.222
  208.2 5.4 squeeze.10
  213.6 6.2 squeeze.11
  219.8 5.9 multiply_reduce_fusion.4
  243.8 12.3 %all-gather.6.cloned.1.call-start = ((), (), s32[]{:S(2)}) async-start(), calls=%async_computation.9 | async-start | bytes 1327104 | tf_op jit(solution)/shard_map/all_gather | solution.py:130
  256.1 10.4 %copy.348 = f32[16,147,768]{2,1,0:T(8,128)} copy(f32[16,147,768]{2,0,1:T(8,128)} %get-tuple-element.347) | data formatting | bytes 14450688 | tf_op jit(solution)/shard_map/add | solution.py:146
  267.7 26.3 %all_gather.26 = bf16[12,64]{0,1:T(8,128)(2,1)S(1)} all-gather(bf16[12,8]{0,1:T(8,128)(2,1)S(1)} %convert_element_type.232), channel_id=1, replica_groups=mesh['dp'=8,'mp'=4] {'dp'}, dimensions={1}, use_global_device_ids=true | all-gather | bytes 1728 | tf_op jit(solution)/shard_map/all_gather | solution.py:132
  297.5 6.2 copy.366
  303.7 5.5 reshape.304
  309.2 5.6 reshape.301
  318.6 5.1 fusion.86
  329.4 21.0 %multiply_convert_fusion.2 = (bf16[2352,768]{1,0:T(8,128)(2,1)S(1)}, f32[2352,768]{1,0:T(8,128)}, f32[2352,768]{1,0:T(8,128)}) fusion(f32[768]{0:T(1024)} %reshape.311, bf16[2352,768]{1,0:T(8,128)(2,1)} %add_convert_fusion.1, bf16[768,768]{1,0:T(8,128)(2,1)} %all-gather.4.cloned.1.call-done), kind=kOutput, calls=%fused_computation.31 | convolution fusion | flops 2893750272 | bytes 22858752 | tf_op jit(solution)/shard_map/dot_general | solution.py:177
  350.4 7.9 convolution_convert_fusion.5
  358.3 34.1 %all_to_all.35 = bf16[8,768,96]{1,2,0:T(8,128)(2,1)S(1)} all-to-all(bf16[8,768,96]{1,2,0:T(8,128)(2,1)S(1)} %bitcast.97), channel_id=1, replica_groups=mesh['dp'=8,'mp'=4] {'dp'}, dimensions={0} | all-to-all | bytes 2359296 | tf_op jit(solution)/shard_map/all_to_all | solution.py:29
  394.6 39.3 %all-gather.6.cloned.1.call-done = bf16[768,768]{0,1:T(8,128)(2,1)} async-done(((bf16[768,96]{0,1:T(8,128)(2,1)}), bf16[768,768]{0,1:T(8,128)(2,1)}) %all-gather.6.cloned.1.call-update) | async-done | bytes 1179664 | tf_op jit(solution)/shard_map/all_gather | solution.py:130
  433.9 11.3 %fusion.91 = (bf16[768]{0:T(1024)(128)(2,1)}, bf16[2352,768]{1,0:T(8,128)(2,1)S(1)}) fusion(f32[2352,768]{1,0:T(8,128)} %get-tuple-element.343, bf16[768,768]{0,1:T(8,128)(2,1)} %all-gather.6.cloned.1.call-done, f32[2352,768]{1,0:T(8,128)} %reshape.304, f32[2352]{0:T(1024)} %mul.444, f32[2352,768]{1,0:T(8,128)} %get-tuple-element.368, f32[768]{0:T(1024)} %reshape.311), kind=kOutput, calls=%fused_computation.191 | convolution fusion | flops 2807045376 | bytes 26482368 | tf_op jit(solution)/shard_map/dot_general | solution.py:80
  447.0 4.5 convolution_convert_fusion
  458.3 68.1 %all-reduce.7.cloned.1.call-done = bf16[2352,768]{1,0:T(8,128)(2,1)} async-done(((bf16[2352,768]{1,0:T(8,128)(2,1)}), bf16[2352,768]{1,0:T(8,128)(2,1)}) %all-reduce.7.cloned.1.call-update) | async-done | bytes 3612688 | tf_op jit(solution)/shard_map/psum | solution.py:202
  526.4 7.8 fusion.10
  534.2 7.6 fusion.82
  546.9 6.2 reshape.305
  553.1 5.6 convolution_bitcast_fusion
  558.7 7.2 multiply_reduce_fusion
  588.9 5.8 all-to-all-start.4
  594.6 7.5 convolution_convert_fusion.6
  602.1 6.0 all-to-all-start.2
  608.2 7.3 convolution_convert_fusion.1
  615.5 4.9 bitcast_convert_fusion
  626.9 9.3 %all-to-all-done.2 = bf16[8,96,768]{2,1,0:T(8,128)(2,1)S(1)} async-done(((bf16[8,96,768]{2,1,0:T(8,128)(2,1)}), bf16[8,96,768]{2,1,0:T(8,128)(2,1)S(1)}, u32[]{:S(2)}, u32[]{:S(2)}) %all-to-all-start.2) | async-done | bytes 1179680 | tf_op jit(solution)/shard_map/all_to_all | solution.py:29
  640.1 6.4 fusion.31
  651.8 4.4 all-to-all-start
  675.7 8.8 %all-to-all-done = bf16[8,96,3,192]{1,3,2,0:T(8,128)(2,1)S(1)} async-done(((bf16[8,96,3,192]{1,3,2,0:T(8,128)(2,1)}), bf16[8,96,3,192]{1,3,2,0:T(8,128)(2,1)S(1)}, u32[]{:S(2)}, u32[]{:S(2)}) %all-to-all-start) | async-done | bytes 884768 | tf_op jit(solution)/shard_map/all_to_all | solution.py:29
  690.4 65.6 %all-reduce.9.cloned.1.call-done = (bf16[2352,768]{1,0:T(8,128)(2,1)}, bf16[2352,768]{1,0:T(8,128)(2,1)}) async-done(((bf16[2352,768]{1,0:T(8,128)(2,1)}, bf16[2352,768]{1,0:T(8,128)(2,1)}), (bf16[2352,768]{1,0:T(8,128)(2,1)}, bf16[2352,768]{1,0:T(8,128)(2,1)})) %all-reduce.9.cloned.1.call-update) | async-done | bytes 7225360 | tf_op jit(solution)/shard_map/psum | solution.py:182
  758.7 7.2 fusion.15
  766.7 5.7 all-to-all-start.6
  772.5 11.5 %fusion.13 = f32[2352,768]{1,0:T(8,128)} fusion(f32[2352,768]{1,0:T(8,128)} %copy-done.2, bf16[2352,768]{1,0:T(8,128)(2,1)} %get-tuple-element.309, f32[2352,768]{1,0:T(8,128)} %reshape.301, f32[2352]{0:T(1024)S(1)} %broadcast_multiply_fusion.1, f32[2352]{0:T(1024)S(1)} %div.112, f32[2352]{0:T(1024)S(1)} %broadcast_multiply_fusion.2, f32[768]{0:T(1024)S(1)} %copy-done.35, ...), kind=kLoop, calls=%fused_computation.22 | loop fusion | flops 16257024 | bytes 25329408 | tf_op jit(solution)/shard_map/add | solution.py:247
  790.7 4.6 copy.395
  795.3 5.4 reshape.306
  800.7 8.5 %copy.396 = f32[16,147,768]{2,0,1:T(8,128)} copy(f32[16,147,768]{2,1,0:T(8,128)} %reshape.306) | data formatting | bytes 14450688
  (272 shorter events, 144.4 us)
Async XLA Ops:
  8.0 310.5 %all-reduce.5.cloned.1.call-start = ((), (), s32[]{:S(2)}) async-start(), calls=%async_computation.7 | async-start | bytes 7225344 | tf_op jit(solution)/shard_map/psum | solution.py:173
  37.5 85.6 %copy-start.34 = (f32[768]{0:T(1024)}, f32[768]{0:T(1024)S(1)}, u32[]{:S(2)}) copy-start(f32[768]{0:T(1024)S(1)} %get-tuple-element.307) | copy-start | bytes 9220
  138.3 33.1 %copy-start.17 = (f32[192,96]{1,0:T(8,128)S(1)}, f32[192,96]{1,0:T(8,128)}, u32[]{:S(2)}) copy-start(f32[192,96]{1,0:T(8,128)} %param.30) | copy-start | bytes 221188
  171.4 56.1 %copy-start.39 = (f32[1,3,64]{2,1,0:T(4,128)}, f32[1,3,64]{2,1,0:T(4,128)S(1)}, u32[]{:S(2)}) copy-start(f32[1,3,64]{2,1,0:T(4,128)S(1)} %copy.357) | copy-start | bytes 2308
  171.5 54.3 %copy-start.37 = (f32[1,3,64]{2,1,0:T(4,128)}, f32[1,3,64]{2,1,0:T(4,128)S(1)}, u32[]{:S(2)}) copy-start(f32[1,3,64]{2,1,0:T(4,128)S(1)} %copy.359) | copy-start | bytes 2308
  242.1 87.3 %all-gather.4.cloned.1.call-start = ((), (), s32[]{:S(2)}) async-start(), calls=%async_computation.8 | async-start | bytes 1327104 | tf_op jit(solution)/shard_map/all_gather | solution.py:129
  243.8 23.9 %copy-start.46 = (f32[12,8]{0,1:T(8,128)S(1)}, f32[12,8]{0,1:T(8,128)}, u32[]{:S(2)}) copy-start(f32[12,8]{0,1:T(8,128)} %param.34) | copy-start | bytes 1156
  243.8 190.0 %all-gather.6.cloned.1.call-start = ((), (), s32[]{:S(2)}) async-start(), calls=%async_computation.9 | async-start | bytes 1327104 | tf_op jit(solution)/shard_map/all_gather | solution.py:130
  309.2 9.3 %copy-start.43 = (f32[768]{0:T(1024)S(1)}, f32[768]{0:T(1024)}, u32[]{:S(2)}) copy-start(f32[768]{0:T(1024)} %get-tuple-element.305) | copy-start | bytes 9220
  329.4 21.0 %copy-start.29 = (f32[2352]{0:T(1024)S(1)}, f32[2352]{0:T(1024)}, u32[]{:S(2)}) copy-start(f32[2352]{0:T(1024)} %mul.444) | copy-start | bytes 28228
  350.4 42.9 %copy-start.20 = (f32[768,96]{0,1:T(8,128)S(1)}, f32[768,96]{0,1:T(8,128)}, u32[]{:S(2)}) copy-start(f32[768,96]{0,1:T(8,128)} %param.32) | copy-start | bytes 884740
  350.4 42.9 %copy-start.21 = (f32[768,96]{0,1:T(8,128)S(1)}, f32[768,96]{0,1:T(8,128)}, u32[]{:S(2)}) copy-start(f32[768,96]{0,1:T(8,128)} %param.39) | copy-start | bytes 884740
  350.4 42.9 %copy-start.22 = (f32[768,96]{0,1:T(8,128)S(1)}, f32[768,96]{0,1:T(8,128)}, u32[]{:S(2)}) copy-start(f32[768,96]{0,1:T(8,128)} %param.46) | copy-start | bytes 884740
  394.5 131.9 %all-reduce.7.cloned.1.call-start = ((), (), s32[]{:S(2)}) async-start(), calls=%async_computation.10 | async-start | bytes 7225344 | tf_op jit(solution)/shard_map/psum | solution.py:202
  433.9 13.2 %copy-start.60 = (bf16[768,768]{1,0:T(8,128)(2,1)S(1)}, bf16[768,768]{1,0:T(8,128)(2,1)}, u32[]{:S(2)}) copy-start(bf16[768,768]{1,0:T(8,128)(2,1)} %all-gather.4.cloned.1.call-done) | copy-start | bytes 3538948
  454.4 134.5 %all-to-all-start.5 = ((bf16[8,12,8]{1,2,0:T(8,128)(2,1)}), bf16[8,12,8]{1,2,0:T(8,128)(2,1)}, u32[]{:S(2)}, u32[]{:S(2)}) async-start(bf16[8,12,8]{1,2,0:T(8,128)(2,1)} %copy.382), calls=%async_computation.5 | async-start | bytes 32768 | tf_op jit(solution)/shard_map/all_to_all | solution.py:29
  546.9 11.8 %copy-start.13 = (f32[16,3,147]{2,1,0:T(4,128)S(1)}, f32[16,3,147]{2,1,0:T(4,128)}, u32[]{:S(2)}) copy-start(f32[16,3,147]{2,1,0:T(4,128)} %copy-done.12) | copy-start | bytes 84676
  546.9 11.8 %copy-start.40 = (f32[1,3,64]{2,1,0:T(4,128)S(1)}, f32[1,3,64]{2,1,0:T(4,128)}, u32[]{:S(2)}) copy-start(f32[1,3,64]{2,1,0:T(4,128)} %copy-done.39) | copy-start | bytes 2308
  553.1 12.9 %slice-start = ((s8[7471104]{0:T(1024)(128)(4,1)}), s8[4194304]{0:T(1024)(128)(4,1)S(1)}, s32[]{:S(2)}) async-start(s8[7471104]{0:T(1024)(128)(4,1)} %bitcast.93), calls=%async_computation.12 | async-start | bytes 8388608
  588.9 13.3 %all-to-all-start.4 = ((bf16[8,2,3,8]{3,1,2,0:T(2,128)(2,1)}), bf16[8,2,3,8]{3,1,2,0:T(2,128)(2,1)S(1)}, u32[]{:S(2)}, u32[]{:S(2)}) async-start(bf16[8,2,3,8]{3,1,2,0:T(2,128)(2,1)} %copy.379), calls=%async_computation.4 | async-start | bytes 24576 | tf_op jit(solution)/shard_map/all_to_all | solution.py:29
  602.1 34.1 %all-to-all-start.2 = ((bf16[8,96,768]{2,1,0:T(8,128)(2,1)}), bf16[8,96,768]{2,1,0:T(8,128)(2,1)S(1)}, u32[]{:S(2)}, u32[]{:S(2)}) async-start(bf16[8,96,768]{2,1,0:T(8,128)(2,1)} %bitcast.18), calls=%async_computation.2 | async-start | bytes 2359296 | tf_op jit(solution)/shard_map/all_to_all | solution.py:29
  608.2 147.9 %all-reduce.9.cloned.1.call-start = ((), (), s32[]{:S(2)}) async-start(), calls=%async_computation.11 | async-start | bytes 14450688 | tf_op jit(solution)/shard_map/psum | solution.py:182
  636.2 15.6 %all-to-all-start.1 = ((bf16[8,192,96]{2,1,0:T(8,128)(2,1)}), bf16[8,192,96]{2,1,0:T(8,128)(2,1)S(1)}, u32[]{:S(2)}, u32[]{:S(2)}) async-start(bf16[8,192,96]{2,1,0:T(8,128)(2,1)} %bitcast.91), calls=%async_computation.1 | async-start | bytes 786432 | tf_op jit(solution)/shard_map/all_to_all | solution.py:29
  640.1 16.2 %copy-start.59 = (f32[16]{0:T(128)S(1)}, f32[16]{0:T(128)}, u32[]{:S(2)}) copy-start(f32[16]{0:T(128)} %compare_convert_fusion) | copy-start | bytes 196
  646.5 14.6 %copy-start.26 = (f32[16,147]{1,0:T(8,128)S(1)}, f32[16,147]{1,0:T(8,128)}, u32[]{:S(2)}) copy-start(f32[16,147]{1,0:T(8,128)} %copy-done.25) | copy-start | bytes 28228
  646.5 14.8 %copy-start.28 = (f32[16,147]{1,0:T(8,128)S(1)}, f32[16,147]{1,0:T(8,128)}, u32[]{:S(2)}) copy-start(f32[16,147]{1,0:T(8,128)} %copy-done.27) | copy-start | bytes 28228
  646.5 19.3 %copy-start.47 = (f32[12,8]{0,1:T(8,128)S(1)}, f32[12,8]{0,1:T(8,128)}, u32[]{:S(2)}) copy-start(f32[12,8]{0,1:T(8,128)} %param.34) | copy-start | bytes 1156
  646.5 19.3 %copy-start.53 = (f32[12,8]{0,1:T(8,128)S(1)}, f32[12,8]{0,1:T(8,128)}, u32[]{:S(2)}) copy-start(f32[12,8]{0,1:T(8,128)} %param.41) | copy-start | bytes 1156
  646.5 19.3 %copy-start.54 = (f32[12,8]{0,1:T(8,128)S(1)}, f32[12,8]{0,1:T(8,128)}, u32[]{:S(2)}) copy-start(f32[12,8]{0,1:T(8,128)} %param.48) | copy-start | bytes 1156
  648.9 20.2 %copy-start.51 = (bf16[768]{0:T(1024)(128)(2,1)S(1)}, bf16[768]{0:T(1024)(128)(2,1)}, u32[]{:S(2)}) copy-start(bf16[768]{0:T(1024)(128)(2,1)} %get-tuple-element.296) | copy-start | bytes 4612
  649.0 20.3 %copy-start.52 = (bf16[768]{0:T(1024)(128)(2,1)S(1)}, bf16[768]{0:T(1024)(128)(2,1)}, u32[]{:S(2)}) copy-start(bf16[768]{0:T(1024)(128)(2,1)} %get-tuple-element.338) | copy-start | bytes 4612
  649.0 21.0 %copy-start.50 = (f32[2,3,8]{2,0,1:T(2,128)S(1)}, f32[2,3,8]{2,0,1:T(2,128)}, u32[]{:S(2)}) copy-start(f32[2,3,8]{2,0,1:T(2,128)} %param.33) | copy-start | bytes 580
  649.0 21.0 %copy-start.57 = (f32[2,3,8]{2,0,1:T(2,128)S(1)}, f32[2,3,8]{2,0,1:T(2,128)}, u32[]{:S(2)}) copy-start(f32[2,3,8]{2,0,1:T(2,128)} %param.40) | copy-start | bytes 580
  649.0 21.0 %copy-start.58 = (f32[2,3,8]{2,0,1:T(2,128)S(1)}, f32[2,3,8]{2,0,1:T(2,128)}, u32[]{:S(2)}) copy-start(f32[2,3,8]{2,0,1:T(2,128)} %param.47) | copy-start | bytes 580
  649.0 23.5 %copy-start.14 = (f32[96,768]{1,0:T(8,128)S(1)}, f32[96,768]{1,0:T(8,128)}, u32[]{:S(2)}) copy-start(f32[96,768]{1,0:T(8,128)} %param.31) | copy-start | bytes 884740
  651.8 32.7 %all-to-all-start = ((bf16[8,96,3,192]{1,3,2,0:T(8,128)(2,1)}), bf16[8,96,3,192]{1,3,2,0:T(8,128)(2,1)S(1)}, u32[]{:S(2)}, u32[]{:S(2)}) async-start(bf16[8,96,3,192]{1,3,2,0:T(8,128)(2,1)} %copy.376), calls=%async_computation | async-start | bytes 2359296 | tf_op jit(solution)/shard_map/all_to_all | solution.py:29
  656.2 18.6 %copy-start.18 = (f32[192,96]{1,0:T(8,128)S(1)}, f32[192,96]{1,0:T(8,128)}, u32[]{:S(2)}) copy-start(f32[192,96]{1,0:T(8,128)} %param.30) | copy-start | bytes 221188
  656.3 18.6 %copy-start.32 = (f32[192,96]{1,0:T(8,128)S(1)}, f32[192,96]{1,0:T(8,128)}, u32[]{:S(2)}) copy-start(f32[192,96]{1,0:T(8,128)} %param.37) | copy-start | bytes 221188
  656.3 18.6 %copy-start.33 = (f32[192,96]{1,0:T(8,128)S(1)}, f32[192,96]{1,0:T(8,128)}, u32[]{:S(2)}) copy-start(f32[192,96]{1,0:T(8,128)} %param.44) | copy-start | bytes 221188
  665.9 24.6 %copy-start.44 = (f32[12,8]{0,1:T(8,128)}, f32[12,8]{0,1:T(8,128)S(1)}, u32[]{:S(2)}) copy-start(f32[12,8]{0,1:T(8,128)S(1)} %convert_reduce_fusion.5) | copy-start | bytes 1156
  672.3 86.4 %copy-start.35 = (f32[768]{0:T(1024)S(1)}, f32[768]{0:T(1024)}, u32[]{:S(2)}) copy-start(f32[768]{0:T(1024)} %copy-done.34) | copy-start | bytes 9220
  674.9 91.1 %copy-start.19 = (f32[192,96]{1,0:T(8,128)}, f32[192,96]{1,0:T(8,128)S(1)}, u32[]{:S(2)}) copy-start(f32[192,96]{1,0:T(8,128)S(1)} %convert_reduce_fusion.3) | copy-start | bytes 221188
  758.7 25.3 %slice-start.2 = ((s8[7225344]{0:T(1024)(128)(4,1)}), s8[3031040]{0:T(1024)(128)(4,1)S(1)}, s32[]{:S(2)}) async-start(s8[7225344]{0:T(1024)(128)(4,1)} %bitcast.95), calls=%async_computation.14 | async-start | bytes 6062080
  766.7 42.5 %all-to-all-start.6 = ((bf16[8,6,96]{2,1,0:T(8,128)(2,1)}), bf16[8,6,96]{2,1,0:T(8,128)(2,1)S(1)}, u32[]{:S(2)}, u32[]{:S(2)}) async-start(bf16[8,6,96]{2,1,0:T(8,128)(2,1)} %copy.384), calls=%async_computation.6 | async-start | bytes 32768 | tf_op jit(solution)/shard_map/all_to_all | solution.py:29
  772.4 11.6 %slice-start.3 = ((s8[7225344]{0:T(1024)(128)(4,1)}), s8[4194304]{0:T(1024)(128)(4,1)S(1)}, s32[]{:S(2)}) async-start(s8[7225344]{0:T(1024)(128)(4,1)} %bitcast.95), calls=%async_computation.15 | async-start | bytes 8388608
  772.5 11.6 %copy-start.10 = (bf16[2352,768]{1,0:T(8,128)(2,1)S(1)}, bf16[2352,768]{1,0:T(8,128)(2,1)}, u32[]{:S(2)}) copy-start(bf16[2352,768]{1,0:T(8,128)(2,1)} %get-tuple-element.308) | copy-start | bytes 10838020
  772.5 11.6 %copy-start.31 = (f32[2352]{0:T(1024)S(1)}, f32[2352]{0:T(1024)}, u32[]{:S(2)}) copy-start(f32[2352]{0:T(1024)} %mul.444) | copy-start | bytes 28228
  772.5 11.6 %copy-start.41 = (f32[768]{0:T(1024)S(1)}, f32[768]{0:T(1024)}, u32[]{:S(2)}) copy-start(f32[768]{0:T(1024)} %get-tuple-element.302) | copy-start | bytes 9220
  (30 other events, 129.2 us)
Sparse Core Ops, SparseCore 0:
  242.2 76.3 all-reduce.4
  451.7 74.6 all-reduce.6
  620.6 135.3 all-reduce.8
Sparse Core Ops, SparseCore 1:
  245.3 41.3 all-gather.3
  394.6 39.2 all-gather.5
where the time goes:
time: 827 us; the launch traced here: 817 us
  waiting for transfers between devices  197 us (24%)
  blocking collectives  183 us (22%)
  local copies, waits for them, and re-layouts  151 us (18%)
  other arithmetic  114 us (14%)
  matrix products  112 us (14%)
  starting transfers between devices  42.1 us (5%)
  between operations  17 us (2%)
    psum x1, waiting for transfers between devices, shards(): lax.psum(normed_two_part.astype(jnp.bfloat16), 'mp').astype(jnp.float32)  68.1 us
    psum x1, waiting for transfers between devices, shards(): lax.psum(feed_part.astype(jnp.bfloat16), 'mp').astype(jnp.float32)  65.6 us
    all_gather x1, waiting for transfers between devices, shards(): lax.all_gather(narrow_weight.astype(jnp.bfloat16), 'dp', axis=1, tiled=True)  39.3 us
    unnamed x155, local copies, waits for them, and re-layouts  36.8 us
    all_to_all x1, blocking collectives, summed_on_arrival(): parts = lax.all_to_all(cut_along(x, dim, size), axis, 0, 0, tiled=True)  34.1 us
    all_gather x1, blocking collectives, shards(): lax.all_gather(attend_weight.astype(jnp.bfloat16), 'dp', axis=0, tiled=True)  33.2 us
    all_gather x1, blocking collectives, shards(): lax.all_gather(project_weight.astype(jnp.bfloat16), 'dp', axis=1, tiled=T...  31.4 us
    all_gather x1, blocking collectives, shards(): lax.all_gather(heads_offset.astype(jnp.bfloat16), 'dp', axis=2, tiled=True)  30.6 us
  transfers between devices with their start and end apart: 11, of which 7 were waited for; matrix products, arithmetic and copies ran while one was open for 25% of the time, Pallas kernels for 0%

commit v1 on v0

--- a/solution.py
+++ b/solution.py
@@ -1,8 +1,12 @@
+import functools
 import math
 
 import jax
 import jax.numpy as jnp
+import numpy as np
 from jax import lax
+from jax.experimental import pallas as pl
+from jax.experimental.pallas import tpu as pltpu
 from jax.sharding import PartitionSpec as P
 
 D = 768
@@ -351,6 +355,774 @@
     )
 
 
+F32 = jnp.float32
+BF16 = jnp.bfloat16
+MESH = pl.DeviceIdType.MESH
+ANY = pl.ANY
+
+
+def nn(former, latter):
+    return lax.dot_general(former, latter, (((1,), (0,)), ((), ())), preferred_element_type=F32)
+
+
+def nt(former, latter):
+    return lax.dot_general(former, latter, (((1,), (1,)), ((), ())), preferred_element_type=F32)
+
+
+def tn(former, latter):
+    return lax.dot_general(former, latter, (((0,), (0,)), ((), ())), preferred_element_type=F32)
+
+
+def iota(shape, dim):
+    return lax.broadcasted_iota(jnp.int32, shape, dim)
+
+
+def whole(ref_shape):
+    rank = len(ref_shape)
+    return pl.BlockSpec(ref_shape, lambda *_: (0,) * rank)
+
+
+def pick_vector(d):
+    shape = (128, D)
+    lane, column = iota(shape, 0), iota(shape, 1)
+    return ((column - lane == 96 * d) & (lane < 96)).astype(F32).astype(BF16)
+
+
+def pick_head(d):
+    shape = (128, D)
+    lane, column = iota(shape, 0), iota(shape, 1)
+    same = (lax.shift_right_logical(column, 6) == lax.shift_right_logical(lane, 3)) & ((column & 7) == (lane & 7))
+    return (same & ((lax.shift_right_logical(column, 3) & 7) == d) & (lane < 24)).astype(F32).astype(BF16)
+
+
+def pick_row():
+    shape = (128, D)
+    return (lax.shift_right_logical(iota(shape, 1), 6) == iota(shape, 0)).astype(F32).astype(BF16)
+
+
+def hidden_places(d):
+    shape = (8, D)
+    column = iota(shape, 1)
+    return ((column & 7) == iota(shape, 0)) & ((lax.shift_right_logical(column, 3) & 7) == d)
+
+
+def pack_kernel(attend, project, widen, narrow, heads, hidden, vectors, w_out, s_out, scratch):
+    w_out[0] = jnp.concatenate([attend[0], attend[1], attend[2], project[...].T], axis=1).astype(BF16)
+    w_out[1] = widen[...].astype(BF16)
+    w_out[2] = narrow[...].astype(BF16)
+    scratch[...] = jnp.zeros_like(scratch)
+    scratch[0:6, 0:96] = vectors[...]
+    for r in range(3):
+        scratch[6:8, 8 * r : 8 * r + 8] = heads[r]
+    scratch[8:16, 0:12] = hidden[...]
+    s_out[...] = scratch[...].astype(BF16)
+
+
+def spread_kernel(s_ref, vec_out, off_out):
+    row_pick = pick_row()
+    vec = jnp.zeros((16, D), F32)
+    heads = [jnp.zeros((16, D), F32) for _ in range(4)]
+    hidden = [jnp.zeros((1, D), F32) for _ in range(4)]
+    for d in range(8):
+        vec += nn(s_ref[0, d], pick_vector(d))
+        head_pick, places = pick_head(d), hidden_places(d)
+        for m in range(4):
+            heads[m] += nn(s_ref[m, d], head_pick)
+            spread = nn(s_ref[m, d], row_pick)[8:16]
+            hidden[m] += jnp.sum(jnp.where(places, spread, 0.0), axis=0, keepdims=True)
+    vec_out[...] = vec
+    for m in range(4):
+        off_out[m, 0:2, :] = heads[m][6:8]
+        off_out[m, 2:3, :] = hidden[m]
+        off_out[m, 3:8, :] = jnp.zeros((5, D), F32)
+
+
+def squeeze_kernel(fore_ref, back_ref, hid_ref, heads_ref, out_ref, rows):
+    rows[...] = jnp.zeros_like(rows)
+    rows[0:2, :] = back_ref[0:2, :]
+    rows[2:6, :] = fore_ref[0:4, :]
+    row_pick = pick_row()
+    shape = (8, 128)
+    for m in range(4):
+        rows[6:7, 0:192] = heads_ref[m, 0:1, 0:192]
+        rows[7:8, 0:192] = heads_ref[m, 1:2, 0:192]
+        block = rows[...].astype(BF16)
+        wide = jnp.broadcast_to(hid_ref[m, 0:1, :], (8, D))
+        for d in range(8):
+            upper = jnp.where(iota(shape, 0) < 6, nt(block, pick_vector(d)), nt(block, pick_head(d)))
+            lower = nt(jnp.where(hidden_places(d), wide, 0.0).astype(BF16), row_pick)
+            out_ref[m, d] = jnp.concatenate([upper, lower], axis=0).astype(BF16)
+
+
+def ln(values):
+    center = values - jnp.mean(values, axis=-1, keepdims=True)
+    inverse = lax.rsqrt(jnp.mean(center * center, axis=-1, keepdims=True) + LN_EPS)
+    return center * inverse, inverse
+
+
+def ln_back(grad, normed, inverse):
+    return inverse * (
+        grad
+        - jnp.mean(grad, axis=-1, keepdims=True)
+        - normed * jnp.mean(grad * normed, axis=-1, keepdims=True)
+    )
+
+
+def position_rows():
+    plane = np.zeros((128, D), np.float32)
+    time_width, space_width = D // 16 * 4, D // 16 * 6
+
+    def sines(count, width):
+        half = width // 2
+        spread = np.arange(half, dtype=np.float32) / np.float32(half)
+        frequency = np.exp(np.float32(-math.log(10000.0)) * spread).astype(np.float32)
+        angles = np.arange(count, dtype=np.float32)[:, None] * frequency
+        return np.concatenate([np.sin(angles), np.cos(angles)], axis=-1).astype(np.float32)
+
+    plane[0:3, 0:time_width] = sines(3, time_width)
+    plane[3 : 3 + GRID, time_width : time_width + space_width] = sines(GRID, space_width)
+    plane[3 + GRID : 3 + 2 * GRID, time_width + space_width :] = sines(GRID, space_width)
+    parts, rest = [], plane
+    for _ in range(3):
+        part = rest.astype(jnp.bfloat16)
+        parts.append(part)
+        rest = rest - part.astype(np.float32)
+    return np.stack(parts)
+
+
+def spread_lanes(ref, wide):
+    for g in range(D // 128):
+        part = ref[:, :, 128 * g : 128 * g + 128].astype(F32)
+        wide[g] = part.reshape(part.shape[0] * 8, 128)
+
+
+def place_rows(places):
+    frame = (places >= GRID * GRID).astype(jnp.int32) + (places >= 2 * GRID * GRID).astype(jnp.int32)
+    within = places - frame * (GRID * GRID)
+    row = jnp.floor((within.astype(F32) + 0.5) * (1.0 / GRID)).astype(jnp.int32)
+    column = within - row * GRID
+    lane = iota((places.shape[0], 128), 1)
+    hot = (lane == frame) | (lane == 3 + row) | (lane == 3 + GRID + column)
+    return hot.astype(F32).astype(BF16)
+
+
+def attend_kernel(seq, pad, tiles, who, tok_ref, vis_ref, tab_ref, vec_ref, off_ref, w_ref,
+                  x_out, h_out, qkv_out, p_out, o_out, wide, low):
+    m = pl.program_id(0)
+    rows_of = lambda t: pl.ds(pl.multiple_of(t * pad, 16), pad)
+
+    @pl.when(m == 0)
+    def _():
+        spread_lanes(tok_ref, wide)
+        at = (who[0] & 1) * tiles
+        tail = pad - seq
+        for t in range(tiles):
+            hot = place_rows(vis_ref[:, t : t + 1])
+            table = nn(hot, tab_ref[0]) + nn(hot, tab_ref[1]) + nn(hot, tab_ref[2])
+            x_out[t * pad + seq - seq % 8 : (t + 1) * pad, :] = jnp.zeros((tail + seq % 8, D), F32)
+            for g in range(D // 128):
+                lanes = slice(128 * g, 128 * g + 128)
+                x_out[t * pad : t * pad + seq, lanes] = wide[g, pl.ds(at + t, seq, stride=8), :] + table[:, lanes]
+
+        @pl.loop(0, tiles)
+        def _(t):
+            x = x_out[rows_of(t), :]
+            normed, _ = ln(x)
+            low[rows_of(t), :] = (normed * vec_ref[0:1, :] + vec_ref[1:2, :]).astype(BF16)
+            h_out[rows_of(t), :] = x + vec_ref[4:5, :]
+
+    linear = nn(low[...], w_ref[0, :, 0:576])
+    zero = jnp.zeros((1, 192), F32)
+    offset = jnp.concatenate([off_ref[0, 0:1, 0:192], zero, off_ref[0, 1:2, 0:192]], axis=1)
+    qkv_out[0] = (linear + offset).astype(BF16)
+
+    @pl.loop(0, tiles)
+    def _(t):
+        rows = rows_of(t)
+        qkv = qkv_out[0, rows, :]
+        parts = []
+        for h in range(3):
+            q, k, v = (qkv[:, 192 * j + 64 * h : 192 * j + 64 * h + 64] for j in range(3))
+            s = nt(q, k) * 0.125
+            s = jnp.where(iota(s.shape, 1) < seq, s, -1e30)
+            e = jnp.exp(s - jnp.max(s, axis=-1, keepdims=True))
+            low_p = (e * (1.0 / jnp.sum(e, axis=-1, keepdims=True))).astype(BF16)
+            p_out[0, h, rows, :] = low_p
+            parts.append(nn(low_p, v))
+        o_out[0, rows, :] = jnp.concatenate(parts, axis=1).astype(BF16)
+
+    h_out[...] += nt(o_out[0], w_ref[0, :, 576:768])
+
+
+def feed_kernel(seq, pad, tiles, who, cot_ref, h_ref, vec_ref, off_ref, w2_ref, w3_ref,
+                out_out, dh_out, sum_out, hid_out, g2_out, g3_out,
+                wide, c, c_t, dy, dy_t, y, dc):
+    m = pl.program_id(0)
+    rows_of = lambda t: pl.ds(pl.multiple_of(t * pad, 16), pad)
+    at = (who[0] & 1) * tiles
+    first = who[0] * tiles
+
+    @pl.when(m == 0)
+    def _():
+        spread_lanes(cot_ref, wide)
+        y[...] = jnp.zeros_like(y)
+        for t in range(tiles):
+            live = (first + t < who[1]).astype(F32)
+            for g in range(D // 128):
+                lanes = slice(128 * g, 128 * g + 128)
+                y[t * pad : t * pad + seq, lanes] = wide[g, pl.ds(at + t, seq, stride=8), :] * live
+        sum_out[...] = jnp.zeros_like(sum_out)
+
+        @pl.loop(0, tiles)
+        def _(t):
+            grad = y[rows_of(t), :]
+            sum_out[3:4, :] += jnp.sum(grad, axis=0, keepdims=True)
+            dy[rows_of(t), :] = grad.astype(BF16)
+            normed, _ = ln(h_ref[rows_of(t), :])
+            c[rows_of(t), :] = (normed * vec_ref[2:3, :] + vec_ref[3:4, :]).astype(BF16)
+
+        dy_t[...] = dy[...].T
+        c_t[...] = c[...].T
+        y[...] = jnp.zeros_like(y)
+        dc[...] = jnp.zeros_like(dc)
+
+    @pl.loop(0, 3)
+    def _(n):
+        cols = pl.ds(pl.multiple_of(n * 256, 256), 256)
+        u = nn(c[...], w2_ref[0, :, cols]) + off_ref[0, 2:3, cols]
+        cdf = 0.5 * (1.0 + lax.erf(u * math.sqrt(0.5)))
+        r = (u * cdf).astype(BF16)
+        slope = cdf + u * (jnp.exp(-0.5 * u * u) * (1.0 / math.sqrt(2.0 * math.pi)))
+        g3_out[0, :, cols] = nn(dy_t[...], r).astype(BF16)
+        du = (nn(dy[...], w3_ref[0, :, cols]) * slope).astype(BF16)
+        hid_out[0, 0:1, cols] = jnp.sum(du.astype(F32), axis=0, keepdims=True)
+        g2_out[0, :, cols] = nn(c_t[...], du).astype(BF16)
+        y[...] += nt(r, w3_ref[0, :, cols])
+        dc[...] += nt(du, w2_ref[0, :, cols])
+
+    @pl.when(m == pl.num_programs(0) - 1)
+    def _():
+        @pl.loop(0, tiles)
+        def _(t):
+            rows = rows_of(t)
+            live = (first + t < who[1]).astype(F32)
+            h = h_ref[rows, :]
+            out_out[rows, :] = ((h + y[rows, :] + vec_ref[5:6, :]) * live).astype(BF16)
+            normed, inverse = ln(h)
+            grad = dc[rows, :]
+            dh = dy[rows, :].astype(F32) + ln_back(grad * vec_ref[2:3, :], normed, inverse)
+            dh_out[rows, :] = dh
+            sum_out[0:1, :] += jnp.sum(grad * normed, axis=0, keepdims=True)
+            sum_out[1:2, :] += jnp.sum(grad, axis=0, keepdims=True)
+            sum_out[2:3, :] += jnp.sum(dh, axis=0, keepdims=True)
+
+
+def back_kernel(seq, pad, tiles, x_ref, dh_ref, vec_ref, w_ref, qkv_ref, p_ref, o_ref,
+                in_out, sum_out, head_out, g1_out, a_t, dh_low, dh_t, do, dqkv, da):
+    m = pl.program_id(0)
+    rows_of = lambda t: pl.ds(pl.multiple_of(t * pad, 16), pad)
+
+    @pl.when(m == 0)
+    def _():
+        @pl.loop(0, tiles)
+        def _(t):
+            rows = rows_of(t)
+            normed, _ = ln(x_ref[rows, :])
+            dh_low[rows, :] = (normed * vec_ref[0:1, :] + vec_ref[1:2, :]).astype(BF16)
+
+        a_t[...] = dh_low[...].T
+        dh_low[...] = dh_ref[...].astype(BF16)
+        dh_t[...] = dh_low[...].T
+        da[...] = jnp.zeros_like(da)
+        sum_out[...] = jnp.zeros_like(sum_out)
+
+    do[...] = nn(dh_low[...], w_ref[0, :, 576:768]).astype(BF16)
+    g1_out[0, :, 576:768] = nn(dh_t[...], o_ref[0]).astype(BF16)
+
+    @pl.loop(0, tiles)
+    def _(t):
+        rows = rows_of(t)
+        qkv = qkv_ref[0, rows, :]
+        grad = do[rows, :]
+        parts = [[], [], []]
+        for h in range(3):
+            q, k, v = (qkv[:, 192 * j + 64 * h : 192 * j + 64 * h + 64] for j in range(3))
+            g = grad[:, 64 * h : 64 * h + 64]
+            low_p = p_ref[0, h, rows, :]
+            p = low_p.astype(F32)
+            dp = nt(g, v)
+            ds = (p * (dp - jnp.sum(dp * p, axis=-1, keepdims=True))).astype(BF16)
+            parts[0].append(nn(ds, k) * 0.125)
+            parts[1].append(tn(ds, q) * 0.125)
+            parts[2].append(tn(low_p, g))
+        dqkv[rows, :] = jnp.concatenate(parts[0] + parts[1] + parts[2], axis=1).astype(BF16)
+
+    sums = jnp.sum(dqkv[...].astype(F32), axis=0, keepdims=True)
+    head_out[0, 0:1, 0:192] = sums[:, 0:192]
+    head_out[0, 1:2, 0:192] = sums[:, 384:576]
+    g1_out[0, :, 0:576] = nn(a_t[...], dqkv[...]).astype(BF16)
+    da[...] += nt(dqkv[...], w_ref[0, :, 0:576])
+
+    @pl.when(m == pl.num_programs(0) - 1)
+    def _():
+        @pl.loop(0, tiles)
+        def _(t):
+            rows = rows_of(t)
+            normed, inverse = ln(x_ref[rows, :])
+            grad = da[rows, :]
+            back = ln_back(grad * vec_ref[0:1, :], normed, inverse)
+            in_out[rows, :] = (dh_ref[rows, :] + back).astype(BF16)
+            sum_out[0:1, :] += jnp.sum(grad * normed, axis=0, keepdims=True)
+            sum_out[1:2, :] += jnp.sum(grad, axis=0, keepdims=True)
+
+
+def lay_kernel(seq, pad, count, out_ref, in_ref, out_out, in_out, wide):
+    for t in range(count):
+        wide[pl.ds(t, seq, stride=count), :] = out_ref[t, 0:seq, :].astype(F32)
+        in_out[pl.ds(t, seq, stride=count), :] = in_ref[t, 0:seq, :].astype(F32)
+    out_out[...] = wide[...].astype(BF16)
+
+
+def update_kernel(*refs):
+    grad_ref, small_ref = refs[:2]
+    state, outs = refs[2:23], refs[23:]
+    correction = 1.0 - 0.5**STEP
+    rates = ((D // 2) ** -0.5, (D // 16) ** -0.5, D**-0.5, FF**-0.5, 0.1, 0.1, 0.15)
+
+    def update(i, at, gradient):
+        master, first, second = (state[i + 7 * j][at] for j in range(3))
+        decay = DECAY if i < 4 else 0.0
+        values = adamw_update(master, first, second, gradient, rates[i], decay, correction)
+        for j, value in enumerate((gradient,) + values + (values[0].astype(BF16),)):
+            outs[i + 7 * j][at] = value
+
+    every = (slice(None), slice(None))
+    for j in range(3):
+        update(0, (j,) + every, grad_ref[0, :, 192 * j : 192 * j + 192])
+    update(1, every, grad_ref[0, :, 576:768].T)
+    update(2, every, grad_ref[1])
+    update(3, every, grad_ref[2])
+    for r in range(3):
+        update(4, (r,) + every, small_ref[6:8, 8 * r : 8 * r + 8])
+    update(5, every, small_ref[8:16, 0:12])
+    update(6, every, small_ref[0:6, 0:96])
+
+
+class Place:
+    def __init__(self):
+        dp, mp = lax.axis_index("dp"), lax.axis_index("mp")
+        self.z, self.y = dp // 2, dp % 2
+        self.x, self.c = mp // 2, mp % 2
+
+    def id(self, z=None, y=None, x=None, c=None):
+        z, y, x, c = (own if new is None else new for own, new in ((self.z, z), (self.y, y), (self.x, x), (self.c, c)))
+        return (2 * z + y, 2 * x + c)
+
+    def neighbours(self):
+        return [
+            *(self.id(z=(self.z + k) % 4) for k in (1, 2, 3)),
+            self.id(y=1 - self.y),
+            self.id(x=1 - self.x),
+            self.id(c=1 - self.c),
+        ]
+
+    def greet(self):
+        barrier = pltpu.get_barrier_semaphore()
+        for device in self.neighbours():
+            pl.semaphore_signal(barrier, inc=1, device_id=device, device_id_type=MESH)
+        pl.semaphore_wait(barrier, 6)
+
+
+class Sends:
+    def __init__(self, send, recv):
+        self.send, self.recv, self.count, self.all = send, recv, 0, []
+
+    def start(self, src, dst, device):
+        copy = pltpu.make_async_remote_copy(
+            src_ref=src,
+            dst_ref=dst,
+            send_sem=self.send.at[self.count],
+            recv_sem=self.recv.at[self.count],
+            device_id=device,
+            device_id_type=MESH,
+        )
+        self.count += 1
+        copy.start()
+        self.all.append(copy)
+        return copy
+
+    def finish(self):
+        for copy in self.all:
+            copy.wait_send()
+
+
+def arrived(copies):
+    for copy in copies:
+        copy.wait_recv()
+
+
+class Gather:
+    def __init__(self, place, sends, own, full, split):
+        self.p, self.s, self.own, self.full, self.split = place, sends, own, full, split
+        self.core = []
+
+    def along_z(self):
+        p = self.p
+        slot = self.full.at[p.x, p.c, p.z, p.y]
+        self.wait = [self.s.start(self.own, slot, p.id(z=(p.z + k) % 4)) for k in (1, 2, 3)]
+
+    def second(self):
+        p, f, s = self.p, self.full, self.s
+        arrived(self.wait)
+        upper, lower = pl.ds(0, self.split), pl.ds(self.split, f.shape[4] - self.split)
+        part = f.at[p.x, p.c, :, p.y, upper]
+        self.wait = [s.start(part, part, p.id(y=1 - p.y))]
+        if self.split < f.shape[4]:
+            part = f.at[p.x, p.c, :, p.y, lower]
+            self.wait.append(s.start(part, part, p.id(x=1 - p.x)))
+        part = f.at[p.x, p.c, :, p.y]
+        self.core.append(s.start(part, part, p.id(c=1 - p.c)))
+
+    def third(self):
+        p, f, s = self.p, self.full, self.s
+        arrived(self.wait)
+        upper, lower = pl.ds(0, self.split), pl.ds(self.split, f.shape[4] - self.split)
+        part = f.at[p.x, p.c, :, :, upper]
+        self.wait = [s.start(part, part, p.id(x=1 - p.x))]
+        core = [f.at[p.x, p.c, :, 1 - p.y, upper]]
+        if self.split < f.shape[4]:
+            for x in (0, 1):
+                part = f.at[x, p.c, :, p.y, lower]
+                self.wait.append(s.start(part, part, p.id(y=1 - p.y)))
+            core.append(f.at[1 - p.x, p.c, :, p.y, lower])
+        self.core += [s.start(part, part, p.id(c=1 - p.c)) for part in core]
+
+    def last(self):
+        p, f, s = self.p, self.full, self.s
+        arrived(self.wait)
+        upper, lower = pl.ds(0, self.split), pl.ds(self.split, f.shape[4] - self.split)
+        core = [f.at[1 - p.x, p.c, :, :, upper]]
+        if self.split < f.shape[4]:
+            core += [f.at[x, p.c, :, 1 - p.y, lower] for x in (0, 1)]
+        self.core += [s.start(part, part, p.id(c=1 - p.c)) for part in core]
+
+    def done(self):
+        arrived(self.core)
+
+    COUNT = 14
+    COUNT_WHOLE = 8
+
+
+def gather_kernel(w_ref, s_ref, f1, f2, f3, fs, send, recv, local):
+    p = Place()
+    p.greet()
+    s = Sends(send, recv)
+    fulls = [(s_ref, fs, 16), (w_ref.at[0], f1, 48), (w_ref.at[1], f2, 48), (w_ref.at[2], f3, 48)]
+    gathers = [Gather(p, s, own, full, split) for own, full, split in fulls]
+    for g in gathers:
+        g.along_z()
+    copies = []
+    for i, (own, full, _) in enumerate(fulls):
+        copies.append(pltpu.make_async_copy(own, full.at[p.x, p.c, p.z, p.y], local.at[i]))
+        copies[-1].start()
+    for copy in copies:
+        copy.wait()
+    stages = [("second", 0), ("second", 1), ("third", 0), ("second", 2), ("third", 1), ("last", 0), ("second", 3),
+              ("third", 2), ("last", 1), ("third", 3), ("last", 2), ("last", 3)]
+    for name, i in stages:
+        getattr(gathers[i], name)()
+    for g in gathers:
+        g.done()
+    s.finish()
+
+
+def add_into(target, other, lead):
+    total = math.prod(lead)
+
+    @pl.loop(0, total)
+    def _(i):
+        index = []
+        for size in reversed(lead):
+            index.append(i % size)
+            i = i // size
+        index = tuple(reversed(index))
+        target[index] = (target[index].astype(F32) + other(*index).astype(F32)).astype(BF16)
+
+
+class Reduce:
+    def __init__(self, place, sends, parts, r0, r1a, r1b, r2a, r2b, r3a, r3b, split):
+        self.p, self.s, self.parts, self.split = place, sends, parts, split
+        self.r0, self.r1a, self.r1b, self.r2a, self.r2b, self.r3a, self.r3b = r0, r1a, r1b, r2a, r2b, r3a, r3b
+        self.both = r1b is not None
+
+    def cores(self):
+        p = self.p
+        self.wait = [self.s.start(self.parts.at[:, 1 - p.c], self.r0, p.id(c=1 - p.c))]
+
+    def first(self):
+        p, s, h = self.p, self.s, self.split
+        arrived(self.wait)
+        add_into(self.r0, lambda x, z, y: self.parts[x, p.c, z, y], self.r0.shape[:3])
+        self.wait = [s.start(self.r0.at[1 - p.x, :, :, pl.ds(0, h)], self.r1a, p.id(x=1 - p.x))]
+        if self.both:
+            low = pl.ds(h, self.r0.shape[3] - h)
+            self.wait.append(s.start(self.r0.at[:, :, 1 - p.y, low], self.r1b, p.id(y=1 - p.y)))
+
+    def second(self):
+        p, s, h = self.p, self.s, self.split
+        arrived(self.wait)
+        add_into(self.r1a, lambda z, y: self.r0[p.x, z, y, 0:h], self.r1a.shape[:2])
+        self.wait = [s.start(self.r1a.at[:, 1 - p.y], self.r2a, p.id(y=1 - p.y))]
+        if self.both:
+            add_into(self.r1b, lambda x, z: self.r0[x, z, p.y, h:], self.r1b.shape[:2])
+            self.wait.append(s.start(self.r1b.at[1 - p.x], self.r2b, p.id(x=1 - p.x)))
+
+    def third(self):
+        p, s = self.p, self.s
+        arrived(self.wait)
+        add_into(self.r2a, lambda z: self.r1a[z, p.y], self.r2a.shape[:1])
+        if self.both:
+            add_into(self.r2b, lambda z: self.r1b[p.x, z], self.r2b.shape[:1])
+        self.wait = []
+        for k in (1, 2, 3):
+            to = (p.z + k) % 4
+            self.wait.append(s.start(self.r2a.at[to], self.r3a.at[k - 1], p.id(z=to)))
+            if self.both:
+                self.wait.append(s.start(self.r2b.at[to], self.r3b.at[k - 1], p.id(z=to)))
+
+    def last(self, out):
+        p = self.p
+        arrived(self.wait)
+        sum_of = lambda r2, r3: r2[p.z].astype(F32) + r3[0].astype(F32) + r3[1].astype(F32) + r3[2].astype(F32)
+        out[0 : self.split] = sum_of(self.r2a, self.r3a)
+        if self.both:
+            out[self.split :] = sum_of(self.r2b, self.r3b)
+
+    @staticmethod
+    def scratch(rows, columns, split):
+        shapes = [(2, 4, 2, rows), (4, 2, split), (2, 4, rows - split), (4, split), (4, rows - split), (3, split), (3, rows - split)]
+        return [pltpu.VMEM(shape + (columns,), BF16) for shape in shapes if shape[-1] > 0]
+
+
+def reduce_kernel(g1, g2, g3, gs, own_out, own_in, total, small, all_out, all_in, *scratch):
+    *buffers, send, recv, local = scratch
+    p = Place()
+    p.greet()
+    s = Sends(send, recv)
+    reduces = [Reduce(p, s, part, *buffers[7 * i : 7 * i + 7], 48) for i, part in enumerate((g3, g2, g1))]
+    b = buffers[21:]
+    reduces.append(Reduce(p, s, gs, b[0], b[1], None, b[2], None, b[3], None, 16))
+    outs = [total.at[2], total.at[1], total.at[0], small]
+    for r in reduces:
+        r.cores()
+    trades, copies = [], []
+    for i, (own, full) in enumerate(((own_out, all_out), (own_in, all_in))):
+        slot = full.at[p.x, p.c]
+        copies.append(pltpu.make_async_copy(own, slot, local.at[i]))
+        copies[-1].start()
+    for i in range(4):
+        reduces[i].first()
+        if i > 0:
+            reduces[i - 1].second()
+        if i > 1:
+            reduces[i - 2].third()
+    for own, full in ((own_out, all_out), (own_in, all_in)):
+        slot = full.at[p.x, p.c]
+        trades.append([s.start(own, slot, p.id(x=1 - p.x)), s.start(own, slot, p.id(c=1 - p.c))])
+    reduces[3].second()
+    reduces[2].third()
+    reduces[3].third()
+    for r, out in zip(reduces, outs):
+        r.last(out)
+    for trade, full in zip(trades, (all_out, all_in)):
+        arrived(trade[:1])
+        slot = full.at[1 - p.x, p.c]
+        trade.append(s.start(slot, slot, p.id(c=1 - p.c)))
+    for trade in trades:
+        arrived(trade[1:])
+    for copy in copies:
+        copy.wait()
+    s.finish()
+
+
+def fast_shards(*args):
+    (tokens, cotangent, visible, tile_counts, *state) = args
+    tile_count, seq, width = tokens.shape
+    mp_size = lax.axis_size("mp")
+    tiles = tile_count // mp_size
+    pad = -(-seq // 16) * 16
+    rows = tiles * pad
+    native = lambda i, a: a.transpose(1, 0, 2) if i in (0, 4) else a.T if i in (3, 5) else a
+    state = [native(i % 7, a) for i, a in enumerate(state)]
+    params = lambda limit=None, **kw: pltpu.CompilerParams(vmem_limit_bytes=60 << 20, **kw)
+    shape = jax.ShapeDtypeStruct
+    me = lax.axis_index("mp").astype(jnp.int32)
+    who = jnp.stack([me, tile_counts[0]])
+
+    own, own_small = pl.pallas_call(
+        pack_kernel,
+        out_shape=(shape((3, 96, D), BF16), shape((16, 128), BF16)),
+        scratch_shapes=[pltpu.VMEM((16, 128), F32)],
+        compiler_params=params(),
+        name="pack",
+    )(*state[:7])
+
+    full = shape((2, 2, 4, 2, 96, D), BF16)
+    copies = 3 * Gather.COUNT + Gather.COUNT_WHOLE
+    f1, f2, f3, fs = pl.pallas_call(
+        gather_kernel,
+        out_shape=(full, full, full, shape((2, 2, 4, 2, 16, 128), BF16)),
+        in_specs=[pl.BlockSpec(memory_space=pltpu.VMEM)] * 2,
+        out_specs=(pl.BlockSpec(memory_space=ANY),) * 4,
+        scratch_shapes=[
+            pltpu.SemaphoreType.DMA((copies,)),
+            pltpu.SemaphoreType.DMA((copies,)),
+            pltpu.SemaphoreType.DMA((4,)),
+        ],
+        compiler_params=params(collective_id=0, has_side_effects=True),
+        name="gather",
+    )(own, own_small)
+    w1, w2, w3 = (f.reshape(4, D, D) for f in (f1, f2, f3))
+
+    vec, off = pl.pallas_call(
+        spread_kernel,
+        out_shape=(shape((16, D), F32), shape((4, 8, D), F32)),
+        compiler_params=params(),
+        name="spread",
+    )(fs.reshape(4, 8, 16, 128))
+
+    by_place = lambda a: a.transpose(1, 0, 2)
+    half = pl.BlockSpec((seq, 8, D), lambda m, who: (0, who[0] // 2, 0))
+    of_group = lambda *shape: pl.BlockSpec((1,) + shape, lambda m, who: (m,) + (0,) * len(shape))
+    all_of = lambda *shape: pl.BlockSpec(shape, lambda m, who: (0,) * len(shape))
+    places = lax.dynamic_slice(visible, (me * tiles, 0), (tiles, seq)).T
+    table = jnp.asarray(position_rows())
+
+    x, h, qkv, probs, o = pl.pallas_call(
+        functools.partial(attend_kernel, seq, pad, tiles),
+        out_shape=(
+            shape((rows, D), F32),
+            shape((rows, D), F32),
+            shape((4, rows, 576), BF16),
+            shape((4, 3, rows, pad), BF16),
+            shape((4, rows, 192), BF16),
+        ),
+        grid_spec=pltpu.PrefetchScalarGridSpec(
+            num_scalar_prefetch=1,
+            grid=(4,),
+            in_specs=[half, all_of(seq, tiles), all_of(3, 128, D), all_of(16, D), of_group(8, D), of_group(D, D)],
+            out_specs=(all_of(rows, D), all_of(rows, D), of_group(rows, 576), of_group(3, rows, pad), of_group(rows, 192)),
+            scratch_shapes=[pltpu.VMEM((D // 128, seq * 8, 128), F32), pltpu.VMEM((rows, D), BF16)],
+        ),
+        compiler_params=params(),
+        name="attend",
+    )(who, by_place(tokens), places, table, vec, off, w1)
+
+    out_own, dh, sum_two, sum_hid, g2, g3 = pl.pallas_call(
+        functools.partial(feed_kernel, seq, pad, tiles),
+        out_shape=(
+            shape((rows, D), BF16),
+            shape((rows, D), F32),
+            shape((8, D), F32),
+            shape((4, 8, D), F32),
+            shape((4, D, D), BF16),
+            shape((4, D, D), BF16),
+        ),
+        grid_spec=pltpu.PrefetchScalarGridSpec(
+            num_scalar_prefetch=1,
+            grid=(4,),
+            in_specs=[half, all_of(rows, D), all_of(16, D), of_group(8, D), of_group(D, D), of_group(D, D)],
+            out_specs=(all_of(rows, D), all_of(rows, D), all_of(8, D), of_group(8, D), of_group(D, D), of_group(D, D)),
+            scratch_shapes=[
+                pltpu.VMEM((D // 128, seq * 8, 128), F32),
+                pltpu.VMEM((rows, D), BF16),
+                pltpu.VMEM((D, rows), BF16),
+                pltpu.VMEM((rows, D), BF16),
+                pltpu.VMEM((D, rows), BF16),
+                pltpu.VMEM((rows, D), F32),
+                pltpu.VMEM((rows, D), F32),
+            ],
+        ),
+        compiler_params=params(),
+        name="feed",
+    )(who, by_place(cotangent), h, vec, off, w2, w3)
+
+    of_group1 = lambda *shape: pl.BlockSpec((1,) + shape, lambda m: (m,) + (0,) * len(shape))
+    all_of1 = lambda *shape: pl.BlockSpec(shape, lambda m: (0,) * len(shape))
+    in_own, sum_one, sum_head, g1 = pl.pallas_call(
+        functools.partial(back_kernel, seq, pad, tiles),
+        out_shape=(
+            shape((rows, D), BF16),
+            shape((8, D), F32),
+            shape((4, 8, D), F32),
+            shape((4, D, D), BF16),
+        ),
+        grid=(4,),
+        in_specs=[all_of1(rows, D), all_of1(rows, D), all_of1(16, D), of_group1(D, D), of_group1(rows, 576),
+                  of_group1(3, rows, pad), of_group1(rows, 192)],
+        out_specs=(all_of1(rows, D), all_of1(8, D), of_group1(8, D), of_group1(D, D)),
+        scratch_shapes=[
+            pltpu.VMEM((D, rows), BF16),
+            pltpu.VMEM((rows, D), BF16),
+            pltpu.VMEM((D, rows), BF16),
+            pltpu.VMEM((rows, 192), BF16),
+            pltpu.VMEM((rows, 576), BF16),
+            pltpu.VMEM((rows, D), F32),
+        ],
+        compiler_params=params(),
+        name="back",
+    )(x, dh, vec, w1, qkv, probs, o)
+
+    gs = pl.pallas_call(
+        squeeze_kernel,
+        out_shape=shape((4, 8, 16, 128), BF16),
+        scratch_shapes=[pltpu.VMEM((8, D), F32)],
+        compiler_params=params(),
+        name="squeeze",
+    )(sum_two, sum_one, sum_hid, sum_head)
+
+    copies = 3 * 11 + 6 + 6
+    everyone = shape((2, 2, rows, D), BF16)
+    total, small, all_out, all_in = pl.pallas_call(
+        reduce_kernel,
+        out_shape=(shape((3, 96, D), F32), shape((16, 128), F32), everyone, everyone),
+        in_specs=[pl.BlockSpec(memory_space=pltpu.VMEM)] * 4 + [pl.BlockSpec(memory_space=ANY)] * 2,
+        out_specs=(pl.BlockSpec(memory_space=pltpu.VMEM),) * 2 + (pl.BlockSpec(memory_space=ANY),) * 2,
+        scratch_shapes=[
+            *(3 * Reduce.scratch(96, D, 48)),
+            *Reduce.scratch(16, 128, 16),
+            pltpu.SemaphoreType.DMA((copies,)),
+            pltpu.SemaphoreType.DMA((copies,)),
+            pltpu.SemaphoreType.DMA((2,)),
+        ],
+        compiler_params=params(collective_id=1, has_side_effects=True),
+        name="reduce",
+    )(*(g.reshape(2, 2, 4, 2, 96, D) for g in (g1, g2, g3)), gs.reshape(2, 2, 4, 2, 16, 128), out_own, in_own)
+
+    flat = seq * tile_count
+    block = pl.BlockSpec((tile_count, pad, 128), lambda n: (0, 0, n))
+    output, input_grad = pl.pallas_call(
+        functools.partial(lay_kernel, seq, pad, tile_count),
+        out_shape=(shape((flat, D), BF16), shape((flat, D), F32)),
+        grid=(D // 128,),
+        in_specs=[block, block],
+        out_specs=(pl.BlockSpec((flat, 128), lambda n: (0, n)),) * 2,
+        scratch_shapes=[pltpu.VMEM((flat, 128), F32)],
+        compiler_params=params(),
+        name="lay",
+    )(*(a.reshape(tile_count, pad, D) for a in (all_out, all_in)))
+    output, input_grad = (a.reshape(seq, tile_count, D).transpose(1, 0, 2) for a in (output, input_grad))
+
+    kinds = [shape(a.shape, F32) for a in state[:7]]
+    results = pl.pallas_call(
+        update_kernel,
+        out_shape=tuple(kinds * 4 + [shape(a.shape, BF16) for a in kinds]),
+        compiler_params=params(),
+        name="update",
+    )(total, small, *state)
+    return (output, input_grad) + tuple(native(i % 7, a) for i, a in enumerate(results))
+
+
 def solution(mesh):
     in_specs = (
         P("dp", None, None),
@@ -418,4 +1190,6 @@
         P("mp", "dp"),
         P(None, "dp"),
     )
-    return jax.shard_map(shards, mesh=mesh, in_specs=in_specs, out_specs=out_specs, check_vma=False)
+    sizes = (mesh.shape["dp"], mesh.shape["mp"])
+    body = fast_shards if sizes == (8, 4) else shards
+    return jax.shard_map(body, mesh=mesh, in_specs=in_specs, out_specs=out_specs, check_vma=False)

time: 827 us -> 349 us (0.42); the launches traced: 817 us -> 349 us
  Pallas kernels: 0 us -> 346 us
  waiting for transfers between devices: 197 us -> 0 us
  blocking collectives: 183 us -> 0 us
  local copies, waits for them, and re-layouts: 151 us -> 0.78 us
  other arithmetic: 114 us -> 0.59 us
  matrix products: 112 us -> 0 us
  starting transfers between devices: 42.1 us -> 0 us
  between operations: 17 us -> 1.55 us
    pallas_call x0 -> x10, Pallas kernels: none -> 346 us  [the longest x1 123 us: fast_shards(): pl.pallas_call(reduce_kernel, out_shape=(shape((3, 96, D), F32), shape((1...]
    all_gather x5 -> x0, blocking collectives: 149 us -> none  [the longest x1 33.2 us: shards(): lax.all_gather(attend_weight.astype(jnp.bfloat16), 'dp', axis=0, tiled=True)]
    psum x3 -> x0, waiting for transfers between devices: 137 us -> none  [the longest x1 68.1 us: shards(): lax.psum(normed_two_part.astype(jnp.bfloat16), 'mp').astype(jnp.float32)]
    dot_general x18 -> x0, matrix products: 112 us -> none  [the longest x4 25.8 us: over_rows(): lax.dot_general(former, latter, (((0,), (0,)), ((), ())), preferred_eleme...]
    reduce_sum x19 -> x0, other arithmetic: 55.2 us -> none  [the longest x2 12.9 us: normalize(): center = values - jnp.mean(values, axis=-1, keepdims=True)]
    all_gather x2 -> x0, waiting for transfers between devices: 39.3 us -> none  [the longest x1 39.3 us: shards(): lax.all_gather(narrow_weight.astype(jnp.bfloat16), 'dp', axis=1, tiled=True)]
    unnamed x155 -> x5, local copies, waits for them, and re-layouts: 36.8 us -> 0.77 us
    all_to_all x1 -> x0, blocking collectives: 34.1 us -> none  [summed_on_arrival(): parts = lax.all_to_all(cut_along(x, dim, size), axis, 0, 0, tiled=True)]
  transfers between devices with their start and end apart: 11 -> 0, of which waited for: 7 -> 0; matrix products, arithmetic and copies ran while one was open for 25% -> 0% of each run, Pallas kernels for 0% -> 0%
where the time goes in v1:
time: 349 us
  Pallas kernels  346 us (99%)
    pallas_call x1, Pallas kernels, fast_shards(): pl.pallas_call(reduce_kernel, out_shape=(shape((3, 96, D), F32), shape((1...  123 us
    pallas_call x1, Pallas kernels, fast_shards(): pl.pallas_call(gather_kernel, out_shape=(full, full, full, shape((2, 2, 4...  92 us
    pallas_call x1, Pallas kernels, fast_shards(): pl.pallas_call(functools.partial(back_kernel, seq, pad, tiles), out_shape...  40.4 us
    pallas_call x1, Pallas kernels, fast_shards(): pl.pallas_call(functools.partial(feed_kernel, seq, pad, tiles), out_shape...  37.3 us
    pallas_call x1, Pallas kernels, fast_shards(): pl.pallas_call(functools.partial(attend_kernel, seq, pad, tiles), out_sha...  29.8 us
    pallas_call x1, Pallas kernels, fast_shards(): pl.pallas_call(functools.partial(lay_kernel, seq, pad, tile_count), out_s...  11.9 us

profile of v1, /device:TPU:0, one launch (start us, length us, event | category | flops | bytes accessed | tf_op | source)
XLA Modules:
  0.0 349.0 jit_solution(5893755564763893334)
XLA Ops:
  0.7 0.0 copy-start
  1.4 0.6 pad_add_fusion.who
  1.9 0.0 copy-done
  2.0 0.8 copy.64
  2.7 2.1 pack.1
  4.8 92.0 %gather.1 = (bf16[2,2,4,2,96,768]{5,4,3,2,1,0:T(8,128)(2,1)}, bf16[2,2,4,2,96,768]{5,4,3,2,1,0:T(8,128)(2,1)}, bf16[2,2,4,2,96,768]{5,4,3,2,1,0:T(8,128)(2,1)}, bf16[2,2,4,2,16,128]{5,4,3,2,1,0:T(8,128)(2,1)}) custom-call(bf16[3,96,768]{2,1,0:T(8,128)(2,1)} %get-tuple-element.101.w_ref, bf16[16,128]{1,0:T(8,128)(2,1)} %get-tuple-element.102.s_ref), custom_call_target="tpu_custom_call" | custom-call | tf_op jit(solution)/shard_map/gather/pallas_call | solution.py:972
  96.9 2.2 spread.1
  99.1 29.8 %attend.1 = (f32[640,768]{1,0:T(8,128)}, f32[640,768]{1,0:T(8,128)}, bf16[4,640,576]{2,1,0:T(8,128)(2,1)}, bf16[4,3,640,160]{3,2,1,0:T(8,128)(2,1)}, bf16[4,640,192]{2,1,0:T(8,128)(2,1)}) custom-call(s32[2]{0:T(128)} %pad_add_fusion.who, bf16[147,16,768]{2,1,0:T(8,128)(2,1)} %bitcast.62, s32[147,4]{1,0:T(8,128)} %bitcast.68, ...), custom_call_target="tpu_custom_call" | custom-call | tf_op jit(solution)/shard_map/attend/pallas_call | solution.py:1001
  128.9 37.3 %feed.1 = (bf16[640,768]{1,0:T(8,128)(2,1)}, f32[640,768]{1,0:T(8,128)}, f32[8,768]{1,0:T(8,128)}, f32[4,8,768]{2,1,0:T(8,128)}, bf16[4,768,768]{2,1,0:T(8,128)(2,1)}, /*index=5*/bf16[4,768,768]{2,1,0:T(8,128)(2,1)}) custom-call(s32[2]{0:T(128)} %pad_add_fusion.who, bf16[147,16,768]{2,1,0:T(8,128)(2,1)} %bitcast.61, f32[640,768]{1,0:T(8,128)} %get-tuple-element.108.h_ref, ...), custom_call_target="tpu_custom_call" | custom-call | tf_op jit(solution)/shard_map/feed/pallas_call | solution.py:1021
  166.2 40.4 %back.1 = (bf16[640,768]{1,0:T(8,128)(2,1)}, f32[8,768]{1,0:T(8,128)}, f32[4,8,768]{2,1,0:T(8,128)}, bf16[4,768,768]{2,1,0:T(8,128)(2,1)}) custom-call(f32[640,768]{1,0:T(8,128)} %get-tuple-element.107.x_ref, f32[640,768]{1,0:T(8,128)} %get-tuple-element.111.dh_ref, f32[16,768]{1,0:T(8,128)} %get-tuple-element.104.vec_ref, bf16[4,768,768]{2,1,0:T(8,128)(2,1)} %bitcast.53, ...), custom_call_target="tpu_custom_call" | custom-call | tf_op jit(solution)/shard_map/back/pallas_call | solution.py:1052
  206.6 3.1 squeeze.1
  209.6 122.5 %reduce.1 = (f32[3,96,768]{2,1,0:T(8,128)}, f32[16,128]{1,0:T(8,128)}, bf16[2,2,640,768]{3,2,1,0:T(8,128)(2,1)}, bf16[2,2,640,768]{3,2,1,0:T(8,128)(2,1)}) custom-call(bf16[2,2,4,2,96,768]{5,4,3,2,1,0:T(8,128)(2,1)} %bitcast.58, bf16[2,2,4,2,96,768]{5,4,3,2,1,0:T(8,128)(2,1)} %bitcast.56, bf16[2,2,4,2,96,768]{5,4,3,2,1,0:T(8,128)(2,1)} %bitcast.57, ...), custom_call_target="tpu_custom_call" | custom-call | tf_op jit(solution)/shard_map/reduce/pallas_call | solution.py:1086
  332.2 0.0 copy-start.1
  332.2 11.9 %lay.1 = (bf16[2352,768]{1,0:T(8,128)(2,1)}, f32[2352,768]{1,0:T(8,128)}) custom-call(bf16[16,160,768]{2,1,0:T(8,128)(2,1)} %bitcast.59, bf16[16,160,768]{2,1,0:T(8,128)(2,1)} %bitcast.60), custom_call_target="tpu_custom_call" | custom-call | tf_op jit(solution)/shard_map/lay/pallas_call | solution.py:1104
  344.0 4.8 %update.1 = (f32[3,96,192]{2,1,0:T(8,128)}, f32[192,96]{1,0:T(8,128)}, f32[96,768]{1,0:T(8,128)}, f32[96,768]{1,0:T(8,128)}, f32[3,2,8]{2,1,0:T(2,128)}, /*index...) custom-call(f32[3,96,768]{2,1,0:T(8,128)} %get-tuple-element.128.ref, ...), custom_call_target="tpu_custom_call" | custom-call | tf_op jit(solution)/shard_map/update/pallas_call | solution.py:1117
  348.8 0.0 copy-done.1
  (1 shorter events, 0.0 us)
Async XLA Ops:
  0.7 1.3 copy-start
  332.2 16.6 %copy-start.1 = (s32[16,147]{1,0:T(8,128)S(1)}, s32[16,147]{1,0:T(8,128)}, u32[]{:S(2)}) copy-start(s32[16,147]{1,0:T(8,128)} %param.28) | copy-start | bytes 28228

commit v2 on v1

--- a/solution.py
+++ b/solution.py
@@ -506,27 +506,52 @@
     return hot.astype(F32).astype(BF16)
 
 
-def attend_kernel(seq, pad, tiles, who, tok_ref, vis_ref, tab_ref, vec_ref, off_ref, w_ref,
-                  x_out, h_out, qkv_out, p_out, o_out, wide, low):
+def prep_kernel(seq, pad, tiles, who, tok_ref, cot_ref, vis_ref, tab_ref, x_out, dy_out, wide, grad):
+    at = (who[0] & 1) * tiles
+    first = who[0] * tiles
+    head = seq - seq % 8
+    spread_lanes(tok_ref, wide)
+    for t in range(tiles):
+        hot = place_rows(vis_ref[:, t : t + 1])
+        table = nn(hot, tab_ref[0]) + nn(hot, tab_ref[1]) + nn(hot, tab_ref[2])
+        x_out[t * pad + head : (t + 1) * pad, :] = jnp.zeros((pad - head, D), F32)
+        for g in range(D // 128):
+            lanes = slice(128 * g, 128 * g + 128)
+            x_out[t * pad : t * pad + seq, lanes] = wide[g, pl.ds(at + t, seq, stride=8), :] + table[:, lanes]
+    spread_lanes(cot_ref, wide)
+    for t in range(tiles):
+        live = (first + t < who[1]).astype(F32)
+        grad[t * pad + head : (t + 1) * pad, :] = jnp.zeros((pad - head, D), F32)
+        for g in range(D // 128):
+            lanes = slice(128 * g, 128 * g + 128)
+            grad[t * pad : t * pad + seq, lanes] = wide[g, pl.ds(at + t, seq, stride=8), :] * live
+    dy_out[...] = grad[...].astype(BF16)
+
+
+def attend_kernel(seq, pad, tiles, x_ref, vec_ref, off_ref, w_ref, col2, own3,
+                  h_out, qkv_out, p_out, o_out, f2, f3, low, send, recv, local):
     m = pl.program_id(0)
     rows_of = lambda t: pl.ds(pl.multiple_of(t * pad, 16), pad)
+    p = Place()
+    s = Sends(send, recv)
+    g2 = Gather(p, s, f2, 48, column=col2)
+    g3 = Gather(p, s, f3, 48, own=own3)
+    mine = [
+        pltpu.make_async_copy(col2, f2.at[p.x, p.c, :, p.y], local.at[0]),
+        pltpu.make_async_copy(own3, f3.at[p.x, p.c, p.z, p.y], local.at[1]),
+    ]
 
     @pl.when(m == 0)
     def _():
-        spread_lanes(tok_ref, wide)
-        at = (who[0] & 1) * tiles
-        tail = pad - seq
-        for t in range(tiles):
-            hot = place_rows(vis_ref[:, t : t + 1])
-            table = nn(hot, tab_ref[0]) + nn(hot, tab_ref[1]) + nn(hot, tab_ref[2])
-            x_out[t * pad + seq - seq % 8 : (t + 1) * pad, :] = jnp.zeros((tail + seq % 8, D), F32)
-            for g in range(D // 128):
-                lanes = slice(128 * g, 128 * g + 128)
-                x_out[t * pad : t * pad + seq, lanes] = wide[g, pl.ds(at + t, seq, stride=8), :] + table[:, lanes]
+        p.greet()
+        g2.second()
+        g3.along_z()
+        for copy in mine:
+            copy.start()
 
         @pl.loop(0, tiles)
         def _(t):
-            x = x_out[rows_of(t), :]
+            x = x_ref[rows_of(t), :]
             normed, _ = ln(x)
             low[rows_of(t), :] = (normed * vec_ref[0:1, :] + vec_ref[1:2, :]).astype(BF16)
             h_out[rows_of(t), :] = x + vec_ref[4:5, :]
@@ -553,31 +578,42 @@
 
     h_out[...] += nt(o_out[0], w_ref[0, :, 576:768])
 
-
-def feed_kernel(seq, pad, tiles, who, cot_ref, h_ref, vec_ref, off_ref, w2_ref, w3_ref,
-                out_out, dh_out, sum_out, hid_out, g2_out, g3_out,
-                wide, c, c_t, dy, dy_t, y, dc):
+    @pl.when(m == 0)
+    def _():
+        for copy in mine:
+            copy.wait()
+        g2.third()
+
+    @pl.when(m == 1)
+    def _():
+        g3.second()
+
+    @pl.when(m == 2)
+    def _():
+        g2.last()
+
+    @pl.when(m == 3)
+    def _():
+        g3.third()
+        g3.last()
+        g2.done()
+        g3.done()
+        s.finish()
+
+
+def feed_kernel(seq, pad, tiles, who, dy, h_ref, vec_ref, off_ref, w2_ref, w3_ref,
+                out_out, dh_out, sum_out, hid_out, g2_out, g3_out, c, c_t, dy_t, y, dc):
     m = pl.program_id(0)
     rows_of = lambda t: pl.ds(pl.multiple_of(t * pad, 16), pad)
-    at = (who[0] & 1) * tiles
     first = who[0] * tiles
 
     @pl.when(m == 0)
     def _():
-        spread_lanes(cot_ref, wide)
-        y[...] = jnp.zeros_like(y)
-        for t in range(tiles):
-            live = (first + t < who[1]).astype(F32)
-            for g in range(D // 128):
-                lanes = slice(128 * g, 128 * g + 128)
-                y[t * pad : t * pad + seq, lanes] = wide[g, pl.ds(at + t, seq, stride=8), :] * live
         sum_out[...] = jnp.zeros_like(sum_out)
 
         @pl.loop(0, tiles)
         def _(t):
-            grad = y[rows_of(t), :]
-            sum_out[3:4, :] += jnp.sum(grad, axis=0, keepdims=True)
-            dy[rows_of(t), :] = grad.astype(BF16)
+            sum_out[3:4, :] += jnp.sum(dy[rows_of(t), :].astype(F32), axis=0, keepdims=True)
             normed, _ = ln(h_ref[rows_of(t), :])
             c[rows_of(t), :] = (normed * vec_ref[2:3, :] + vec_ref[3:4, :]).astype(BF16)
 
@@ -708,47 +744,51 @@
     update(6, every, small_ref[0:6, 0:96])
 
 
+ALL = slice(None)
+
+
 class Place:
     def __init__(self):
         dp, mp = lax.axis_index("dp"), lax.axis_index("mp")
         self.z, self.y = dp // 2, dp % 2
         self.x, self.c = mp // 2, mp % 2
+        self.zs = [(self.z + k) % 4 for k in (1, 2, 3)]
+        self.oy, self.ox, self.oc = 1 - self.y, 1 - self.x, 1 - self.c
+        self.to_z = [self.id(z=z) for z in self.zs]
+        self.to_y, self.to_x, self.to_c = self.id(y=self.oy), self.id(x=self.ox), self.id(c=self.oc)
 
     def id(self, z=None, y=None, x=None, c=None):
         z, y, x, c = (own if new is None else new for own, new in ((self.z, z), (self.y, y), (self.x, x), (self.c, c)))
         return (2 * z + y, 2 * x + c)
 
-    def neighbours(self):
-        return [
-            *(self.id(z=(self.z + k) % 4) for k in (1, 2, 3)),
-            self.id(y=1 - self.y),
-            self.id(x=1 - self.x),
-            self.id(c=1 - self.c),
-        ]
-
     def greet(self):
         barrier = pltpu.get_barrier_semaphore()
-        for device in self.neighbours():
+        for device in (*self.to_z, self.to_y, self.to_x, self.to_c):
             pl.semaphore_signal(barrier, inc=1, device_id=device, device_id_type=MESH)
         pl.semaphore_wait(barrier, 6)
 
 
 class Sends:
     def __init__(self, send, recv):
-        self.send, self.recv, self.count, self.all = send, recv, 0, []
+        self.send, self.recv, self.all = send, recv, []
+
+    def copy(self, src, dst, device):
+        i = len(self.all)
+        self.all.append(
+            pltpu.make_async_remote_copy(
+                src_ref=src,
+                dst_ref=dst,
+                send_sem=self.send.at[i],
+                recv_sem=self.recv.at[i],
+                device_id=device,
+                device_id_type=MESH,
+            )
+        )
+        return self.all[-1]
 
     def start(self, src, dst, device):
-        copy = pltpu.make_async_remote_copy(
-            src_ref=src,
-            dst_ref=dst,
-            send_sem=self.send.at[self.count],
-            recv_sem=self.recv.at[self.count],
-            device_id=device,
-            device_id_type=MESH,
-        )
-        self.count += 1
+        copy = self.copy(src, dst, device)
         copy.start()
-        self.all.append(copy)
         return copy
 
     def finish(self):
@@ -756,83 +796,88 @@
             copy.wait_send()
 
 
+def start(copies):
+    for copy in copies:
+        copy.start()
+
+
 def arrived(copies):
     for copy in copies:
         copy.wait_recv()
 
 
 class Gather:
-    def __init__(self, place, sends, own, full, split):
-        self.p, self.s, self.own, self.full, self.split = place, sends, own, full, split
-        self.core = []
+    def __init__(self, p, s, full, split, cols=ALL, own=None, column=None):
+        every = full.shape[4]
+        at = lambda x, c, z, y, rows: full.at[x, c, z, y, rows, cols]
+        col = lambda rows: at(p.x, p.c, ALL, p.y, rows) if column is None else column.at[:, rows, cols]
+        both = lambda view, device: s.copy(view, view, device)
+        high, low = pl.ds(0, split), pl.ds(split, every - split)
+        here = at(p.x, p.c, p.z, p.y, ALL)
+        self.z = [s.copy(own, here, device) for device in p.to_z] if column is None else []
+        self.two = [s.copy(col(high), at(p.x, p.c, ALL, p.y, high), p.to_y)]
+        self.three = [both(at(p.x, p.c, ALL, ALL, high), p.to_x)]
+        self.core_two = [s.copy(col(ALL), at(p.x, p.c, ALL, p.y, ALL), p.to_c)]
+        self.core_three = [both(at(p.x, p.c, ALL, p.oy, high), p.to_c)]
+        self.core_last = [both(at(p.ox, p.c, ALL, ALL, high), p.to_c)]
+        if split < every:
+            self.two.append(s.copy(col(low), at(p.x, p.c, ALL, p.y, low), p.to_x))
+            self.three += [both(at(x, p.c, ALL, p.y, low), p.to_y) for x in (0, 1)]
+            self.core_three.append(both(at(p.ox, p.c, ALL, p.y, low), p.to_c))
+            self.core_last += [both(at(x, p.c, ALL, p.oy, low), p.to_c) for x in (0, 1)]
 
     def along_z(self):
-        p = self.p
-        slot = self.full.at[p.x, p.c, p.z, p.y]
-        self.wait = [self.s.start(self.own, slot, p.id(z=(p.z + k) % 4)) for k in (1, 2, 3)]
+        start(self.z)
 
     def second(self):
-        p, f, s = self.p, self.full, self.s
-        arrived(self.wait)
-        upper, lower = pl.ds(0, self.split), pl.ds(self.split, f.shape[4] - self.split)
-        part = f.at[p.x, p.c, :, p.y, upper]
-        self.wait = [s.start(part, part, p.id(y=1 - p.y))]
-        if self.split < f.shape[4]:
-            part = f.at[p.x, p.c, :, p.y, lower]
-            self.wait.append(s.start(part, part, p.id(x=1 - p.x)))
-        part = f.at[p.x, p.c, :, p.y]
-        self.core.append(s.start(part, part, p.id(c=1 - p.c)))
+        arrived(self.z)
+        start(self.two)
+        start(self.core_two)
 
     def third(self):
-        p, f, s = self.p, self.full, self.s
-        arrived(self.wait)
-        upper, lower = pl.ds(0, self.split), pl.ds(self.split, f.shape[4] - self.split)
-        part = f.at[p.x, p.c, :, :, upper]
-        self.wait = [s.start(part, part, p.id(x=1 - p.x))]
-        core = [f.at[p.x, p.c, :, 1 - p.y, upper]]
-        if self.split < f.shape[4]:
-            for x in (0, 1):
-                part = f.at[x, p.c, :, p.y, lower]
-                self.wait.append(s.start(part, part, p.id(y=1 - p.y)))
-            core.append(f.at[1 - p.x, p.c, :, p.y, lower])
-        self.core += [s.start(part, part, p.id(c=1 - p.c)) for part in core]
+        arrived(self.two)
+        start(self.three)
+        start(self.core_three)
 
     def last(self):
-        p, f, s = self.p, self.full, self.s
-        arrived(self.wait)
-        upper, lower = pl.ds(0, self.split), pl.ds(self.split, f.shape[4] - self.split)
-        core = [f.at[1 - p.x, p.c, :, :, upper]]
-        if self.split < f.shape[4]:
-            core += [f.at[x, p.c, :, 1 - p.y, lower] for x in (0, 1)]
-        self.core += [s.start(part, part, p.id(c=1 - p.c)) for part in core]
+        arrived(self.three)
+        start(self.core_last)
 
     def done(self):
-        arrived(self.core)
-
-    COUNT = 14
-    COUNT_WHOLE = 8
-
-
-def gather_kernel(w_ref, s_ref, f1, f2, f3, fs, send, recv, local):
+        arrived(self.core_two + self.core_three + self.core_last)
+
+    COPIES = 14
+    COPIES_WHOLE = 8
+
+
+def gather_kernel(w_ref, s_ref, f1, col2, fs, send, recv, local):
     p = Place()
     p.greet()
     s = Sends(send, recv)
-    fulls = [(s_ref, fs, 16), (w_ref.at[0], f1, 48), (w_ref.at[1], f2, 48), (w_ref.at[2], f3, 48)]
-    gathers = [Gather(p, s, own, full, split) for own, full, split in fulls]
+    half = pl.ds(0, 384), pl.ds(384, 384)
+    gathers = [
+        Gather(p, s, fs, 16, own=s_ref),
+        *(Gather(p, s, f1, 48, cols, own=w_ref.at[0, :, cols]) for cols in half),
+    ]
     for g in gathers:
         g.along_z()
-    copies = []
-    for i, (own, full, _) in enumerate(fulls):
-        copies.append(pltpu.make_async_copy(own, full.at[p.x, p.c, p.z, p.y], local.at[i]))
-        copies[-1].start()
-    for copy in copies:
+    ahead = [s.copy(w_ref.at[1], col2.at[p.z], device) for device in p.to_z]
+    start(ahead)
+    mine = [
+        pltpu.make_async_copy(s_ref, fs.at[p.x, p.c, p.z, p.y], local.at[0]),
+        pltpu.make_async_copy(w_ref.at[0], f1.at[p.x, p.c, p.z, p.y], local.at[1]),
+        pltpu.make_async_copy(w_ref.at[1], col2.at[p.z], local.at[2]),
+    ]
+    start(mine)
+    for copy in mine:
         copy.wait()
-    stages = [("second", 0), ("second", 1), ("third", 0), ("second", 2), ("third", 1), ("last", 0), ("second", 3),
-              ("third", 2), ("last", 1), ("third", 3), ("last", 2), ("last", 3)]
+    stages = [("second", 0), ("second", 1), ("third", 0), ("last", 0), ("second", 2), ("third", 1), ("third", 2),
+              ("last", 1), ("last", 2)]
     for name, i in stages:
         getattr(gathers[i], name)()
     for g in gathers:
         g.done()
+    arrived(ahead)
     s.finish()
 
 
@@ -968,21 +1013,18 @@
     )(*state[:7])
 
     full = shape((2, 2, 4, 2, 96, D), BF16)
-    copies = 3 * Gather.COUNT + Gather.COUNT_WHOLE
-    f1, f2, f3, fs = pl.pallas_call(
+    dma = lambda count: pltpu.SemaphoreType.DMA((count,))
+    copies = 2 * Gather.COPIES + Gather.COPIES_WHOLE + 3
+    f1, col2, fs = pl.pallas_call(
         gather_kernel,
-        out_shape=(full, full, full, shape((2, 2, 4, 2, 16, 128), BF16)),
+        out_shape=(full, shape((4, 96, D), BF16), shape((2, 2, 4, 2, 16, 128), BF16)),
         in_specs=[pl.BlockSpec(memory_space=pltpu.VMEM)] * 2,
-        out_specs=(pl.BlockSpec(memory_space=ANY),) * 4,
-        scratch_shapes=[
-            pltpu.SemaphoreType.DMA((copies,)),
-            pltpu.SemaphoreType.DMA((copies,)),
-            pltpu.SemaphoreType.DMA((4,)),
-        ],
+        out_specs=(pl.BlockSpec(memory_space=ANY),) * 3,
+        scratch_shapes=[dma(copies), dma(copies), dma(3)],
         compiler_params=params(collective_id=0, has_side_effects=True),
         name="gather",
     )(own, own_small)
-    w1, w2, w3 = (f.reshape(4, D, D) for f in (f1, f2, f3))
+    w1 = f1.reshape(4, D, D)
 
     vec, off = pl.pallas_call(
         spread_kernel,
@@ -998,25 +1040,42 @@
     places = lax.dynamic_slice(visible, (me * tiles, 0), (tiles, seq)).T
     table = jnp.asarray(position_rows())
 
-    x, h, qkv, probs, o = pl.pallas_call(
+    x, dy = pl.pallas_call(
+        functools.partial(prep_kernel, seq, pad, tiles),
+        out_shape=(shape((rows, D), F32), shape((rows, D), BF16)),
+        grid_spec=pltpu.PrefetchScalarGridSpec(
+            num_scalar_prefetch=1,
+            grid=(1,),
+            in_specs=[half, half, all_of(seq, tiles), all_of(3, 128, D)],
+            out_specs=(all_of(rows, D),) * 2,
+            scratch_shapes=[pltpu.VMEM((D // 128, seq * 8, 128), F32), pltpu.VMEM((rows, D), F32)],
+        ),
+        compiler_params=params(),
+        name="prep",
+    )(who, by_place(tokens), by_place(cotangent), places, table)
+
+    of_group1 = lambda *shape: pl.BlockSpec((1,) + shape, lambda m: (m,) + (0,) * len(shape))
+    all_of1 = lambda *shape: pl.BlockSpec(shape, lambda m: (0,) * len(shape))
+    copies = Gather.COPIES * 2 - 3
+    h, qkv, probs, o, f2, f3 = pl.pallas_call(
         functools.partial(attend_kernel, seq, pad, tiles),
         out_shape=(
-            shape((rows, D), F32),
             shape((rows, D), F32),
             shape((4, rows, 576), BF16),
             shape((4, 3, rows, pad), BF16),
             shape((4, rows, 192), BF16),
+            full,
+            full,
         ),
-        grid_spec=pltpu.PrefetchScalarGridSpec(
-            num_scalar_prefetch=1,
-            grid=(4,),
-            in_specs=[half, all_of(seq, tiles), all_of(3, 128, D), all_of(16, D), of_group(8, D), of_group(D, D)],
-            out_specs=(all_of(rows, D), all_of(rows, D), of_group(rows, 576), of_group(3, rows, pad), of_group(rows, 192)),
-            scratch_shapes=[pltpu.VMEM((D // 128, seq * 8, 128), F32), pltpu.VMEM((rows, D), BF16)],
-        ),
-        compiler_params=params(),
+        grid=(4,),
+        in_specs=[all_of1(rows, D), all_of1(16, D), of_group1(8, D), of_group1(D, D), all_of1(4, 96, D), all_of1(96, D)],
+        out_specs=(all_of1(rows, D), of_group1(rows, 576), of_group1(3, rows, pad), of_group1(rows, 192))
+        + (pl.BlockSpec(memory_space=ANY),) * 2,
+        scratch_shapes=[pltpu.VMEM((rows, D), BF16), dma(copies), dma(copies), dma(2)],
+        compiler_params=params(collective_id=2, has_side_effects=True),
         name="attend",
-    )(who, by_place(tokens), places, table, vec, off, w1)
+    )(x, vec, off, w1, col2, own[2])
+    w2, w3 = (f.reshape(4, D, D) for f in (f2, f3))
 
     out_own, dh, sum_two, sum_hid, g2, g3 = pl.pallas_call(
         functools.partial(feed_kernel, seq, pad, tiles),
@@ -1031,13 +1090,11 @@
         grid_spec=pltpu.PrefetchScalarGridSpec(
             num_scalar_prefetch=1,
             grid=(4,),
-            in_specs=[half, all_of(rows, D), all_of(16, D), of_group(8, D), of_group(D, D), of_group(D, D)],
+            in_specs=[all_of(rows, D), all_of(rows, D), all_of(16, D), of_group(8, D), of_group(D, D), of_group(D, D)],
             out_specs=(all_of(rows, D), all_of(rows, D), all_of(8, D), of_group(8, D), of_group(D, D), of_group(D, D)),
             scratch_shapes=[
-                pltpu.VMEM((D // 128, seq * 8, 128), F32),
                 pltpu.VMEM((rows, D), BF16),
                 pltpu.VMEM((D, rows), BF16),
-                pltpu.VMEM((rows, D), BF16),
                 pltpu.VMEM((D, rows), BF16),
                 pltpu.VMEM((rows, D), F32),
                 pltpu.VMEM((rows, D), F32),
@@ -1045,10 +1102,8 @@
         ),
         compiler_params=params(),
         name="feed",
-    )(who, by_place(cotangent), h, vec, off, w2, w3)
-
-    of_group1 = lambda *shape: pl.BlockSpec((1,) + shape, lambda m: (m,) + (0,) * len(shape))
-    all_of1 = lambda *shape: pl.BlockSpec(shape, lambda m: (0,) * len(shape))
+    )(who, dy, h, vec, off, w2, w3)
+
     in_own, sum_one, sum_head, g1 = pl.pallas_call(
         functools.partial(back_kernel, seq, pad, tiles),
         out_shape=(

time: 349 us -> 330 us (0.946)
  Pallas kernels: 346 us -> 325 us
    pallas_call x1 -> x2, Pallas kernels: 92 us -> 50.2 us  [the longest x1 43.1 us: fast_shards(): pl.pallas_call(gather_kernel, out_shape=(full, shape((4, 96, D), BF16), s...]
    pallas_call x1, Pallas kernels: 29.8 us -> 55.7 us  [fast_shards(): pl.pallas_call(functools.partial(attend_kernel, seq, pad, tiles), out_sha...]
    pallas_call x1, Pallas kernels: 123 us -> 118 us  [fast_shards(): pl.pallas_call(reduce_kernel, out_shape=(shape((3, 96, D), F32), shape((1...]
where the time goes in v2:
time: 330 us; the launch traced here: 329 us
  Pallas kernels  325 us (98%)
    pallas_call x1, Pallas kernels, fast_shards(): pl.pallas_call(reduce_kernel, out_shape=(shape((3, 96, D), F32), shape((1...  118 us
    pallas_call x1, Pallas kernels, fast_shards(): pl.pallas_call(functools.partial(attend_kernel, seq, pad, tiles), out_sha...  55.7 us
    pallas_call x1, Pallas kernels, fast_shards(): pl.pallas_call(gather_kernel, out_shape=(full, shape((4, 96, D), BF16), s...  43.1 us
    pallas_call x1, Pallas kernels, fast_shards(): pl.pallas_call(functools.partial(back_kernel, seq, pad, tiles), out_shape...  40.4 us
    pallas_call x1, Pallas kernels, fast_shards(): pl.pallas_call(functools.partial(feed_kernel, seq, pad, tiles), out_shape...  36.2 us
    pallas_call x1, Pallas kernels, fast_shards(): pl.pallas_call(functools.partial(lay_kernel, seq, pad, tile_count), out_s...  11.9 us
    pallas_call x1, Pallas kernels, fast_shards(): pl.pallas_call(functools.partial(prep_kernel, seq, pad, tiles), out_shape...  7.14 us

profile of v2, /device:TPU:0, one launch (start us, length us, event | category | flops | bytes accessed | tf_op | source)
XLA Modules:
  0.0 329.4 jit_solution(7457299232971912974)
XLA Ops:
  0.7 0.0 copy-start
  1.4 0.6 pad_add_fusion.who
  1.9 0.0 copy-done
  2.0 0.8 copy.64
  2.7 2.1 pack.1
  4.8 1.6 slice_bitcast_fusion.own3
  6.4 7.1 %prep.1 = (f32[640,768]{1,0:T(8,128)}, bf16[640,768]{1,0:T(8,128)(2,1)}) custom-call(s32[2]{0:T(128)} %pad_add_fusion.who, bf16[147,16,768]{2,1,0:T(8,128)(2,1)} %bitcast.63, bf16[147,16,768]{2,1,0:T(8,128)(2,1)} %bitcast.64, s32[147,4]{1,0:T(8,128)} %bitcast.70, bf16[3,128,768]{2,1,0:T(8,128)(2,1)} %constant.12.clone.tab_ref), custom_call_target="tpu_custom_call" | custom-call | tf_op jit(solution)/shard_map/prep/pallas_call | solution.py:1043
  13.6 43.1 %gather.1 = (bf16[2,2,4,2,96,768]{5,4,3,2,1,0:T(8,128)(2,1)}, bf16[4,96,768]{2,1,0:T(8,128)(2,1)}, bf16[2,2,4,2,16,128]{5,4,3,2,1,0:T(8,128)(2,1)}) custom-call(bf16[3,96,768]{2,1,0:T(8,128)(2,1)} %get-tuple-element.105.w_ref, bf16[16,128]{1,0:T(8,128)(2,1)} %get-tuple-element.106.s_ref), custom_call_target="tpu_custom_call" | custom-call | tf_op jit(solution)/shard_map/gather/pallas_call | solution.py:1018
  56.6 2.2 spread.1
  58.8 55.7 %attend.1 = (f32[640,768]{1,0:T(8,128)}, bf16[4,640,576]{2,1,0:T(8,128)(2,1)}, bf16[4,3,640,160]{3,2,1,0:T(8,128)(2,1)}, bf16[4,640,192]{2,1,0:T(8,128)(2,1)}, b...) custom-call(f32[640,768]{1,0:T(8,128)} %get-tuple-element.103.x_ref, ...), custom_call_target="tpu_custom_call" | custom-call | tf_op jit(solution)/shard_map/attend/pallas_call | solution.py:1060
  114.6 36.2 %feed.1 = (bf16[640,768]{1,0:T(8,128)(2,1)}, f32[640,768]{1,0:T(8,128)}, f32[8,768]{1,0:T(8,128)}, f32[4,8,768]{2,1,0:T(8,128)}, bf16[4,768,768]{2,1,0:T(8,128)(2,1)}, /*index=5*/bf16[4,768,768]{2,1,0:T(8,128)(2,1)}) custom-call(s32[2]{0:T(128)} %pad_add_fusion.who, bf16[640,768]{1,0:T(8,128)(2,1)} %get-tuple-element.104.dy, ...), custom_call_target="tpu_custom_call" | custom-call | tf_op jit(solution)/shard_map/feed/pallas_call | solution.py:1080
  150.8 40.4 %back.1 = (bf16[640,768]{1,0:T(8,128)(2,1)}, f32[8,768]{1,0:T(8,128)}, f32[4,8,768]{2,1,0:T(8,128)}, bf16[4,768,768]{2,1,0:T(8,128)(2,1)}) custom-call(f32[640,768]{1,0:T(8,128)} %get-tuple-element.103.x_ref, f32[640,768]{1,0:T(8,128)} %get-tuple-element.115.dh_ref, f32[16,768]{1,0:T(8,128)} %get-tuple-element.108.vec_ref, bf16[4,768,768]{2,1,0:T(8,128)(2,1)} %bitcast.55, ...), custom_call_target="tpu_custom_call" | custom-call | tf_op jit(solution)/shard_map/back/pallas_call | solution.py:1107
  191.2 3.1 squeeze.5
  194.3 118.3 %reduce.1 = (f32[3,96,768]{2,1,0:T(8,128)}, f32[16,128]{1,0:T(8,128)}, bf16[2,2,640,768]{3,2,1,0:T(8,128)(2,1)}, bf16[2,2,640,768]{3,2,1,0:T(8,128)(2,1)}) custom-call(bf16[2,2,4,2,96,768]{5,4,3,2,1,0:T(8,128)(2,1)} %bitcast.60, bf16[2,2,4,2,96,768]{5,4,3,2,1,0:T(8,128)(2,1)} %bitcast.58, bf16[2,2,4,2,96,768]{5,4,3,2,1,0:T(8,128)(2,1)} %bitcast.59, ...), custom_call_target="tpu_custom_call" | custom-call | tf_op jit(solution)/shard_map/reduce/pallas_call | solution.py:1141
  312.6 0.0 copy-start.1
  312.6 11.9 %lay.1 = (bf16[2352,768]{1,0:T(8,128)(2,1)}, f32[2352,768]{1,0:T(8,128)}) custom-call(bf16[16,160,768]{2,1,0:T(8,128)(2,1)} %bitcast.61, bf16[16,160,768]{2,1,0:T(8,128)(2,1)} %bitcast.62), custom_call_target="tpu_custom_call" | custom-call | tf_op jit(solution)/shard_map/lay/pallas_call | solution.py:1159
  324.5 4.8 %update.1 = (f32[3,96,192]{2,1,0:T(8,128)}, f32[192,96]{1,0:T(8,128)}, f32[96,768]{1,0:T(8,128)}, f32[96,768]{1,0:T(8,128)}, f32[3,2,8]{2,1,0:T(2,128)}, /*index...) custom-call(f32[3,96,768]{2,1,0:T(8,128)} %get-tuple-element.132.ref, ...), custom_call_target="tpu_custom_call" | custom-call | tf_op jit(solution)/shard_map/update/pallas_call | solution.py:1172
  329.3 0.0 copy-done.1
  (1 shorter events, 0.0 us)
Async XLA Ops:
  0.7 1.3 copy-start
  312.6 16.6 %copy-start.1 = (s32[16,147]{1,0:T(8,128)S(1)}, s32[16,147]{1,0:T(8,128)}, u32[]{:S(2)}) copy-start(s32[16,147]{1,0:T(8,128)} %param.28) | copy-start | bytes 28228

commit v3 on v2

--- a/solution.py
+++ b/solution.py
@@ -418,17 +418,18 @@
     s_out[...] = scratch[...].astype(BF16)
 
 
-def spread_kernel(s_ref, vec_out, off_out):
+def spread_small(s_ref, vec_out, off_out):
     row_pick = pick_row()
     vec = jnp.zeros((16, D), F32)
     heads = [jnp.zeros((16, D), F32) for _ in range(4)]
     hidden = [jnp.zeros((1, D), F32) for _ in range(4)]
     for d in range(8):
-        vec += nn(s_ref[0, d], pick_vector(d))
+        vec += nn(s_ref[0, 0, d // 2, d % 2], pick_vector(d))
         head_pick, places = pick_head(d), hidden_places(d)
         for m in range(4):
-            heads[m] += nn(s_ref[m, d], head_pick)
-            spread = nn(s_ref[m, d], row_pick)[8:16]
+            block = s_ref[m // 2, m % 2, d // 2, d % 2]
+            heads[m] += nn(block, head_pick)
+            spread = nn(block, row_pick)[8:16]
             hidden[m] += jnp.sum(jnp.where(places, spread, 0.0), axis=0, keepdims=True)
     vec_out[...] = vec
     for m in range(4):
@@ -437,7 +438,7 @@
         off_out[m, 3:8, :] = jnp.zeros((5, D), F32)
 
 
-def squeeze_kernel(fore_ref, back_ref, hid_ref, heads_ref, out_ref, rows):
+def squeeze_small(fore_ref, back_ref, hid_ref, heads_ref, out_ref, rows):
     rows[...] = jnp.zeros_like(rows)
     rows[0:2, :] = back_ref[0:2, :]
     rows[2:6, :] = fore_ref[0:4, :]
@@ -451,7 +452,7 @@
         for d in range(8):
             upper = jnp.where(iota(shape, 0) < 6, nt(block, pick_vector(d)), nt(block, pick_head(d)))
             lower = nt(jnp.where(hidden_places(d), wide, 0.0).astype(BF16), row_pick)
-            out_ref[m, d] = jnp.concatenate([upper, lower], axis=0).astype(BF16)
+            out_ref[m // 2, m % 2, d // 2, d % 2] = jnp.concatenate([upper, lower], axis=0).astype(BF16)
 
 
 def ln(values):
@@ -506,9 +507,7 @@
     return hot.astype(F32).astype(BF16)
 
 
-def prep_kernel(seq, pad, tiles, who, tok_ref, cot_ref, vis_ref, tab_ref, x_out, dy_out, wide, grad):
-    at = (who[0] & 1) * tiles
-    first = who[0] * tiles
+def lay_tokens(seq, pad, tiles, at, tok_ref, vis_ref, tab_ref, x_out, wide):
     head = seq - seq % 8
     spread_lanes(tok_ref, wide)
     for t in range(tiles):
@@ -518,9 +517,13 @@
         for g in range(D // 128):
             lanes = slice(128 * g, 128 * g + 128)
             x_out[t * pad : t * pad + seq, lanes] = wide[g, pl.ds(at + t, seq, stride=8), :] + table[:, lanes]
+
+
+def lay_cotangent(seq, pad, tiles, at, live_ref, cot_ref, dy_out, wide, grad):
+    head = seq - seq % 8
     spread_lanes(cot_ref, wide)
     for t in range(tiles):
-        live = (first + t < who[1]).astype(F32)
+        live = live_ref[t : t + 1, :]
         grad[t * pad + head : (t + 1) * pad, :] = jnp.zeros((pad - head, D), F32)
         for g in range(D // 128):
             lanes = slice(128 * g, 128 * g + 128)
@@ -535,10 +538,10 @@
     p = Place()
     s = Sends(send, recv)
     g2 = Gather(p, s, f2, 48, column=col2)
-    g3 = Gather(p, s, f3, 48, own=own3)
+    g3 = Gather(p, s, f3, 48, own=own3.at[0])
     mine = [
         pltpu.make_async_copy(col2, f2.at[p.x, p.c, :, p.y], local.at[0]),
-        pltpu.make_async_copy(own3, f3.at[p.x, p.c, p.z, p.y], local.at[1]),
+        pltpu.make_async_copy(own3.at[0], f3.at[p.x, p.c, p.z, p.y], local.at[1]),
     ]
 
     @pl.when(m == 0)
@@ -601,11 +604,10 @@
         s.finish()
 
 
-def feed_kernel(seq, pad, tiles, who, dy, h_ref, vec_ref, off_ref, w2_ref, w3_ref,
+def feed_kernel(seq, pad, tiles, live_ref, dy, h_ref, vec_ref, off_ref, w2_ref, w3_ref,
                 out_out, dh_out, sum_out, hid_out, g2_out, g3_out, c, c_t, dy_t, y, dc):
     m = pl.program_id(0)
     rows_of = lambda t: pl.ds(pl.multiple_of(t * pad, 16), pad)
-    first = who[0] * tiles
 
     @pl.when(m == 0)
     def _():
@@ -641,7 +643,7 @@
         @pl.loop(0, tiles)
         def _(t):
             rows = rows_of(t)
-            live = (first + t < who[1]).astype(F32)
+            live = live_ref[pl.ds(t, 1), 0:1]
             h = h_ref[rows, :]
             out_out[rows, :] = ((h + y[rows, :] + vec_ref[5:6, :]) * live).astype(BF16)
             normed, inverse = ln(h)
@@ -653,13 +655,27 @@
             sum_out[2:3, :] += jnp.sum(dh, axis=0, keepdims=True)
 
 
-def back_kernel(seq, pad, tiles, x_ref, dh_ref, vec_ref, w_ref, qkv_ref, p_ref, o_ref,
-                in_out, sum_out, head_out, g1_out, a_t, dh_low, dh_t, do, dqkv, da):
+def back_kernel(seq, pad, tiles, x_ref, dh_ref, vec_ref, w_ref, qkv_ref, p_ref, o_ref, g2, g3, own_out,
+                in_out, sum_out, head_out, g1_out, part_out, all_out, a_t, dh_low, dh_t, do, dqkv, da, *scratch):
+    *buffers, send, recv, local = scratch
     m = pl.program_id(0)
     rows_of = lambda t: pl.ds(pl.multiple_of(t * pad, 16), pad)
+    p = Place()
+    s = Sends(send, recv)
+    halves = pl.ds(0, 384), pl.ds(384, 384)
+    reduces = [
+        Reduce(p, s, g, [*buffers[4 * i : 4 * i + 4], None], None, cols, local.at[i])
+        for i, (g, cols) in enumerate((g, cols) for g in (g2, g3) for cols in halves)
+    ]
+    trade = Trade(p, s, own_out, all_out, local.at[4])
 
     @pl.when(m == 0)
     def _():
+        p.greet()
+        for r in reduces:
+            r.cores()
+        trade.begin()
+
         @pl.loop(0, tiles)
         def _(t):
             rows = rows_of(t)
@@ -671,6 +687,8 @@
         dh_t[...] = dh_low[...].T
         da[...] = jnp.zeros_like(da)
         sum_out[...] = jnp.zeros_like(sum_out)
+        reduces[0].first()
+        reduces[1].first()
 
     do[...] = nn(dh_low[...], w_ref[0, :, 576:768]).astype(BF16)
     g1_out[0, :, 576:768] = nn(dh_t[...], o_ref[0]).astype(BF16)
@@ -685,9 +703,9 @@
             q, k, v = (qkv[:, 192 * j + 64 * h : 192 * j + 64 * h + 64] for j in range(3))
             g = grad[:, 64 * h : 64 * h + 64]
             low_p = p_ref[0, h, rows, :]
-            p = low_p.astype(F32)
+            prob = low_p.astype(F32)
             dp = nt(g, v)
-            ds = (p * (dp - jnp.sum(dp * p, axis=-1, keepdims=True))).astype(BF16)
+            ds = (prob * (dp - jnp.sum(dp * prob, axis=-1, keepdims=True))).astype(BF16)
             parts[0].append(nn(ds, k) * 0.125)
             parts[1].append(tn(ds, q) * 0.125)
             parts[2].append(tn(low_p, g))
@@ -698,6 +716,20 @@
     head_out[0, 1:2, 0:192] = sums[:, 384:576]
     g1_out[0, :, 0:576] = nn(a_t[...], dqkv[...]).astype(BF16)
     da[...] += nt(dqkv[...], w_ref[0, :, 0:576])
+
+    @pl.when(m == 0)
+    def _():
+        reduces[2].first()
+        reduces[3].first()
+
+    @pl.when(m == 1)
+    def _():
+        reduces[0].second()
+
+    @pl.when(m == 2)
+    def _():
+        trade.relay()
+        reduces[1].second()
 
     @pl.when(m == pl.num_programs(0) - 1)
     def _():
@@ -711,6 +743,13 @@
             sum_out[0:1, :] += jnp.sum(grad * normed, axis=0, keepdims=True)
             sum_out[1:2, :] += jnp.sum(grad, axis=0, keepdims=True)
 
+        reduces[2].second()
+        reduces[3].second()
+        for i, r in enumerate(reduces):
+            r.hand_on(part_out, i // 2, halves[i % 2])
+        trade.done()
+        s.finish()
+
 
 def lay_kernel(seq, pad, count, out_ref, in_ref, out_out, in_out, wide):
     for t in range(count):
@@ -720,8 +759,8 @@
 
 
 def update_kernel(*refs):
-    grad_ref, small_ref = refs[:2]
-    state, outs = refs[2:23], refs[23:]
+    attend_ref, feed_ref, small_ref = refs[:3]
+    state, outs = refs[3:24], refs[24:]
     correction = 1.0 - 0.5**STEP
     rates = ((D // 2) ** -0.5, (D // 16) ** -0.5, D**-0.5, FF**-0.5, 0.1, 0.1, 0.15)
 
@@ -734,10 +773,10 @@
 
     every = (slice(None), slice(None))
     for j in range(3):
-        update(0, (j,) + every, grad_ref[0, :, 192 * j : 192 * j + 192])
-    update(1, every, grad_ref[0, :, 576:768].T)
-    update(2, every, grad_ref[1])
-    update(3, every, grad_ref[2])
+        update(0, (j,) + every, attend_ref[:, 192 * j : 192 * j + 192])
+    update(1, every, attend_ref[:, 576:768].T)
+    update(2, every, feed_ref[0])
+    update(3, every, feed_ref[1])
     for r in range(3):
         update(4, (r,) + every, small_ref[6:8, 8 * r : 8 * r + 8])
     update(5, every, small_ref[8:16, 0:12])
@@ -850,33 +889,46 @@
     COPIES_WHOLE = 8
 
 
-def gather_kernel(w_ref, s_ref, f1, col2, fs, send, recv, local):
+def gather_kernel(seq, pad, tiles, w_ref, s_ref, tok, cot, vis_ref, tab_ref, live_ref,
+                  f1, col2, x_out, dy_out, vec_out, off_out, fs, tok_ref, cot_ref, wide, grad, send, recv, local):
     p = Place()
-    p.greet()
     s = Sends(send, recv)
     half = pl.ds(0, 384), pl.ds(384, 384)
     gathers = [
         Gather(p, s, fs, 16, own=s_ref),
         *(Gather(p, s, f1, 48, cols, own=w_ref.at[0, :, cols]) for cols in half),
     ]
-    for g in gathers:
-        g.along_z()
     ahead = [s.copy(w_ref.at[1], col2.at[p.z], device) for device in p.to_z]
-    start(ahead)
+    group = pl.ds(pl.multiple_of(8 * p.x, 8), 8)
+    rows_in = [
+        pltpu.make_async_copy(tok.at[:, group], tok_ref, local.at[3]),
+        pltpu.make_async_copy(cot.at[:, group], cot_ref, local.at[4]),
+    ]
     mine = [
         pltpu.make_async_copy(s_ref, fs.at[p.x, p.c, p.z, p.y], local.at[0]),
         pltpu.make_async_copy(w_ref.at[0], f1.at[p.x, p.c, p.z, p.y], local.at[1]),
         pltpu.make_async_copy(w_ref.at[1], col2.at[p.z], local.at[2]),
     ]
+    p.greet()
+    for g in gathers:
+        g.along_z()
+    start(ahead)
     start(mine)
+    start(rows_in)
+    rows_in[0].wait()
+    lay_tokens(seq, pad, tiles, p.c * tiles, tok_ref, vis_ref, tab_ref, x_out, wide)
     for copy in mine:
         copy.wait()
-    stages = [("second", 0), ("second", 1), ("third", 0), ("last", 0), ("second", 2), ("third", 1), ("third", 2),
-              ("last", 1), ("last", 2)]
+    gathers[0].second()
+    gathers[1].second()
+    rows_in[1].wait()
+    lay_cotangent(seq, pad, tiles, p.c * tiles, live_ref, cot_ref, dy_out, wide, grad)
+    stages = [("third", 0), ("second", 2), ("third", 1), ("last", 0), ("third", 2), ("done", 0)]
     for name, i in stages:
         getattr(gathers[i], name)()
-    for g in gathers:
-        g.done()
+    spread_small(fs, vec_out, off_out)
+    for name, i in [("last", 1), ("last", 2), ("done", 1), ("done", 2)]:
+        getattr(gathers[i], name)()
     arrived(ahead)
     s.finish()
 
@@ -895,98 +947,114 @@
 
 
 class Reduce:
-    def __init__(self, place, sends, parts, r0, r1a, r1b, r2a, r2b, r3a, r3b, split):
-        self.p, self.s, self.parts, self.split = place, sends, parts, split
-        self.r0, self.r1a, self.r1b, self.r2a, self.r2b, self.r3a, self.r3b = r0, r1a, r1b, r2a, r2b, r3a, r3b
-        self.both = r1b is not None
+    COPIES = 6
+
+    def __init__(self, p, s, parts, buffers, out, cols, load):
+        own, r0, r1, r2, r3 = buffers
+        self.p, self.out, self.own, self.r0, self.r1, self.r2, self.r3 = p, out, own, r0, r1, r2, r3
+        self.load = pltpu.make_async_copy(parts.at[:, p.c, :, :, :, cols], own, load)
+        self.core = [s.copy(parts.at[:, p.oc, :, :, :, cols], r0, p.to_c)]
+        self.over_y = [s.copy(r0.at[:, :, p.oy], r1, p.to_y)]
+        self.over_x = [s.copy(r1.at[p.ox], r2, p.to_x)]
+        if r3 is not None:
+            self.over_z = [s.copy(r2.at[z], r3.at[k], device) for k, (z, device) in enumerate(zip(p.zs, p.to_z))]
 
     def cores(self):
-        p = self.p
-        self.wait = [self.s.start(self.parts.at[:, 1 - p.c], self.r0, p.id(c=1 - p.c))]
+        start(self.core)
+        self.load.start()
 
     def first(self):
-        p, s, h = self.p, self.s, self.split
-        arrived(self.wait)
-        add_into(self.r0, lambda x, z, y: self.parts[x, p.c, z, y], self.r0.shape[:3])
-        self.wait = [s.start(self.r0.at[1 - p.x, :, :, pl.ds(0, h)], self.r1a, p.id(x=1 - p.x))]
-        if self.both:
-            low = pl.ds(h, self.r0.shape[3] - h)
-            self.wait.append(s.start(self.r0.at[:, :, 1 - p.y, low], self.r1b, p.id(y=1 - p.y)))
+        self.load.wait()
+        arrived(self.core)
+        add_into(self.r0, lambda x, z, y: self.own[x, z, y], self.r0.shape[:3])
+        start(self.over_y)
 
     def second(self):
-        p, s, h = self.p, self.s, self.split
-        arrived(self.wait)
-        add_into(self.r1a, lambda z, y: self.r0[p.x, z, y, 0:h], self.r1a.shape[:2])
-        self.wait = [s.start(self.r1a.at[:, 1 - p.y], self.r2a, p.id(y=1 - p.y))]
-        if self.both:
-            add_into(self.r1b, lambda x, z: self.r0[x, z, p.y, h:], self.r1b.shape[:2])
-            self.wait.append(s.start(self.r1b.at[1 - p.x], self.r2b, p.id(x=1 - p.x)))
+        arrived(self.over_y)
+        add_into(self.r1, lambda x, z: self.r0[x, z, self.p.y], self.r1.shape[:2])
+        start(self.over_x)
 
     def third(self):
-        p, s = self.p, self.s
-        arrived(self.wait)
-        add_into(self.r2a, lambda z: self.r1a[z, p.y], self.r2a.shape[:1])
-        if self.both:
-            add_into(self.r2b, lambda z: self.r1b[p.x, z], self.r2b.shape[:1])
-        self.wait = []
-        for k in (1, 2, 3):
-            to = (p.z + k) % 4
-            self.wait.append(s.start(self.r2a.at[to], self.r3a.at[k - 1], p.id(z=to)))
-            if self.both:
-                self.wait.append(s.start(self.r2b.at[to], self.r3b.at[k - 1], p.id(z=to)))
-
-    def last(self, out):
-        p = self.p
-        arrived(self.wait)
-        sum_of = lambda r2, r3: r2[p.z].astype(F32) + r3[0].astype(F32) + r3[1].astype(F32) + r3[2].astype(F32)
-        out[0 : self.split] = sum_of(self.r2a, self.r3a)
-        if self.both:
-            out[self.split :] = sum_of(self.r2b, self.r3b)
+        arrived(self.over_x)
+        add_into(self.r2, lambda z: self.r1[self.p.x, z], self.r2.shape[:1])
+        start(self.over_z)
+
+    def hand_on(self, out, i, cols):
+        arrived(self.over_x)
+        for z in range(4):
+            out[z, i, :, cols] = (self.r2[z].astype(F32) + self.r1[self.p.x, z].astype(F32)).astype(BF16)
+
+    def last(self):
+        arrived(self.over_z)
+        r2, r3 = self.r2, self.r3
+        self.out[...] = r2[self.p.z].astype(F32) + r3[0].astype(F32) + r3[1].astype(F32) + r3[2].astype(F32)
 
     @staticmethod
-    def scratch(rows, columns, split):
-        shapes = [(2, 4, 2, rows), (4, 2, split), (2, 4, rows - split), (4, split), (4, rows - split), (3, split), (3, rows - split)]
-        return [pltpu.VMEM(shape + (columns,), BF16) for shape in shapes if shape[-1] > 0]
-
-
-def reduce_kernel(g1, g2, g3, gs, own_out, own_in, total, small, all_out, all_in, *scratch):
+    def scratch(rows, columns):
+        lead = (2, 4, 2), (2, 4, 2), (2, 4), (4,), (3,)
+        return [pltpu.VMEM(shape + (rows, columns), BF16) for shape in lead]
+
+
+class Trade:
+    COPIES = 3
+
+    def __init__(self, p, s, own, full, local):
+        here, there = full.at[p.x, p.c], full.at[p.ox, p.c]
+        self.mine = pltpu.make_async_copy(own, here, local)
+        self.x, self.c = [s.copy(own, here, p.to_x)], [s.copy(own, here, p.to_c)]
+        self.further = [s.copy(there, there, p.to_c)]
+
+    def begin(self):
+        start(self.x)
+        start(self.c)
+        self.mine.start()
+
+    def relay(self):
+        arrived(self.x)
+        start(self.further)
+
+    def done(self):
+        arrived(self.c + self.further)
+        self.mine.wait()
+
+
+def reduce_kernel(g1, own_in, part, sum_two, sum_one, sum_hid, sum_head, total, feed, small, all_in,
+                  part_z, gs, lines, *scratch):
     *buffers, send, recv, local = scratch
     p = Place()
+    s = Sends(send, recv)
+    thirds = [pl.ds(256 * i, 256) for i in range(3)]
+    reduces = [
+        Reduce(p, s, g1, buffers[5 * i : 5 * i + 5], total.at[:, cols], cols, local.at[i])
+        for i, cols in enumerate(thirds)
+    ]
+    reduces.append(Reduce(p, s, gs, buffers[15:20], small, ALL, local.at[3]))
+    over_z = [s.copy(part.at[z], part_z.at[k], device) for k, (z, device) in enumerate(zip(p.zs, p.to_z))]
+    trade = Trade(p, s, own_in, all_in, local.at[4])
     p.greet()
-    s = Sends(send, recv)
-    reduces = [Reduce(p, s, part, *buffers[7 * i : 7 * i + 7], 48) for i, part in enumerate((g3, g2, g1))]
-    b = buffers[21:]
-    reduces.append(Reduce(p, s, gs, b[0], b[1], None, b[2], None, b[3], None, 16))
-    outs = [total.at[2], total.at[1], total.at[0], small]
+    for r in reduces[:3]:
+        r.cores()
+    trade.begin()
+    start(over_z)
+    squeeze_small(sum_two, sum_one, sum_hid, sum_head, gs, lines)
+    reduces[3].cores()
     for r in reduces:
-        r.cores()
-    trades, copies = [], []
-    for i, (own, full) in enumerate(((own_out, all_out), (own_in, all_in))):
-        slot = full.at[p.x, p.c]
-        copies.append(pltpu.make_async_copy(own, slot, local.at[i]))
-        copies[-1].start()
-    for i in range(4):
-        reduces[i].first()
-        if i > 0:
-            reduces[i - 1].second()
-        if i > 1:
-            reduces[i - 2].third()
-    for own, full in ((own_out, all_out), (own_in, all_in)):
-        slot = full.at[p.x, p.c]
-        trades.append([s.start(own, slot, p.id(x=1 - p.x)), s.start(own, slot, p.id(c=1 - p.c))])
+        r.first()
+    reduces[0].second()
+    reduces[1].second()
+    reduces[0].third()
+    reduces[2].second()
+    reduces[1].third()
     reduces[3].second()
+    trade.relay()
     reduces[2].third()
     reduces[3].third()
-    for r, out in zip(reduces, outs):
-        r.last(out)
-    for trade, full in zip(trades, (all_out, all_in)):
-        arrived(trade[:1])
-        slot = full.at[1 - p.x, p.c]
-        trade.append(s.start(slot, slot, p.id(c=1 - p.c)))
-    for trade in trades:
-        arrived(trade[1:])
-    for copy in copies:
-        copy.wait()
+    arrived(over_z)
+    for i in range(2):
+        feed[i] = part[p.z, i].astype(F32) + sum(part_z[k, i].astype(F32) for k in range(3))
+    for r in reduces:
+        r.last()
+    trade.done()
     s.finish()
 
 
@@ -1002,7 +1070,12 @@
     params = lambda limit=None, **kw: pltpu.CompilerParams(vmem_limit_bytes=60 << 20, **kw)
     shape = jax.ShapeDtypeStruct
     me = lax.axis_index("mp").astype(jnp.int32)
-    who = jnp.stack([me, tile_counts[0]])
+    place = me * tiles + jnp.arange(tiles, dtype=jnp.int32)
+    live = jnp.broadcast_to((place < tile_counts[0]).astype(F32)[:, None], (tiles, 128))
+    by_place = lambda a: a.transpose(1, 0, 2)
+    places = lax.dynamic_slice(visible, (me * tiles, 0), (tiles, seq)).T
+    table = jnp.asarray(position_rows())
+    vmem, anywhere = pl.BlockSpec(memory_space=pltpu.VMEM), pl.BlockSpec(memory_space=ANY)
 
     own, own_small = pl.pallas_call(
         pack_kernel,
@@ -1015,44 +1088,32 @@
     full = shape((2, 2, 4, 2, 96, D), BF16)
     dma = lambda count: pltpu.SemaphoreType.DMA((count,))
     copies = 2 * Gather.COPIES + Gather.COPIES_WHOLE + 3
-    f1, col2, fs = pl.pallas_call(
-        gather_kernel,
-        out_shape=(full, shape((4, 96, D), BF16), shape((2, 2, 4, 2, 16, 128), BF16)),
-        in_specs=[pl.BlockSpec(memory_space=pltpu.VMEM)] * 2,
-        out_specs=(pl.BlockSpec(memory_space=ANY),) * 3,
-        scratch_shapes=[dma(copies), dma(copies), dma(3)],
+    f1, col2, x, dy, vec, off = pl.pallas_call(
+        functools.partial(gather_kernel, seq, pad, tiles),
+        out_shape=(
+            full,
+            shape((4, 96, D), BF16),
+            shape((rows, D), F32),
+            shape((rows, D), BF16),
+            shape((16, D), F32),
+            shape((4, 8, D), F32),
+        ),
+        in_specs=[vmem] * 2 + [anywhere] * 2 + [vmem] * 3,
+        out_specs=[anywhere] * 2 + [vmem] * 4,
+        scratch_shapes=[
+            pltpu.VMEM((2, 2, 4, 2, 16, 128), BF16),
+            pltpu.VMEM((seq, 8, D), BF16),
+            pltpu.VMEM((seq, 8, D), BF16),
+            pltpu.VMEM((D // 128, seq * 8, 128), F32),
+            pltpu.VMEM((rows, D), F32),
+            dma(copies),
+            dma(copies),
+            dma(5),
+        ],
         compiler_params=params(collective_id=0, has_side_effects=True),
         name="gather",
-    )(own, own_small)
+    )(own, own_small, by_place(tokens), by_place(cotangent), places, table, live)
     w1 = f1.reshape(4, D, D)
-
-    vec, off = pl.pallas_call(
-        spread_kernel,
-        out_shape=(shape((16, D), F32), shape((4, 8, D), F32)),
-        compiler_params=params(),
-        name="spread",
-    )(fs.reshape(4, 8, 16, 128))
-
-    by_place = lambda a: a.transpose(1, 0, 2)
-    half = pl.BlockSpec((seq, 8, D), lambda m, who: (0, who[0] // 2, 0))
-    of_group = lambda *shape: pl.BlockSpec((1,) + shape, lambda m, who: (m,) + (0,) * len(shape))
-    all_of = lambda *shape: pl.BlockSpec(shape, lambda m, who: (0,) * len(shape))
-    places = lax.dynamic_slice(visible, (me * tiles, 0), (tiles, seq)).T
-    table = jnp.asarray(position_rows())
-
-    x, dy = pl.pallas_call(
-        functools.partial(prep_kernel, seq, pad, tiles),
-        out_shape=(shape((rows, D), F32), shape((rows, D), BF16)),
-        grid_spec=pltpu.PrefetchScalarGridSpec(
-            num_scalar_prefetch=1,
-            grid=(1,),
-            in_specs=[half, half, all_of(seq, tiles), all_of(3, 128, D)],
-            out_specs=(all_of(rows, D),) * 2,
-            scratch_shapes=[pltpu.VMEM((D // 128, seq * 8, 128), F32), pltpu.VMEM((rows, D), F32)],
-        ),
-        compiler_params=params(),
-        name="prep",
-    )(who, by_place(tokens), by_place(cotangent), places, table)
 
     of_group1 = lambda *shape: pl.BlockSpec((1,) + shape, lambda m: (m,) + (0,) * len(shape))
     all_of1 = lambda *shape: pl.BlockSpec(shape, lambda m: (0,) * len(shape))
@@ -1068,13 +1129,13 @@
             full,
         ),
         grid=(4,),
-        in_specs=[all_of1(rows, D), all_of1(16, D), of_group1(8, D), of_group1(D, D), all_of1(4, 96, D), all_of1(96, D)],
+        in_specs=[all_of1(rows, D), all_of1(16, D), of_group1(8, D), of_group1(D, D), all_of1(4, 96, D), pl.BlockSpec((1, 96, D), lambda m: (2, 0, 0))],
         out_specs=(all_of1(rows, D), of_group1(rows, 576), of_group1(3, rows, pad), of_group1(rows, 192))
         + (pl.BlockSpec(memory_space=ANY),) * 2,
         scratch_shapes=[pltpu.VMEM((rows, D), BF16), dma(copies), dma(copies), dma(2)],
         compiler_params=params(collective_id=2, has_side_effects=True),
         name="attend",
-    )(x, vec, off, w1, col2, own[2])
+    )(x, vec, off, w1, col2, own)
     w2, w3 = (f.reshape(4, D, D) for f in (f2, f3))
 
     out_own, dh, sum_two, sum_hid, g2, g3 = pl.pallas_call(
@@ -1087,35 +1148,39 @@
             shape((4, D, D), BF16),
             shape((4, D, D), BF16),
         ),
-        grid_spec=pltpu.PrefetchScalarGridSpec(
-            num_scalar_prefetch=1,
-            grid=(4,),
-            in_specs=[all_of(rows, D), all_of(rows, D), all_of(16, D), of_group(8, D), of_group(D, D), of_group(D, D)],
-            out_specs=(all_of(rows, D), all_of(rows, D), all_of(8, D), of_group(8, D), of_group(D, D), of_group(D, D)),
-            scratch_shapes=[
-                pltpu.VMEM((rows, D), BF16),
-                pltpu.VMEM((D, rows), BF16),
-                pltpu.VMEM((D, rows), BF16),
-                pltpu.VMEM((rows, D), F32),
-                pltpu.VMEM((rows, D), F32),
-            ],
-        ),
+        grid=(4,),
+        in_specs=[all_of1(tiles, 128), all_of1(rows, D), all_of1(rows, D), all_of1(16, D), of_group1(8, D),
+                  of_group1(D, D), of_group1(D, D)],
+        out_specs=(all_of1(rows, D), all_of1(rows, D), all_of1(8, D), of_group1(8, D), of_group1(D, D), of_group1(D, D)),
+        scratch_shapes=[
+            pltpu.VMEM((rows, D), BF16),
+            pltpu.VMEM((D, rows), BF16),
+            pltpu.VMEM((D, rows), BF16),
+            pltpu.VMEM((rows, D), F32),
+            pltpu.VMEM((rows, D), F32),
+        ],
         compiler_params=params(),
         name="feed",
-    )(who, dy, h, vec, off, w2, w3)
-
-    in_own, sum_one, sum_head, g1 = pl.pallas_call(
+    )(live, dy, h, vec, off, w2, w3)
+
+    by_device = lambda g: g.reshape(2, 2, 4, 2, 96, D)
+    everyone = shape((2, 2, rows, D), BF16)
+    copies = 4 * (Reduce.COPIES - 3) + Trade.COPIES
+    in_own, sum_one, sum_head, g1, part, all_out = pl.pallas_call(
         functools.partial(back_kernel, seq, pad, tiles),
         out_shape=(
             shape((rows, D), BF16),
             shape((8, D), F32),
             shape((4, 8, D), F32),
             shape((4, D, D), BF16),
+            shape((4, 2, 96, D), BF16),
+            everyone,
         ),
         grid=(4,),
         in_specs=[all_of1(rows, D), all_of1(rows, D), all_of1(16, D), of_group1(D, D), of_group1(rows, 576),
-                  of_group1(3, rows, pad), of_group1(rows, 192)],
-        out_specs=(all_of1(rows, D), all_of1(8, D), of_group1(8, D), of_group1(D, D)),
+                  of_group1(3, rows, pad), of_group1(rows, 192)] + [pl.BlockSpec(memory_space=ANY)] * 3,
+        out_specs=(all_of1(rows, D), all_of1(8, D), of_group1(8, D), of_group1(D, D), all_of1(4, 2, 96, D),
+                   pl.BlockSpec(memory_space=ANY)),
         scratch_shapes=[
             pltpu.VMEM((D, rows), BF16),
             pltpu.VMEM((rows, D), BF16),
@@ -1123,36 +1188,34 @@
             pltpu.VMEM((rows, 192), BF16),
             pltpu.VMEM((rows, 576), BF16),
             pltpu.VMEM((rows, D), F32),
+            *(4 * Reduce.scratch(96, 384)[:4]),
+            dma(copies),
+            dma(copies),
+            dma(5),
         ],
-        compiler_params=params(),
+        compiler_params=params(collective_id=3, has_side_effects=True),
         name="back",
-    )(x, dh, vec, w1, qkv, probs, o)
-
-    gs = pl.pallas_call(
-        squeeze_kernel,
-        out_shape=shape((4, 8, 16, 128), BF16),
-        scratch_shapes=[pltpu.VMEM((8, D), F32)],
-        compiler_params=params(),
-        name="squeeze",
-    )(sum_two, sum_one, sum_hid, sum_head)
-
-    copies = 3 * 11 + 6 + 6
-    everyone = shape((2, 2, rows, D), BF16)
-    total, small, all_out, all_in = pl.pallas_call(
+    )(x, dh, vec, w1, qkv, probs, o, by_device(g2), by_device(g3), out_own)
+
+    copies = 4 * Reduce.COPIES + 3 + Trade.COPIES
+    total_attend, total_feed, small, all_in = pl.pallas_call(
         reduce_kernel,
-        out_shape=(shape((3, 96, D), F32), shape((16, 128), F32), everyone, everyone),
-        in_specs=[pl.BlockSpec(memory_space=pltpu.VMEM)] * 4 + [pl.BlockSpec(memory_space=ANY)] * 2,
-        out_specs=(pl.BlockSpec(memory_space=pltpu.VMEM),) * 2 + (pl.BlockSpec(memory_space=ANY),) * 2,
+        out_shape=(shape((96, D), F32), shape((2, 96, D), F32), shape((16, 128), F32), everyone),
+        in_specs=[anywhere] * 2 + [vmem] * 5,
+        out_specs=[vmem] * 3 + [anywhere],
         scratch_shapes=[
-            *(3 * Reduce.scratch(96, D, 48)),
-            *Reduce.scratch(16, 128, 16),
-            pltpu.SemaphoreType.DMA((copies,)),
-            pltpu.SemaphoreType.DMA((copies,)),
-            pltpu.SemaphoreType.DMA((2,)),
+            pltpu.VMEM((3, 2, 96, D), BF16),
+            pltpu.VMEM((2, 2, 4, 2, 16, 128), BF16),
+            pltpu.VMEM((8, D), F32),
+            *(3 * Reduce.scratch(96, 256)),
+            *Reduce.scratch(16, 128),
+            dma(copies),
+            dma(copies),
+            dma(5),
         ],
         compiler_params=params(collective_id=1, has_side_effects=True),
         name="reduce",
-    )(*(g.reshape(2, 2, 4, 2, 96, D) for g in (g1, g2, g3)), gs.reshape(2, 2, 4, 2, 16, 128), out_own, in_own)
+    )(by_device(g1), in_own, part, sum_two, sum_one, sum_hid, sum_head)
 
     flat = seq * tile_count
     block = pl.BlockSpec((tile_count, pad, 128), lambda n: (0, 0, n))
@@ -1174,7 +1237,7 @@
         out_shape=tuple(kinds * 4 + [shape(a.shape, BF16) for a in kinds]),
         compiler_params=params(),
         name="update",
-    )(total, small, *state)
+    )(total_attend, total_feed, small, *state)
     return (output, input_grad) + tuple(native(i % 7, a) for i, a in enumerate(results))
 
 

time: 330 us -> 279 us (0.85)
  Pallas kernels: 325 us -> 276 us
    pallas_call x5 -> x2, Pallas kernels: 174 us -> 92.9 us  [the longest x1 47.9 us: fast_shards(): pl.pallas_call(reduce_kernel, out_shape=(shape((96, D), F32), shape((2, 9...]
    pallas_call x1, Pallas kernels: 40.4 us -> 72.5 us  [fast_shards(): pl.pallas_call(functools.partial(back_kernel, seq, pad, tiles), out_shape...]
where the time goes in v3:
time: 279 us
  Pallas kernels  276 us (99%)
    pallas_call x1, Pallas kernels, fast_shards(): pl.pallas_call(functools.partial(back_kernel, seq, pad, tiles), out_shape...  72.5 us
    pallas_call x1, Pallas kernels, fast_shards(): pl.pallas_call(functools.partial(attend_kernel, seq, pad, tiles), out_sha...  55.6 us
    pallas_call x1, Pallas kernels, fast_shards(): pl.pallas_call(reduce_kernel, out_shape=(shape((96, D), F32), shape((2, 9...  47.9 us
    pallas_call x1, Pallas kernels, fast_shards(): pl.pallas_call(functools.partial(gather_kernel, seq, pad, tiles), out_sha...  44.9 us
    pallas_call x1, Pallas kernels, fast_shards(): pl.pallas_call(functools.partial(feed_kernel, seq, pad, tiles), out_shape...  35.9 us
    pallas_call x1, Pallas kernels, fast_shards(): pl.pallas_call(functools.partial(lay_kernel, seq, pad, tile_count), out_s...  11.9 us

profile of v3, /device:TPU:0, one launch (start us, length us, event | category | flops | bytes accessed | tf_op | source)
XLA Modules:
  0.0 278.5 jit_solution(5056122211739220722)
XLA Ops:
  0.7 0.0 copy-start
  1.4 0.6 broadcast_in_dim.2.live_ref
  2.0 0.0 copy-done
  2.0 0.8 copy.64
  2.8 2.1 pack.1
  4.9 44.9 %gather.1 = (bf16[2,2,4,2,96,768]{5,4,3,2,1,0:T(8,128)(2,1)}, bf16[4,96,768]{2,1,0:T(8,128)(2,1)}, f32[640,768]{1,0:T(8,128)}, bf16[640,768]{1,0:T(8,128)(2,1)},...) custom-call(bf16[3,96,768]{2,1,0:T(8,128)(2,1)} %get-tuple-element.104.w_ref.own3, bf16[16,128]{1,0:T(8,128)(2,1)} %get-tuple-element.105.s_ref, ...), custom_call_target="tpu_custom_call" | custom-call | tf_op jit(solution)/shard_map/gather/pallas_call | solution.py:1091
  49.9 55.6 %attend.1 = (f32[640,768]{1,0:T(8,128)}, bf16[4,640,576]{2,1,0:T(8,128)(2,1)}, bf16[4,3,640,160]{3,2,1,0:T(8,128)(2,1)}, bf16[4,640,192]{2,1,0:T(8,128)(2,1)}, b...) custom-call(f32[640,768]{1,0:T(8,128)} %get-tuple-element.106.x_ref, ...), custom_call_target="tpu_custom_call" | custom-call | tf_op jit(solution)/shard_map/attend/pallas_call | solution.py:1121
  105.5 35.9 %feed.1 = (bf16[640,768]{1,0:T(8,128)(2,1)}, f32[640,768]{1,0:T(8,128)}, f32[8,768]{1,0:T(8,128)}, f32[4,8,768]{2,1,0:T(8,128)}, bf16[4,768,768]{2,1,0:T(8,128)(2,1)}, /*index=5*/bf16[4,768,768]{2,1,0:T(8,128)(2,1)}) custom-call(f32[4,128]{1,0:T(4,128)} %broadcast_in_dim.2.live_ref, bf16[640,768]{1,0:T(8,128)(2,1)} %get-tuple-element.107.dy, ...), custom_call_target="tpu_custom_call" | custom-call | tf_op jit(solution)/shard_map/feed/pallas_call | solution.py:1141
  141.4 72.5 %back.1 = (bf16[640,768]{1,0:T(8,128)(2,1)}, f32[8,768]{1,0:T(8,128)}, f32[4,8,768]{2,1,0:T(8,128)}, bf16[4,768,768]{2,1,0:T(8,128)(2,1)}, bf16[4,2,96,768]{3,2,...) custom-call(f32[640,768]{1,0:T(8,128)} %get-tuple-element.106.x_ref, f32[640,768]{1,0:T(8,128)} %get-tuple-element.115.dh_ref, ...), custom_call_target="tpu_custom_call" | custom-call | tf_op jit(solution)/shard_map/back/pallas_call | solution.py:1169
  213.8 47.9 %reduce.1 = (f32[96,768]{1,0:T(8,128)}, f32[2,96,768]{2,1,0:T(8,128)}, f32[16,128]{1,0:T(8,128)}, bf16[2,2,640,768]{3,2,1,0:T(8,128)(2,1)}) custom-call(bf16[2,2,4,2,96,768]{5,4,3,2,1,0:T(8,128)(2,1)} %bitcast.53, bf16[640,768]{1,0:T(8,128)(2,1)} %get-tuple-element.124.own_in, bf16[4,2,96,768]{3,2,1,0:T(8,128)(2,1)} %get-tuple-element.125.part, ...), custom_call_target="tpu_custom_call" | custom-call | tf_op jit(solution)/shard_map/reduce/pallas_call | solution.py:1201
  261.8 0.0 copy-start.1
  261.8 11.9 %lay.1 = (bf16[2352,768]{1,0:T(8,128)(2,1)}, f32[2352,768]{1,0:T(8,128)}) custom-call(bf16[16,160,768]{2,1,0:T(8,128)(2,1)} %bitcast.58, bf16[16,160,768]{2,1,0:T(8,128)(2,1)} %bitcast.59), custom_call_target="tpu_custom_call" | custom-call | tf_op jit(solution)/shard_map/lay/pallas_call | solution.py:1222
  273.6 4.7 %update.1 = (f32[3,96,192]{2,1,0:T(8,128)}, f32[192,96]{1,0:T(8,128)}, f32[96,768]{1,0:T(8,128)}, f32[96,768]{1,0:T(8,128)}, f32[3,2,8]{2,1,0:T(2,128)}, /*index...) custom-call(f32[96,768]{1,0:T(8,128)} %get-tuple-element.133.refs_0_, ...), custom_call_target="tpu_custom_call" | custom-call | tf_op jit(solution)/shard_map/update/pallas_call | solution.py:1235
  278.4 0.0 copy-done.1
  (2 shorter events, 0.0 us)
Async XLA Ops:
  0.7 1.3 copy-start
  261.8 16.6 %copy-start.1 = (s32[16,147]{1,0:T(8,128)S(1)}, s32[16,147]{1,0:T(8,128)}, u32[]{:S(2)}) copy-start(s32[16,147]{1,0:T(8,128)} %param.28) | copy-start | bytes 28228

commit v4 on v3

--- a/solution.py
+++ b/solution.py
@@ -531,231 +531,243 @@
     dy_out[...] = grad[...].astype(BF16)
 
 
-def attend_kernel(seq, pad, tiles, x_ref, vec_ref, off_ref, w_ref, col2, own3,
-                  h_out, qkv_out, p_out, o_out, f2, f3, low, send, recv, local):
-    m = pl.program_id(0)
+def fore_kernel(seq, pad, tiles, x_ref, a_ref, dy_t, vec_ref, off_ref, w_ref, part2, own3,
+                h_out, qkv_out, p_out, o_out, r_out, slope_out, g3_out, c_t, w2_out, f3,
+                low, f2, send, recv, local):
+    step = pl.program_id(0)
+    m = step % 4
     rows_of = lambda t: pl.ds(pl.multiple_of(t * pad, 16), pad)
     p = Place()
     s = Sends(send, recv)
-    g2 = Gather(p, s, f2, 48, column=col2)
-    g3 = Gather(p, s, f3, 48, own=own3.at[0])
+    g2 = Gather(p, s, f2, 48, part=part2)
+    halves = pl.ds(0, 384), pl.ds(384, 384)
+    g3 = [Gather(p, s, f3, 48, cols, own=own3.at[0, :, cols]) for cols in halves]
     mine = [
-        pltpu.make_async_copy(col2, f2.at[p.x, p.c, :, p.y], local.at[0]),
-        pltpu.make_async_copy(own3.at[0], f3.at[p.x, p.c, p.z, p.y], local.at[1]),
+        *Gather.present(p, part2, f2, 48, local),
+        pltpu.make_async_copy(own3.at[0], f3.at[p.x, p.c, p.z, p.y], local.at[4]),
     ]
-
-    @pl.when(m == 0)
+    hand_on = pltpu.make_async_copy(f2, w2_out, local.at[5])
+
+    @pl.when(step == 0)
     def _():
         p.greet()
-        g2.second()
-        g3.along_z()
+        g2.third()
+        for g in g3:
+            g.along_z()
+        start(mine)
+        h_out[...] = x_ref[...] + vec_ref[4:5, :]
+
+    @pl.when(step < 4)
+    def _():
+        linear = nn(a_ref[...], w_ref[0, :, 0:576])
+        zero = jnp.zeros((1, 192), F32)
+        offset = jnp.concatenate([off_ref[0, 0:1, 0:192], zero, off_ref[0, 1:2, 0:192]], axis=1)
+        qkv_out[0] = (linear + offset).astype(BF16)
+
+        @pl.loop(0, tiles, unroll=2)
+        def _(t):
+            rows = rows_of(t)
+            qkv = qkv_out[0, rows, :]
+            parts = []
+            for h in range(3):
+                q, k, v = (qkv[:, 192 * j + 64 * h : 192 * j + 64 * h + 64] for j in range(3))
+                s = nt(q, k) * 0.125
+                s = jnp.where(iota(s.shape, 1) < seq, s, -1e30)
+                e = jnp.exp(s - jnp.max(s, axis=-1, keepdims=True))
+                low_p = (e * (1.0 / jnp.sum(e, axis=-1, keepdims=True))).astype(BF16)
+                p_out[0, h, rows, :] = low_p
+                parts.append(nn(low_p, v))
+            o_out[0, rows, :] = jnp.concatenate(parts, axis=1).astype(BF16)
+
+        h_out[...] += nt(o_out[0], w_ref[0, :, 576:768])
+
+    @pl.when(step == 0)
+    def _():
         for copy in mine:
-            copy.start()
+            copy.wait()
+
+    @pl.when(step == 1)
+    def _():
+        g3[0].second()
+
+    @pl.when(step == 2)
+    def _():
+        g3[1].second()
+
+    @pl.when(step == 3)
+    def _():
+        g2.last()
 
         @pl.loop(0, tiles)
         def _(t):
-            x = x_ref[rows_of(t), :]
-            normed, _ = ln(x)
-            low[rows_of(t), :] = (normed * vec_ref[0:1, :] + vec_ref[1:2, :]).astype(BF16)
-            h_out[rows_of(t), :] = x + vec_ref[4:5, :]
-
-    linear = nn(low[...], w_ref[0, :, 0:576])
-    zero = jnp.zeros((1, 192), F32)
-    offset = jnp.concatenate([off_ref[0, 0:1, 0:192], zero, off_ref[0, 1:2, 0:192]], axis=1)
-    qkv_out[0] = (linear + offset).astype(BF16)
-
-    @pl.loop(0, tiles)
-    def _(t):
-        rows = rows_of(t)
-        qkv = qkv_out[0, rows, :]
-        parts = []
-        for h in range(3):
-            q, k, v = (qkv[:, 192 * j + 64 * h : 192 * j + 64 * h + 64] for j in range(3))
-            s = nt(q, k) * 0.125
-            s = jnp.where(iota(s.shape, 1) < seq, s, -1e30)
-            e = jnp.exp(s - jnp.max(s, axis=-1, keepdims=True))
-            low_p = (e * (1.0 / jnp.sum(e, axis=-1, keepdims=True))).astype(BF16)
-            p_out[0, h, rows, :] = low_p
-            parts.append(nn(low_p, v))
-        o_out[0, rows, :] = jnp.concatenate(parts, axis=1).astype(BF16)
-
-    h_out[...] += nt(o_out[0], w_ref[0, :, 576:768])
-
-    @pl.when(m == 0)
-    def _():
-        for copy in mine:
-            copy.wait()
-        g2.third()
-
-    @pl.when(m == 1)
-    def _():
-        g3.second()
-
-    @pl.when(m == 2)
-    def _():
-        g2.last()
-
-    @pl.when(m == 3)
-    def _():
-        g3.third()
-        g3.last()
+            normed, _ = ln(h_out[rows_of(t), :])
+            low[rows_of(t), :] = (normed * vec_ref[2:3, :] + vec_ref[3:4, :]).astype(BF16)
+
         g2.done()
-        g3.done()
+        hand_on.start()
+
+    @pl.when(step >= 4)
+    def _():
+        @pl.loop(0, 3)
+        def _(n):
+            cols = pl.ds(pl.multiple_of(n * 256, 256), 256)
+            w2 = f2[m // 2, m % 2, :, :, :, cols].reshape(D, 256)
+            u = nn(low[...], w2) + off_ref[0, 2:3, cols]
+            cdf = 0.5 * (1.0 + lax.erf(u * math.sqrt(0.5)))
+            r = (u * cdf).astype(BF16)
+            r_out[0, :, cols] = r
+            slope_out[0, :, cols] = cdf + u * (jnp.exp(-0.5 * u * u) * (1.0 / math.sqrt(2.0 * math.pi)))
+            g3_out[0, :, cols] = nn(dy_t[...], r).astype(BF16)
+
+    @pl.when(step == 4)
+    def _():
+        g3[0].third()
+        g3[1].third()
+
+    @pl.when(step == 7)
+    def _():
+        g3[0].last()
+        c_t[...] = low[...].T
+        g3[1].last()
+        for g in g3:
+            g.done()
+        hand_on.wait()
         s.finish()
 
 
-def feed_kernel(seq, pad, tiles, live_ref, dy, h_ref, vec_ref, off_ref, w2_ref, w3_ref,
-                out_out, dh_out, sum_out, hid_out, g2_out, g3_out, c, c_t, dy_t, y, dc):
-    m = pl.program_id(0)
-    rows_of = lambda t: pl.ds(pl.multiple_of(t * pad, 16), pad)
-
-    @pl.when(m == 0)
-    def _():
-        sum_out[...] = jnp.zeros_like(sum_out)
-
-        @pl.loop(0, tiles)
-        def _(t):
-            sum_out[3:4, :] += jnp.sum(dy[rows_of(t), :].astype(F32), axis=0, keepdims=True)
-            normed, _ = ln(h_ref[rows_of(t), :])
-            c[rows_of(t), :] = (normed * vec_ref[2:3, :] + vec_ref[3:4, :]).astype(BF16)
-
-        dy_t[...] = dy[...].T
-        c_t[...] = c[...].T
-        y[...] = jnp.zeros_like(y)
-        dc[...] = jnp.zeros_like(dc)
-
-    @pl.loop(0, 3)
-    def _(n):
-        cols = pl.ds(pl.multiple_of(n * 256, 256), 256)
-        u = nn(c[...], w2_ref[0, :, cols]) + off_ref[0, 2:3, cols]
-        cdf = 0.5 * (1.0 + lax.erf(u * math.sqrt(0.5)))
-        r = (u * cdf).astype(BF16)
-        slope = cdf + u * (jnp.exp(-0.5 * u * u) * (1.0 / math.sqrt(2.0 * math.pi)))
-        g3_out[0, :, cols] = nn(dy_t[...], r).astype(BF16)
-        du = (nn(dy[...], w3_ref[0, :, cols]) * slope).astype(BF16)
-        hid_out[0, 0:1, cols] = jnp.sum(du.astype(F32), axis=0, keepdims=True)
-        g2_out[0, :, cols] = nn(c_t[...], du).astype(BF16)
-        y[...] += nt(r, w3_ref[0, :, cols])
-        dc[...] += nt(du, w2_ref[0, :, cols])
-
-    @pl.when(m == pl.num_programs(0) - 1)
-    def _():
-        @pl.loop(0, tiles)
-        def _(t):
-            rows = rows_of(t)
-            live = live_ref[pl.ds(t, 1), 0:1]
-            h = h_ref[rows, :]
-            out_out[rows, :] = ((h + y[rows, :] + vec_ref[5:6, :]) * live).astype(BF16)
-            normed, inverse = ln(h)
-            grad = dc[rows, :]
-            dh = dy[rows, :].astype(F32) + ln_back(grad * vec_ref[2:3, :], normed, inverse)
-            dh_out[rows, :] = dh
-            sum_out[0:1, :] += jnp.sum(grad * normed, axis=0, keepdims=True)
-            sum_out[1:2, :] += jnp.sum(grad, axis=0, keepdims=True)
-            sum_out[2:3, :] += jnp.sum(dh, axis=0, keepdims=True)
-
-
-def back_kernel(seq, pad, tiles, x_ref, dh_ref, vec_ref, w_ref, qkv_ref, p_ref, o_ref, g2, g3, own_out,
-                in_out, sum_out, head_out, g1_out, part_out, all_out, a_t, dh_low, dh_t, do, dqkv, da, *scratch):
+def back_kernel(seq, pad, tiles, live_ref, dy, h_ref, c_t, a_t, vec_ref, w2_ref, w3_ref, r_ref, slope_ref,
+                w_ref, qkv_ref, p_ref, o_ref, g3,
+                da, dh, sum_two, hid_out, head_out, g1_out, part_out, low_out, all_out,
+                low, dh_t, y, dc, do, dqkv, g2, own_out, *scratch):
     *buffers, send, recv, local = scratch
-    m = pl.program_id(0)
+    step = pl.program_id(0)
+    m = step % 4
     rows_of = lambda t: pl.ds(pl.multiple_of(t * pad, 16), pad)
     p = Place()
     s = Sends(send, recv)
     halves = pl.ds(0, 384), pl.ds(384, 384)
-    reduces = [
-        Reduce(p, s, g, [*buffers[4 * i : 4 * i + 4], None], None, cols, local.at[i])
-        for i, (g, cols) in enumerate((g, cols) for g in (g2, g3) for cols in halves)
-    ]
-    trade = Trade(p, s, own_out, all_out, local.at[4])
-
-    @pl.when(m == 0)
+    early = [FeedReduce(p, s, g3, buffers[7 * i : 7 * i + 7], cols, local.at[i]) for i, cols in enumerate(halves)]
+    late = [FeedReduce(p, s, g2, buffers[14 + 6 * i : 20 + 6 * i], cols) for i, cols in enumerate(halves)]
+    trade = Trade(p, s, own_out, all_out, local.at[2], 1)
+
+    @pl.when(step == 0)
     def _():
         p.greet()
-        for r in reduces:
+        for r in early:
             r.cores()
-        trade.begin()
+        sum_two[...] = jnp.zeros_like(sum_two)
+
+        @pl.loop(0, tiles)
+        def _(t):
+            sum_two[3:4, :] += jnp.sum(dy[rows_of(t), :].astype(F32), axis=0, keepdims=True)
+
+        y[...] = jnp.zeros_like(y)
+        dc[...] = jnp.zeros_like(dc)
+
+    @pl.when(step < 4)
+    def _():
+        @pl.loop(0, 3)
+        def _(n):
+            cols = pl.ds(pl.multiple_of(n * 256, 256), 256)
+            du = (nn(dy[...], w3_ref[0, :, cols]) * slope_ref[0, :, cols]).astype(BF16)
+            hid_out[0, 0:1, cols] = jnp.sum(du.astype(F32), axis=0, keepdims=True)
+            g2[m // 2, m % 2, :, :, :, cols] = nn(c_t[...], du).astype(BF16).reshape(4, 2, 96, 256)
+            y[...] += nt(r_ref[0, :, cols], w3_ref[0, :, cols])
+            dc[...] += nt(du, w2_ref[0, :, cols])
+
+    @pl.when(step == 0)
+    def _():
+        for r in early:
+            r.first()
+
+    @pl.when(step == 2)
+    def _():
+        early[0].second()
+        early[0].low_second()
+
+    @pl.when(step == 3)
+    def _():
+        for r in late:
+            r.cores()
 
         @pl.loop(0, tiles)
         def _(t):
             rows = rows_of(t)
-            normed, _ = ln(x_ref[rows, :])
-            dh_low[rows, :] = (normed * vec_ref[0:1, :] + vec_ref[1:2, :]).astype(BF16)
-
-        a_t[...] = dh_low[...].T
-        dh_low[...] = dh_ref[...].astype(BF16)
-        dh_t[...] = dh_low[...].T
+            h = h_ref[rows, :]
+            own_out[rows, :] = ((h + y[rows, :] + vec_ref[5:6, :]) * live_ref[pl.ds(t, 1), 0:1]).astype(BF16)
+            normed, inverse = ln(h)
+            grad = dc[rows, :]
+            back = dy[rows, :].astype(F32) + ln_back(grad * vec_ref[2:3, :], normed, inverse)
+            dh[rows, :] = back
+            sum_two[0:1, :] += jnp.sum(grad * normed, axis=0, keepdims=True)
+            sum_two[1:2, :] += jnp.sum(grad, axis=0, keepdims=True)
+            sum_two[2:3, :] += jnp.sum(back, axis=0, keepdims=True)
+            low[rows, :] = back.astype(BF16)
+
+        trade.begin()
+        early[1].second()
+        early[1].low_second()
+        for r in late:
+            r.first()
+        dh_t[...] = low[...].T
         da[...] = jnp.zeros_like(da)
-        sum_out[...] = jnp.zeros_like(sum_out)
-        reduces[0].first()
-        reduces[1].first()
-
-    do[...] = nn(dh_low[...], w_ref[0, :, 576:768]).astype(BF16)
-    g1_out[0, :, 576:768] = nn(dh_t[...], o_ref[0]).astype(BF16)
-
-    @pl.loop(0, tiles)
-    def _(t):
-        rows = rows_of(t)
-        qkv = qkv_ref[0, rows, :]
-        grad = do[rows, :]
-        parts = [[], [], []]
-        for h in range(3):
-            q, k, v = (qkv[:, 192 * j + 64 * h : 192 * j + 64 * h + 64] for j in range(3))
-            g = grad[:, 64 * h : 64 * h + 64]
-            low_p = p_ref[0, h, rows, :]
-            prob = low_p.astype(F32)
-            dp = nt(g, v)
-            ds = (prob * (dp - jnp.sum(dp * prob, axis=-1, keepdims=True))).astype(BF16)
-            parts[0].append(nn(ds, k) * 0.125)
-            parts[1].append(tn(ds, q) * 0.125)
-            parts[2].append(tn(low_p, g))
-        dqkv[rows, :] = jnp.concatenate(parts[0] + parts[1] + parts[2], axis=1).astype(BF16)
-
-    sums = jnp.sum(dqkv[...].astype(F32), axis=0, keepdims=True)
-    head_out[0, 0:1, 0:192] = sums[:, 0:192]
-    head_out[0, 1:2, 0:192] = sums[:, 384:576]
-    g1_out[0, :, 0:576] = nn(a_t[...], dqkv[...]).astype(BF16)
-    da[...] += nt(dqkv[...], w_ref[0, :, 0:576])
-
-    @pl.when(m == 0)
-    def _():
-        reduces[2].first()
-        reduces[3].first()
-
-    @pl.when(m == 1)
-    def _():
-        reduces[0].second()
-
-    @pl.when(m == 2)
-    def _():
-        trade.relay()
-        reduces[1].second()
-
-    @pl.when(m == pl.num_programs(0) - 1)
-    def _():
-        @pl.loop(0, tiles)
+
+    @pl.when(step >= 4)
+    def _():
+        do[...] = nn(low[...], w_ref[0, :, 576:768]).astype(BF16)
+        g1_out[0, :, 576:768] = nn(dh_t[...], o_ref[0]).astype(BF16)
+
+        @pl.loop(0, tiles, unroll=2)
         def _(t):
             rows = rows_of(t)
-            normed, inverse = ln(x_ref[rows, :])
-            grad = da[rows, :]
-            back = ln_back(grad * vec_ref[0:1, :], normed, inverse)
-            in_out[rows, :] = (dh_ref[rows, :] + back).astype(BF16)
-            sum_out[0:1, :] += jnp.sum(grad * normed, axis=0, keepdims=True)
-            sum_out[1:2, :] += jnp.sum(grad, axis=0, keepdims=True)
-
-        reduces[2].second()
-        reduces[3].second()
-        for i, r in enumerate(reduces):
-            r.hand_on(part_out, i // 2, halves[i % 2])
+            qkv = qkv_ref[0, rows, :]
+            grad = do[rows, :]
+            parts = [[], [], []]
+            for h in range(3):
+                q, k, v = (qkv[:, 192 * j + 64 * h : 192 * j + 64 * h + 64] for j in range(3))
+                g = grad[:, 64 * h : 64 * h + 64]
+                low_p = p_ref[0, h, rows, :]
+                prob = low_p.astype(F32)
+                dp = nt(g, v)
+                ds = (prob * (dp - jnp.sum(dp * prob, axis=-1, keepdims=True))).astype(BF16)
+                parts[0].append(nn(ds, k) * 0.125)
+                parts[1].append(tn(ds, q) * 0.125)
+                parts[2].append(tn(low_p, g))
+            dqkv[rows, :] = jnp.concatenate(parts[0] + parts[1] + parts[2], axis=1).astype(BF16)
+
+        sums = jnp.sum(dqkv[...].astype(F32), axis=0, keepdims=True)
+        head_out[0, 0:1, 0:192] = sums[:, 0:192]
+        head_out[0, 1:2, 0:192] = sums[:, 384:576]
+        g1_out[0, :, 0:576] = nn(a_t[...], dqkv[...]).astype(BF16)
+        da[...] += nt(dqkv[...], w_ref[0, :, 0:576])
+
+    @pl.when(step == 5)
+    def _():
+        early[0].low_third()
+        late[0].second()
+        late[0].low_second()
+
+    @pl.when(step == 6)
+    def _():
+        late[1].second()
+        late[1].low_second()
+        early[1].low_third()
+        trade.relay()
+
+    @pl.when(step == 7)
+    def _():
+        for r in late:
+            r.low_third()
+        for i, r in enumerate(late + early):
+            r.hand_on(part_out, low_out, i // 2, halves[i % 2])
         trade.done()
         s.finish()
 
 
-def lay_kernel(seq, pad, count, out_ref, in_ref, out_out, in_out, wide):
-    for t in range(count):
-        wide[pl.ds(t, seq, stride=count), :] = out_ref[t, 0:seq, :].astype(F32)
-        in_out[pl.ds(t, seq, stride=count), :] = in_ref[t, 0:seq, :].astype(F32)
-    out_out[...] = wide[...].astype(BF16)
+def lay_kernel(seq, out_ref, in_ref, out_out, in_out):
+    for ref, out in ((out_ref, out_out), (in_ref, in_out)):
+        by_place = jnp.swapaxes(ref[...].astype(F32), 0, 1)[0:seq]
+        out[...] = by_place.astype(out.dtype)
 
 
 def update_kernel(*refs):
@@ -846,24 +858,35 @@
 
 
 class Gather:
-    def __init__(self, p, s, full, split, cols=ALL, own=None, column=None):
+    def __init__(self, p, s, full, split, cols=ALL, own=None, part=None, to_end=True):
         every = full.shape[4]
-        at = lambda x, c, z, y, rows: full.at[x, c, z, y, rows, cols]
-        col = lambda rows: at(p.x, p.c, ALL, p.y, rows) if column is None else column.at[:, rows, cols]
-        both = lambda view, device: s.copy(view, view, device)
+        of = lambda ref, x, c, z, y, rows: ref.at[x, c, z, y, rows, cols]
+        at = lambda *where: of(full, *where)
+        source = full if part is None else part
+        both = lambda where, device, ref=full: s.copy(of(ref, *where), at(*where), device)
         high, low = pl.ds(0, split), pl.ds(split, every - split)
-        here = at(p.x, p.c, p.z, p.y, ALL)
-        self.z = [s.copy(own, here, device) for device in p.to_z] if column is None else []
-        self.two = [s.copy(col(high), at(p.x, p.c, ALL, p.y, high), p.to_y)]
-        self.three = [both(at(p.x, p.c, ALL, ALL, high), p.to_x)]
-        self.core_two = [s.copy(col(ALL), at(p.x, p.c, ALL, p.y, ALL), p.to_c)]
-        self.core_three = [both(at(p.x, p.c, ALL, p.oy, high), p.to_c)]
-        self.core_last = [both(at(p.ox, p.c, ALL, ALL, high), p.to_c)]
-        if split < every:
-            self.two.append(s.copy(col(low), at(p.x, p.c, ALL, p.y, low), p.to_x))
-            self.three += [both(at(x, p.c, ALL, p.y, low), p.to_y) for x in (0, 1)]
-            self.core_three.append(both(at(p.ox, p.c, ALL, p.y, low), p.to_c))
-            self.core_last += [both(at(x, p.c, ALL, p.oy, low), p.to_c) for x in (0, 1)]
+        self.z, self.two, self.core_two, self.core_three, self.core_last = [], [], [], [], []
+        if own is not None:
+            here = at(p.x, p.c, p.z, p.y, ALL)
+            self.z = [s.copy(own, here, device) for device in p.to_z]
+            self.two = [both((p.x, p.c, ALL, p.y, high), p.to_y)]
+            self.core_two = [both((p.x, p.c, ALL, p.y, ALL), p.to_c)]
+            if split < every:
+                self.two.append(both((p.x, p.c, ALL, p.y, low), p.to_x))
+        if to_end:
+            self.three = [both((p.x, p.c, ALL, ALL, high), p.to_x, source)]
+            self.core_three = [both((p.x, p.c, ALL, p.oy, high), p.to_c, source)]
+            self.core_last = [both((p.ox, p.c, ALL, ALL, high), p.to_c)]
+            if split < every:
+                self.three += [both((x, p.c, ALL, p.y, low), p.to_y, source) for x in (0, 1)]
+                self.core_three.append(both((p.ox, p.c, ALL, p.y, low), p.to_c, source))
+                self.core_last += [both((x, p.c, ALL, p.oy, low), p.to_c) for x in (0, 1)]
+
+    @staticmethod
+    def present(p, part, full, split, local):
+        high, low = pl.ds(0, split), pl.ds(split, full.shape[4] - split)
+        where = [(p.x, p.c, ALL, ALL, high), (p.x, p.oc, ALL, p.y, ALL), *((x, p.c, ALL, p.y, low) for x in (0, 1))]
+        return [pltpu.make_async_copy(part.at[w], full.at[w], local.at[i]) for i, w in enumerate(where)]
 
     def along_z(self):
         start(self.z)
@@ -890,15 +913,15 @@
 
 
 def gather_kernel(seq, pad, tiles, w_ref, s_ref, tok, cot, vis_ref, tab_ref, live_ref,
-                  f1, col2, x_out, dy_out, vec_out, off_out, fs, tok_ref, cot_ref, wide, grad, send, recv, local):
+                  f1, part2, x_out, dy_out, dy_t, a_out, a_t, vec_out, off_out, fs, tok_ref, cot_ref, wide, grad, send, recv, local):
     p = Place()
     s = Sends(send, recv)
-    half = pl.ds(0, 384), pl.ds(384, 384)
+    thirds = [pl.ds(256 * i, 256) for i in range(3)]
     gathers = [
         Gather(p, s, fs, 16, own=s_ref),
-        *(Gather(p, s, f1, 48, cols, own=w_ref.at[0, :, cols]) for cols in half),
+        *(Gather(p, s, f1, 48, cols, own=w_ref.at[0, :, cols]) for cols in thirds),
     ]
-    ahead = [s.copy(w_ref.at[1], col2.at[p.z], device) for device in p.to_z]
+    ahead = Gather(p, s, part2, 48, own=w_ref.at[1], to_end=False)
     group = pl.ds(pl.multiple_of(8 * p.x, 8), 8)
     rows_in = [
         pltpu.make_async_copy(tok.at[:, group], tok_ref, local.at[3]),
@@ -907,12 +930,12 @@
     mine = [
         pltpu.make_async_copy(s_ref, fs.at[p.x, p.c, p.z, p.y], local.at[0]),
         pltpu.make_async_copy(w_ref.at[0], f1.at[p.x, p.c, p.z, p.y], local.at[1]),
-        pltpu.make_async_copy(w_ref.at[1], col2.at[p.z], local.at[2]),
+        pltpu.make_async_copy(w_ref.at[1], part2.at[p.x, p.c, p.z, p.y], local.at[2]),
     ]
     p.greet()
     for g in gathers:
         g.along_z()
-    start(ahead)
+    ahead.along_z()
     start(mine)
     start(rows_in)
     rows_in[0].wait()
@@ -923,13 +946,25 @@
     gathers[1].second()
     rows_in[1].wait()
     lay_cotangent(seq, pad, tiles, p.c * tiles, live_ref, cot_ref, dy_out, wide, grad)
-    stages = [("third", 0), ("second", 2), ("third", 1), ("last", 0), ("third", 2), ("done", 0)]
+    stages = [("second", 2), ("third", 0), ("third", 1), ("second", 3), ("last", 0), ("third", 2), ("third", 3), ("done", 0)]
     for name, i in stages:
         getattr(gathers[i], name)()
     spread_small(fs, vec_out, off_out)
-    for name, i in [("last", 1), ("last", 2), ("done", 1), ("done", 2)]:
+    gathers[1].last()
+
+    @pl.loop(0, tiles)
+    def _(t):
+        rows = pl.ds(pl.multiple_of(t * pad, 16), pad)
+        normed, _ = ln(x_out[rows, :])
+        a_out[rows, :] = (normed * vec_out[0:1, :] + vec_out[1:2, :]).astype(BF16)
+
+    a_t[...] = a_out[...].T
+    dy_t[...] = dy_out[...].T
+    gathers[2].last()
+    ahead.second()
+    for name, i in [("last", 3), ("done", 1), ("done", 2), ("done", 3)]:
         getattr(gathers[i], name)()
-    arrived(ahead)
+    arrived(ahead.two + ahead.core_two)
     s.finish()
 
 
@@ -951,13 +986,13 @@
 
     def __init__(self, p, s, parts, buffers, out, cols, load):
         own, r0, r1, r2, r3 = buffers
-        self.p, self.out, self.own, self.r0, self.r1, self.r2, self.r3 = p, out, own, r0, r1, r2, r3
+        self.p, self.out, self.r0, self.r1, self.r2, self.r3 = p, out, r0, r1, r2, r3
         self.load = pltpu.make_async_copy(parts.at[:, p.c, :, :, :, cols], own, load)
+        self.own = lambda x, z, y: own[x, z, y]
         self.core = [s.copy(parts.at[:, p.oc, :, :, :, cols], r0, p.to_c)]
         self.over_y = [s.copy(r0.at[:, :, p.oy], r1, p.to_y)]
         self.over_x = [s.copy(r1.at[p.ox], r2, p.to_x)]
-        if r3 is not None:
-            self.over_z = [s.copy(r2.at[z], r3.at[k], device) for k, (z, device) in enumerate(zip(p.zs, p.to_z))]
+        self.over_z = [s.copy(r2.at[z], r3.at[k], device) for k, (z, device) in enumerate(zip(p.zs, p.to_z))]
 
     def cores(self):
         start(self.core)
@@ -966,7 +1001,7 @@
     def first(self):
         self.load.wait()
         arrived(self.core)
-        add_into(self.r0, lambda x, z, y: self.own[x, z, y], self.r0.shape[:3])
+        add_into(self.r0, self.own, self.r0.shape[:3])
         start(self.over_y)
 
     def second(self):
@@ -979,11 +1014,6 @@
         add_into(self.r2, lambda z: self.r1[self.p.x, z], self.r2.shape[:1])
         start(self.over_z)
 
-    def hand_on(self, out, i, cols):
-        arrived(self.over_x)
-        for z in range(4):
-            out[z, i, :, cols] = (self.r2[z].astype(F32) + self.r1[self.p.x, z].astype(F32)).astype(BF16)
-
     def last(self):
         arrived(self.over_z)
         r2, r3 = self.r2, self.r3
@@ -995,19 +1025,89 @@
         return [pltpu.VMEM(shape + (rows, columns), BF16) for shape in lead]
 
 
+class FeedReduce:
+    COPIES = 8
+
+    def __init__(self, p, s, parts, buffers, cols, load=None):
+        *own, r0, r1, r2, e1, e2, e3 = buffers
+        self.p, self.r0, self.r1, self.r2, self.e1, self.e2, self.e3 = p, r0, r1, r2, e1, e2, e3
+        every, split = r0.shape[3], r1.shape[2]
+        self.split = split
+        high, low = pl.ds(0, split), pl.ds(split, every - split)
+        if own:
+            self.load = [pltpu.make_async_copy(parts.at[:, p.c, :, :, :, cols], own[0], load)]
+            self.own = lambda x, z, y: own[0][x, z, y]
+        else:
+            self.load, self.own = [], lambda x, z, y: parts[x, p.c, z, y, :, cols]
+        self.core = [s.copy(parts.at[:, p.oc, :, :, :, cols], r0, p.to_c)]
+        self.over_y = [s.copy(r0.at[:, :, p.oy, high], r1, p.to_y)]
+        self.over_x = [s.copy(r1.at[p.ox], r2, p.to_x)]
+        self.low_z = [s.copy(r0.at[:, z, :, low], e1.at[k], device) for k, (z, device) in enumerate(zip(p.zs, p.to_z))]
+        self.low_y = [s.copy(e1.at[0, :, p.oy], e2, p.to_y)]
+        self.low_x = [s.copy(e2.at[p.ox], e3, p.to_x)]
+
+    def cores(self):
+        start(self.core + self.load)
+
+    def first(self):
+        for copy in self.load:
+            copy.wait()
+        arrived(self.core)
+        add_into(self.r0, self.own, self.r0.shape[:3])
+        start(self.over_y + self.low_z)
+
+    def second(self):
+        arrived(self.over_y)
+        add_into(self.r1, lambda x, z: self.r0[x, z, self.p.y, 0 : self.split], self.r1.shape[:2])
+        start(self.over_x)
+
+    def low_second(self):
+        arrived(self.low_z)
+        for x in range(2):
+            for y in range(2):
+                total = self.r0[x, self.p.z, y, self.split :].astype(F32)
+                for k in range(3):
+                    total += self.e1[k, x, y].astype(F32)
+                self.e1[0, x, y] = total.astype(BF16)
+        start(self.low_y)
+
+    def low_third(self):
+        arrived(self.low_y)
+        for x in range(2):
+            self.e2[x] = (self.e2[x].astype(F32) + self.e1[0, x, self.p.y].astype(F32)).astype(BF16)
+        start(self.low_x)
+
+    def hand_on(self, out, low_out, i, cols):
+        arrived(self.over_x)
+        for z in range(4):
+            out[z, i, :, cols] = (self.r2[z].astype(F32) + self.r1[self.p.x, z].astype(F32)).astype(BF16)
+        arrived(self.low_x)
+        low_out[i, :, cols] = self.e2[self.p.x].astype(F32) + self.e3[...].astype(F32)
+
+    @staticmethod
+    def scratch(rows, split, columns):
+        low = rows - split
+        shapes = (2, 4, 2, rows), (2, 4, 2, rows), (2, 4, split), (4, split), (3, 2, 2, low), (2, low), (low,)
+        return [pltpu.VMEM(shape + (columns,), BF16) for shape in shapes]
+
+
 class Trade:
-    COPIES = 3
-
-    def __init__(self, p, s, own, full, local):
+    def __init__(self, p, s, own, full, local, pieces):
         here, there = full.at[p.x, p.c], full.at[p.ox, p.c]
         self.mine = pltpu.make_async_copy(own, here, local)
-        self.x, self.c = [s.copy(own, here, p.to_x)], [s.copy(own, here, p.to_c)]
+        size = own.shape[0] // pieces
+        cuts = [pl.ds(size * i, size) for i in range(pieces)]
+        self.x = [s.copy(own.at[cut], here.at[cut], p.to_x) for cut in cuts]
+        self.c = [s.copy(own, here, p.to_c)]
         self.further = [s.copy(there, there, p.to_c)]
 
     def begin(self):
-        start(self.x)
+        start(self.x[:1])
         start(self.c)
         self.mine.start()
+
+    def more(self, i):
+        start(self.x[i : i + 1])
 
     def relay(self):
         arrived(self.x)
@@ -1018,9 +1118,10 @@
         self.mine.wait()
 
 
-def reduce_kernel(g1, own_in, part, sum_two, sum_one, sum_hid, sum_head, total, feed, small, all_in,
-                  part_z, gs, lines, *scratch):
+def reduce_kernel(pad, tiles, g1, x_in, da_in, dh_in, vec_ref, part, part_low, sum_two, sum_hid, sum_head,
+                  total, feed, small, all_in, x, da, dh, own_in, sum_one, part_z, gs, lines, *scratch):
     *buffers, send, recv, local = scratch
+    fetch = [pltpu.make_async_copy(src, dst, local.at[5 + i]) for i, (src, dst) in enumerate(((x_in, x), (da_in, da), (dh_in, dh)))]
     p = Place()
     s = Sends(send, recv)
     thirds = [pl.ds(256 * i, 256) for i in range(3)]
@@ -1030,30 +1131,50 @@
     ]
     reduces.append(Reduce(p, s, gs, buffers[15:20], small, ALL, local.at[3]))
     over_z = [s.copy(part.at[z], part_z.at[k], device) for k, (z, device) in enumerate(zip(p.zs, p.to_z))]
-    trade = Trade(p, s, own_in, all_in, local.at[4])
+    trade = Trade(p, s, own_in, all_in, local.at[4], 4)
     p.greet()
     for r in reduces[:3]:
         r.cores()
+    start(over_z)
+    start(fetch)
+    sum_one[...] = jnp.zeros_like(sum_one)
+    for r in reduces[:3]:
+        r.first()
+    for copy in fetch:
+        copy.wait()
+
+    @pl.loop(0, tiles)
+    def _(t):
+        rows = pl.ds(pl.multiple_of(t * pad, 16), pad)
+        normed, inverse = ln(x[rows, :])
+        grad = da[rows, :]
+        back = ln_back(grad * vec_ref[0:1, :], normed, inverse)
+        own_in[rows, :] = (dh[rows, :] + back).astype(BF16)
+        sum_one[0:1, :] += jnp.sum(grad * normed, axis=0, keepdims=True)
+        sum_one[1:2, :] += jnp.sum(grad, axis=0, keepdims=True)
+
     trade.begin()
-    start(over_z)
     squeeze_small(sum_two, sum_one, sum_hid, sum_head, gs, lines)
     reduces[3].cores()
-    for r in reduces:
-        r.first()
     reduces[0].second()
+    trade.more(1)
+    reduces[3].first()
+    reduces[0].third()
     reduces[1].second()
-    reduces[0].third()
-    reduces[2].second()
+    trade.more(2)
     reduces[1].third()
     reduces[3].second()
-    trade.relay()
+    reduces[2].second()
+    trade.more(3)
+    reduces[3].third()
     reduces[2].third()
-    reduces[3].third()
     arrived(over_z)
     for i in range(2):
-        feed[i] = part[p.z, i].astype(F32) + sum(part_z[k, i].astype(F32) for k in range(3))
+        feed[i, 0:64] = part[p.z, i].astype(F32) + sum(part_z[k, i].astype(F32) for k in range(3))
+        feed[i, 64:96] = part_low[i]
     for r in reduces:
         r.last()
+    trade.relay()
     trade.done()
     s.finish()
 
@@ -1087,19 +1208,22 @@
 
     full = shape((2, 2, 4, 2, 96, D), BF16)
     dma = lambda count: pltpu.SemaphoreType.DMA((count,))
-    copies = 2 * Gather.COPIES + Gather.COPIES_WHOLE + 3
-    f1, col2, x, dy, vec, off = pl.pallas_call(
+    copies = 3 * Gather.COPIES + Gather.COPIES_WHOLE + 6
+    f1, part2, x, dy, dy_t, a, a_t, vec, off = pl.pallas_call(
         functools.partial(gather_kernel, seq, pad, tiles),
         out_shape=(
             full,
-            shape((4, 96, D), BF16),
+            full,
             shape((rows, D), F32),
             shape((rows, D), BF16),
+            shape((D, rows), BF16),
+            shape((rows, D), BF16),
+            shape((D, rows), BF16),
             shape((16, D), F32),
             shape((4, 8, D), F32),
         ),
         in_specs=[vmem] * 2 + [anywhere] * 2 + [vmem] * 3,
-        out_specs=[anywhere] * 2 + [vmem] * 4,
+        out_specs=[anywhere] * 2 + [vmem] * 7,
         scratch_shapes=[
             pltpu.VMEM((2, 2, 4, 2, 16, 128), BF16),
             pltpu.VMEM((seq, 8, D), BF16),
@@ -1115,121 +1239,120 @@
     )(own, own_small, by_place(tokens), by_place(cotangent), places, table, live)
     w1 = f1.reshape(4, D, D)
 
-    of_group1 = lambda *shape: pl.BlockSpec((1,) + shape, lambda m: (m,) + (0,) * len(shape))
-    all_of1 = lambda *shape: pl.BlockSpec(shape, lambda m: (0,) * len(shape))
-    copies = Gather.COPIES * 2 - 3
-    h, qkv, probs, o, f2, f3 = pl.pallas_call(
-        functools.partial(attend_kernel, seq, pad, tiles),
+    all_of1 = lambda *shape: pl.BlockSpec(shape, lambda i: (0,) * len(shape))
+    each = lambda *shape: pl.BlockSpec((1,) + shape, lambda i: (i % 4,) + (0,) * len(shape))
+    former = lambda *shape: pl.BlockSpec((1,) + shape, lambda i: (i + i // 4 * (3 - i),) + (0,) * len(shape))
+    latter = lambda *shape: pl.BlockSpec((1,) + shape, lambda i: (i // 4 * (i - 4),) + (0,) * len(shape))
+    copies = Gather.COPIES * 3 - 6
+    h, qkv, probs, o, r, slope, g3, c_t, f2, f3 = pl.pallas_call(
+        functools.partial(fore_kernel, seq, pad, tiles),
         out_shape=(
             shape((rows, D), F32),
             shape((4, rows, 576), BF16),
             shape((4, 3, rows, pad), BF16),
             shape((4, rows, 192), BF16),
+            shape((4, rows, D), BF16),
+            shape((4, rows, D), F32),
+            shape((4, D, D), BF16),
+            shape((D, rows), BF16),
             full,
             full,
         ),
-        grid=(4,),
-        in_specs=[all_of1(rows, D), all_of1(16, D), of_group1(8, D), of_group1(D, D), all_of1(4, 96, D), pl.BlockSpec((1, 96, D), lambda m: (2, 0, 0))],
-        out_specs=(all_of1(rows, D), of_group1(rows, 576), of_group1(3, rows, pad), of_group1(rows, 192))
-        + (pl.BlockSpec(memory_space=ANY),) * 2,
-        scratch_shapes=[pltpu.VMEM((rows, D), BF16), dma(copies), dma(copies), dma(2)],
+        grid=(8,),
+        in_specs=[all_of1(rows, D), all_of1(rows, D), all_of1(D, rows), all_of1(16, D), each(8, D), former(D, D),
+                  anywhere,
+                  pl.BlockSpec((1, 96, D), lambda i: (2, 0, 0))],
+        out_specs=[all_of1(rows, D), former(rows, 576), former(3, rows, pad), former(rows, 192), latter(rows, D),
+                   latter(rows, D), latter(D, D), all_of1(D, rows), anywhere, anywhere],
+        scratch_shapes=[
+            pltpu.VMEM((rows, D), BF16),
+            pltpu.VMEM((2, 2, 4, 2, 96, D), BF16),
+            dma(copies),
+            dma(copies),
+            dma(6),
+        ],
         compiler_params=params(collective_id=2, has_side_effects=True),
-        name="attend",
-    )(x, vec, off, w1, col2, own)
+        name="fore",
+    )(x, a, dy_t, vec, off, w1, part2, own)
     w2, w3 = (f.reshape(4, D, D) for f in (f2, f3))
 
-    out_own, dh, sum_two, sum_hid, g2, g3 = pl.pallas_call(
-        functools.partial(feed_kernel, seq, pad, tiles),
+    by_device = lambda g: g.reshape(2, 2, 4, 2, 96, D)
+    everyone = shape((2, 2, rows, D), BF16)
+    copies = 4 * FeedReduce.COPIES + 3
+    da, dh, sum_two, sum_hid, sum_head, g1, part, part_low, all_out = pl.pallas_call(
+        functools.partial(back_kernel, seq, pad, tiles),
         out_shape=(
-            shape((rows, D), BF16),
+            shape((rows, D), F32),
             shape((rows, D), F32),
             shape((8, D), F32),
             shape((4, 8, D), F32),
+            shape((4, 8, D), F32),
             shape((4, D, D), BF16),
-            shape((4, D, D), BF16),
+            shape((4, 2, 64, D), BF16),
+            shape((2, 32, D), F32),
+            everyone,
         ),
-        grid=(4,),
-        in_specs=[all_of1(tiles, 128), all_of1(rows, D), all_of1(rows, D), all_of1(16, D), of_group1(8, D),
-                  of_group1(D, D), of_group1(D, D)],
-        out_specs=(all_of1(rows, D), all_of1(rows, D), all_of1(8, D), of_group1(8, D), of_group1(D, D), of_group1(D, D)),
+        grid=(8,),
+        in_specs=[all_of1(tiles, 128), all_of1(rows, D), all_of1(rows, D), all_of1(D, rows), all_of1(D, rows), all_of1(16, D),
+                  former(D, D), former(D, D), former(rows, D), former(rows, D), latter(D, D), latter(rows, 576),
+                  latter(3, rows, pad), latter(rows, 192), anywhere],
+        out_specs=[all_of1(rows, D), all_of1(rows, D), all_of1(8, D), former(8, D), latter(8, D), latter(D, D),
+                   all_of1(4, 2, 64, D), all_of1(2, 32, D), anywhere],
         scratch_shapes=[
             pltpu.VMEM((rows, D), BF16),
             pltpu.VMEM((D, rows), BF16),
-            pltpu.VMEM((D, rows), BF16),
             pltpu.VMEM((rows, D), F32),
             pltpu.VMEM((rows, D), F32),
-        ],
-        compiler_params=params(),
-        name="feed",
-    )(live, dy, h, vec, off, w2, w3)
-
-    by_device = lambda g: g.reshape(2, 2, 4, 2, 96, D)
-    everyone = shape((2, 2, rows, D), BF16)
-    copies = 4 * (Reduce.COPIES - 3) + Trade.COPIES
-    in_own, sum_one, sum_head, g1, part, all_out = pl.pallas_call(
-        functools.partial(back_kernel, seq, pad, tiles),
-        out_shape=(
-            shape((rows, D), BF16),
-            shape((8, D), F32),
-            shape((4, 8, D), F32),
-            shape((4, D, D), BF16),
-            shape((4, 2, 96, D), BF16),
-            everyone,
-        ),
-        grid=(4,),
-        in_specs=[all_of1(rows, D), all_of1(rows, D), all_of1(16, D), of_group1(D, D), of_group1(rows, 576),
-                  of_group1(3, rows, pad), of_group1(rows, 192)] + [pl.BlockSpec(memory_space=ANY)] * 3,
-        out_specs=(all_of1(rows, D), all_of1(8, D), of_group1(8, D), of_group1(D, D), all_of1(4, 2, 96, D),
-                   pl.BlockSpec(memory_space=ANY)),
-        scratch_shapes=[
-            pltpu.VMEM((D, rows), BF16),
-            pltpu.VMEM((rows, D), BF16),
-            pltpu.VMEM((D, rows), BF16),
             pltpu.VMEM((rows, 192), BF16),
             pltpu.VMEM((rows, 576), BF16),
-            pltpu.VMEM((rows, D), F32),
-            *(4 * Reduce.scratch(96, 384)[:4]),
+            pltpu.VMEM((2, 2, 4, 2, 96, D), BF16),
+            pltpu.VMEM((rows, D), BF16),
+            *(2 * FeedReduce.scratch(96, 64, 384)),
+            *(2 * FeedReduce.scratch(96, 64, 384)[1:]),
             dma(copies),
             dma(copies),
-            dma(5),
+            dma(3),
         ],
         compiler_params=params(collective_id=3, has_side_effects=True),
         name="back",
-    )(x, dh, vec, w1, qkv, probs, o, by_device(g2), by_device(g3), out_own)
-
-    copies = 4 * Reduce.COPIES + 3 + Trade.COPIES
+    )(live, dy, h, c_t, a_t, vec, w2, w3, r, slope, w1, qkv, probs, o, by_device(g3))
+
+    copies = 4 * Reduce.COPIES + 3 + 6
     total_attend, total_feed, small, all_in = pl.pallas_call(
-        reduce_kernel,
+        functools.partial(reduce_kernel, pad, tiles),
         out_shape=(shape((96, D), F32), shape((2, 96, D), F32), shape((16, 128), F32), everyone),
-        in_specs=[anywhere] * 2 + [vmem] * 5,
+        in_specs=[anywhere] * 4 + [vmem] * 6,
         out_specs=[vmem] * 3 + [anywhere],
         scratch_shapes=[
-            pltpu.VMEM((3, 2, 96, D), BF16),
+            pltpu.VMEM((rows, D), F32),
+            pltpu.VMEM((rows, D), F32),
+            pltpu.VMEM((rows, D), F32),
+            pltpu.VMEM((rows, D), BF16),
+            pltpu.VMEM((8, D), F32),
+            pltpu.VMEM((3, 2, 64, D), BF16),
             pltpu.VMEM((2, 2, 4, 2, 16, 128), BF16),
             pltpu.VMEM((8, D), F32),
             *(3 * Reduce.scratch(96, 256)),
             *Reduce.scratch(16, 128),
             dma(copies),
             dma(copies),
-            dma(5),
+            dma(8),
         ],
         compiler_params=params(collective_id=1, has_side_effects=True),
         name="reduce",
-    )(by_device(g1), in_own, part, sum_two, sum_one, sum_hid, sum_head)
-
-    flat = seq * tile_count
+    )(by_device(g1), x, da, dh, vec, part, part_low, sum_two, sum_hid, sum_head)
+
     block = pl.BlockSpec((tile_count, pad, 128), lambda n: (0, 0, n))
     output, input_grad = pl.pallas_call(
-        functools.partial(lay_kernel, seq, pad, tile_count),
-        out_shape=(shape((flat, D), BF16), shape((flat, D), F32)),
+        functools.partial(lay_kernel, seq),
+        out_shape=(shape((seq, tile_count, D), BF16), shape((seq, tile_count, D), F32)),
         grid=(D // 128,),
         in_specs=[block, block],
-        out_specs=(pl.BlockSpec((flat, 128), lambda n: (0, n)),) * 2,
-        scratch_shapes=[pltpu.VMEM((flat, 128), F32)],
+        out_specs=(pl.BlockSpec((seq, tile_count, 128), lambda n: (0, 0, n)),) * 2,
         compiler_params=params(),
         name="lay",
     )(*(a.reshape(tile_count, pad, D) for a in (all_out, all_in)))
-    output, input_grad = (a.reshape(seq, tile_count, D).transpose(1, 0, 2) for a in (output, input_grad))
+    output, input_grad = by_place(output), by_place(input_grad)
 
     kinds = [shape(a.shape, F32) for a in state[:7]]
     results = pl.pallas_call(

time: 279 us -> 251 us (0.90)
  Pallas kernels: 276 us -> 247 us
    pallas_call x4 -> x3, Pallas kernels: 151 us -> 112 us  [the longest x1 52.6 us: fast_shards(): pl.pallas_call(functools.partial(reduce_kernel, pad, tiles), out_shape=(s...]
    pallas_call x1, Pallas kernels: 44.9 us -> 50.5 us  [fast_shards(): pl.pallas_call(functools.partial(gather_kernel, seq, pad, tiles), out_sha...]
    pallas_call x1, Pallas kernels: 72.5 us -> 77.8 us  [fast_shards(): pl.pallas_call(functools.partial(back_kernel, seq, pad, tiles), out_shape...]
where the time goes in v4:
time: 251 us; the launch traced here: 250 us
  Pallas kernels  247 us (98%)
    pallas_call x1, Pallas kernels, fast_shards(): pl.pallas_call(functools.partial(back_kernel, seq, pad, tiles), out_shape...  77.8 us
    pallas_call x1, Pallas kernels, fast_shards(): pl.pallas_call(functools.partial(reduce_kernel, pad, tiles), out_shape=(s...  52.6 us
    pallas_call x1, Pallas kernels, fast_shards(): pl.pallas_call(functools.partial(gather_kernel, seq, pad, tiles), out_sha...  50.5 us
    pallas_call x1, Pallas kernels, fast_shards(): pl.pallas_call(functools.partial(fore_kernel, seq, pad, tiles), out_shape...  49.8 us
    pallas_call x1, Pallas kernels, fast_shards(): pl.pallas_call(functools.partial(lay_kernel, seq), out_shape=(shape((seq,...  9.18 us

profile of v4, /device:TPU:0, one launch (start us, length us, event | category | flops | bytes accessed | tf_op | source)
XLA Modules:
  0.0 249.8 jit_solution(13049103240280346134)
XLA Ops:
  0.7 0.0 copy-start
  1.4 0.6 broadcast_in_dim.2.live_ref
  2.0 0.0 copy-done
  2.0 0.8 copy.64
  2.8 2.1 pack.1
  4.9 50.5 %gather.1 = (bf16[2,2,4,2,96,768]{5,4,3,2,1,0:T(8,128)(2,1)}, bf16[2,2,4,2,96,768]{5,4,3,2,1,0:T(8,128)(2,1)}, f32[640,768]{1,0:T(8,128)}, bf16[640,768]{1,0:T(8...) custom-call(bf16[3,96,768]{2,1,0:T(8,128)(2,1)} %get-tuple-element.1, ...), custom_call_target="tpu_custom_call" | custom-call | tf_op jit(solution)/shard_map/gather/pallas_call | solution.py:1212
  55.4 49.8 %fore.1 = (f32[640,768]{1,0:T(8,128)}, bf16[4,640,576]{2,1,0:T(8,128)(2,1)}, bf16[4,3,640,160]{3,2,1,0:T(8,128)(2,1)}, bf16[4,640,192]{2,1,0:T(8,128)(2,1)}, bf1...) custom-call(f32[640,768]{1,0:T(8,128)} %get-tuple-element.111.x_ref., ...), custom_call_target="tpu_custom_call" | custom-call | tf_op jit(solution)/shard_map/fore/pallas_call | solution.py:1247
  105.3 77.8 %back.1 = (f32[640,768]{1,0:T(8,128)}, f32[640,768]{1,0:T(8,128)}, f32[8,768]{1,0:T(8,128)}, f32[4,8,768]{2,1,0:T(8,128)}, f32[4,8,768]{2,1,0:T(8,128)}, /*index...) custom-call(f32[4,128]{1,0:T(4,128)} %broadcast_in_dim.2.live_ref, ...), custom_call_target="tpu_custom_call" | custom-call | tf_op jit(solution)/shard_map/back/pallas_call | solution.py:1282
  183.0 52.6 %reduce.1 = (f32[96,768]{1,0:T(8,128)}, f32[2,96,768]{2,1,0:T(8,128)}, f32[16,128]{1,0:T(8,128)}, bf16[2,2,640,768]{3,2,1,0:T(8,128)(2,1)}) custom-call(bf16[2,2,4,2,96,768]{5,4,3,2,1,0:T(8,128)(2,1)} %bitcast.51, f32[640,768]{1,0:T(8,128)} %get-tuple-element.111.x_ref.x_in, f32[640,768]{1,0:T(8,128)} %get-tuple-element.131.da_in, ...), custom_call_target="tpu_custom_call" | custom-call | tf_op jit(solution)/shard_map/reduce/pallas_call | solution.py:1321
  235.7 0.0 copy-start.1
  235.7 9.2 %lay.1 = (bf16[147,16,768]{2,1,0:T(8,128)(2,1)}, f32[147,16,768]{2,1,0:T(8,128)}) custom-call(bf16[16,160,768]{2,1,0:T(8,128)(2,1)} %bitcast.52, bf16[16,160,768]{2,1,0:T(8,128)(2,1)} %bitcast.53), custom_call_target="tpu_custom_call" | custom-call | tf_op jit(solution)/shard_map/lay/pallas_call | solution.py:1346
  244.9 4.7 %update.1 = (f32[3,96,192]{2,1,0:T(8,128)}, f32[192,96]{1,0:T(8,128)}, f32[96,768]{1,0:T(8,128)}, f32[96,768]{1,0:T(8,128)}, f32[3,2,8]{2,1,0:T(2,128)}, /*index...) custom-call(f32[96,768]{1,0:T(8,128)} %get-tuple-element.141.refs_0_, ...), custom_call_target="tpu_custom_call" | custom-call | tf_op jit(solution)/shard_map/update/pallas_call | solution.py:1358
  249.6 0.0 copy-done.1
  (2 shorter events, 0.0 us)
Async XLA Ops:
  0.7 1.3 copy-start
  235.7 13.9 %copy-start.1 = (s32[16,147]{1,0:T(8,128)S(1)}, s32[16,147]{1,0:T(8,128)}, u32[]{:S(2)}) copy-start(s32[16,147]{1,0:T(8,128)} %param.28) | copy-start | bytes 28228
